TPU v7x, 128 devices: a whole 4x4x4 slice. The times are simulated.
128 devices in a mesh: lat: 4 (over x_hi, core), lon: 32 (over z, y, x_lo).
Axes of the slice: x: 4 (x_hi: 2, x_lo: 2; x = x_hi * 2 + x_lo), y: 4, z: 4, core: 2. Of those that a mesh axis runs over, the one named last changes fastest.
Arguments:
- background: bfloat16 [512, 4096, 128], P('lat', 'lon'), may hold values from -6 to 6
- obs_values: bfloat16 [128, 128, 96, 128], P(('lat', 'lon')), may hold values from -6 to 6
- obs_cells: int32 [128, 128, 96], P(('lat', 'lon')), may hold values from 0 to 16383
- obs_counts: int32 [128, 128], P(('lat', 'lon')), may hold values from 0 to 96, as said below
- conv1_weight: bfloat16 [3, 3, 128, 128], replicated, may hold values from -0.1875 to 0.1875
- conv1_bias: float32 [128], replicated, may hold values from -3 to 3
- conv2_weight: bfloat16 [3, 3, 128, 128], replicated, may hold values from -0.1875 to 0.1875
- conv2_bias: float32 [128], replicated, may hold values from -3 to 3
Outputs:
- coarse: bfloat16 [256, 2048, 128], P('lat', 'lon')
Inputs may be any that keep to these rules, and one draw needn't show every extreme that they name: `obs_counts`: every draw has an owner that receives 96 live slots from every device.
All inputs are finite; a program needn't handle non-finite values.
Results may differ from a plain program's by a relative error of at most 0.0051.
Values may be sent and summed in bfloat16 or wider, within the bound.
No kernel may reach another device: no remote copies, remote signals or barrier semaphores. Data moves between devices by JAX's collectives and lax.ppermute only.
A program may use at most 128 MiB of HBM per device.

v0:
```python
import jax
import jax.numpy as jnp
from jax import lax
from jax.sharding import PartitionSpec as P


def padded_2(x, sides, width, wrap):
    for axis, dim in sides:
        devices, length = (lax.axis_size(axis), x.shape[dim])
        up = [(i, (i + 1) % devices) for i in range(devices if wrap else devices - 1)]
        down = [(j, i) for i, j in up]
        last = lax.slice_in_dim(x, length - width, length, axis=dim)
        leading = lax.slice_in_dim(x, 0, width, axis=dim)
        before = lax.ppermute(last, axis, up)
        after = lax.ppermute(leading, axis, down)
        x = jnp.concatenate([before, x, after], axis=dim)
    return x


def passed_along(value, axis, steps):
    count = lax.axis_size(axis)
    pairs = [(source, (source + steps) % count) for source in range(count)]
    return lax.ppermute(value, axis, pairs)


def surround(field):
    sides = padded_2(field, (("lon", 1),), 1, True)
    padded = padded_2(sides, (("lat", 0),), 1, False)
    across = passed_along(jnp.stack([sides[0], sides[-1]]), "lon", lax.axis_size("lon") // 2)
    band = lax.axis_index("lat")
    top = jnp.where(band == 0, across[0], padded[0])
    bottom = jnp.where(band == lax.axis_size("lat") - 1, across[1], padded[-1])
    return padded.at[0].set(top).at[-1].set(bottom)


def convolve(padded, weight, stride):
    rows = (padded.shape[0] - 2) // stride
    cols = (padded.shape[1] - 2) // stride
    chans = padded.shape[2]
    outs = weight.shape[3]
    widened = jnp.concatenate(
        [padded[:, dj : dj + cols * stride : stride] for dj in range(3)], axis=2
    )
    total = jnp.zeros((rows * cols, outs), jnp.float32)
    for di in range(3):
        window = widened[di : di + rows * stride]
        if stride == 2:
            window = window.reshape(rows, 2, cols, 3 * chans)[:, 0]
        total = total + jnp.dot(
            window.reshape(rows * cols, 3 * chans),
            weight[di].reshape(3 * chans, outs),
            preferred_element_type=jnp.float32,
        )
    return total.reshape(rows, cols, outs)


def shards(
    background,
    obs_values,
    obs_cells,
    obs_counts,
    conv1_weight,
    conv1_bias,
    conv2_weight,
    conv2_bias,
):
    rows, cols, chans = background.shape
    slots = obs_values.shape[2]
    live = jnp.arange(slots)[None, :] < obs_counts[0][:, None]
    sent = jnp.where(live[:, :, None], obs_values[0], jnp.zeros((), jnp.bfloat16))
    places = jnp.where(live, obs_cells[0], 0)
    got_values, got_cells = (
        lax.all_to_all(sent, ("lat", "lon"), split_axis=0, concat_axis=0, tiled=True),
        lax.all_to_all(places, ("lat", "lon"), split_axis=0, concat_axis=0, tiled=True),
    )
    flat_values = got_values.reshape(-1, chans).astype(jnp.float32)
    flat_cells = got_cells.reshape(-1)
    increment = jnp.zeros((rows * cols, chans), jnp.float32).at[flat_cells].add(flat_values)
    analysis = (background.astype(jnp.float32) + increment.reshape(rows, cols, chans)).astype(
        jnp.bfloat16
    )
    hidden = jax.nn.gelu(convolve(surround(analysis), conv1_weight, 1) + conv1_bias).astype(
        jnp.bfloat16
    )
    coarse = convolve(surround(hidden), conv2_weight, 2) + conv2_bias
    return coarse.astype(jnp.bfloat16)


def solution(mesh):
    placed = (
        P("lat", "lon", None),
        P(("lat", "lon"), None, None, None),
        P(("lat", "lon"), None, None),
        P(("lat", "lon"), None),
        P(),
        P(),
        P(),
        P(),
    )
    return jax.shard_map(
        shards, mesh=mesh, in_specs=placed, out_specs=P("lat", "lon", None), check_vma=False
    )
```

profile of v0, /device:TPU:1, one launch (start us, length us, event | category | flops | bytes accessed | tf_op | source)
XLA Modules:
  0.0 330.0 jit_solution(17980232840484357942)
XLA Ops:
  2.4 11.5 %all-to-all-start = ((s32[128,1,96]{2,1,0:T(1,128)}), s32[128,1,96]{2,1,0:T(1,128)S(1)}, u32[]{:S(2)}, u32[]{:S(2)}) async-start(s32[128,1,96]{2,1,0:T(1,128)} %compare_select_fusion.1), calls=%async_computation | async-start | bytes 131072 | tf_op jit(solution)/shard_map/all_to_all | solution.py:74
  14.6 7.0 %bitcast_select_fusion = bf16[128,96,128]{2,1,0:T(8,128)(2,1)} fusion(bf16[1,128,96,128]{3,2,1,0:T(8,128)(2,1)} %param.17, pred[128,96]{1,0:T(8,128)(4,1)S(1)} %iota_compare_fusion), kind=kLoop, calls=%fused_computation.22 | loop fusion | flops 1572864 | bytes 6303744 | tf_op jit(solution)/shard_map/jit(_where)/select_n | solution.py:70
  23.4 7.9 %all-to-all-start.1 = ((bf16[128,96,128]{2,1,0:T(8,128)(2,1)}), bf16[128,96,128]{2,1,0:T(8,128)(2,1)S(1)}, u32[]{:S(2)}, u32[]{:S(2)}) async-start(bf16[128,96,128]{2,1,0:T(8,128)(2,1)} %bitcast_select_fusion), calls=%async_computation.1 | async-start | bytes 6291456 | tf_op jit(solution)/shard_map/all_to_all | solution.py:73
  32.9 40.2 %all-to-all-done.1 = bf16[128,96,128]{2,1,0:T(8,128)(2,1)S(1)} async-done(((bf16[128,96,128]{2,1,0:T(8,128)(2,1)}), bf16[128,96,128]{2,1,0:T(8,128)(2,1)S(1)}, u32[]{:S(2)}, u32[]{:S(2)}) %all-to-all-start.1) | async-done | bytes 3145760 | tf_op jit(solution)/shard_map/all_to_all | solution.py:73
  73.1 77.2 %scatter_custom_fusion = f32[16384,128]{1,0:T(8,128)} fusion(s32[12288]{0:T(1024)S(1)} %bitcast.59, bf16[12288,128]{1,0:T(8,128)(2,1)S(1)} %bitcast.51, f32[]{:T(128)} %constant.107.clone.1), kind=kCustom, calls=%fused_computation.15 | custom fusion | flops 3145728 | bytes 11534340 | tf_op jit(solution)/shard_map/scatter-add | solution.py:78
  150.3 5.9 %add_convert_fusion = bf16[128,128,128]{2,1,0:T(8,128)(2,1)S(1)} fusion(f32[128,128,128]{2,1,0:T(8,128)} %bitcast.42, bf16[128,128,128]{2,1,0:T(8,128)(2,1)} %param.16), kind=kLoop, calls=%fused_computation.13 | loop fusion | flops 6291456 | bytes 16777216 | tf_op jit(solution)/shard_map/convert_element_type | solution.py:79
  158.3 7.1 %collective-permute-start = (bf16[128,1,128]{2,1,0:T(2,128)(2,1)S(1)}, bf16[128,1,128]{2,1,0:T(2,128)(2,1)S(1)}, u32[]{:S(2)}, u32[]{:S(2)}) collective-permute-start(bf16[128,1,128]{2,1,0:T(2,128)(2,1)S(1)} %get-tuple-element.68), channel_id=1, source_target_pairs={{0,1},{1,2},{2,3},{3,4},{4,5},{5,6},{6,7},{7,8},{8,9},{9,10},{10,1... | collective-permute-start | bytes 98312 | tf_op jit(solution)/shard_map/ppermute | solution.py:14
  170.2 4.7 %collective-permute-start.2 = (bf16[1,130,128]{2,1,0:T(8,128)(2,1)S(1)}, bf16[1,130,128]{2,1,0:T(8,128)(2,1)S(1)}, u32[]{:S(2)}, u32[]{:S(2)}) collective-permute-start(bf16[1,130,128]{2,1,0:T(8,128)(2,1)S(1)} %get-tuple-element.64), channel_id=1, source_target_pairs={{0,32},{32,64},{64,96},{1,33},{33,65},{65,97},{2,34},{34,66},{66,9... | collective-permute-start | bytes 99848 | tf_op jit(solution)/shard_map/ppermute | solution.py:14
  177.1 4.5 %collective-permute-done.3 = bf16[1,130,128]{2,1,0:T(8,128)(2,1)S(1)} collective-permute-done((bf16[1,130,128]{2,1,0:T(8,128)(2,1)S(1)}, bf16[1,130,128]{2,1,0:T(8,128)(2,1)S(1)}, u32[]{:S(2)}, u32[]{:S(2)}) %collective-permute-start.3) | collective-permute-done | bytes 33312 | tf_op jit(solution)/shard_map/ppermute | solution.py:15
  181.7 3.9 %pad_maximum_fusion.2 = bf16[130,130,128]{2,1,0:T(8,128)(2,1)S(1)} fusion(bf16[1,130,128]{2,1,0:T(8,128)(2,1)S(1)} %collective-permute-done.3, bf16[128,1,128]{2,1,0:T(2,128)(2,1)S(1)} %collective-permute-done.1, bf16[128,128,128]{2,1,0:T(8,128)(2,1)S(1)} %copy-done.1, bf16[128,1,128]{2,1,0:T(2,128)(2,1)S(1)} %collective-permute-done, ...), kind=kLoop, calls=%fused_computation.19 | loop fusion | flops 21632000 | bytes 8652800 | tf_op jit(solution)/shard_map/concatenate | solution.py:16
  185.6 4.9 %fusion.17 = (bf16[130,128,128]{2,1,0:T(8,128)(2,1)S(1)}, bf16[130,128,128]{2,1,0:T(8,128)(2,1)}, bf16[130,128,128]{2,1,0:T(8,128)(2,1)}) fusion(bf16[130,130,128]{2,1,0:T(8,128)(2,1)S(1)} %fusion.13), kind=kLoop, calls=%fused_computation.45 | loop fusion | bytes 25559040 | tf_op jit(solution)/shard_map/slice | solution.py:42
  190.5 5.7 %pad_maximum_fusion = bf16[130,128,384]{2,1,0:T(8,128)(2,1)S(1)} fusion(bf16[130,128,128]{2,1,0:T(8,128)(2,1)} %get-tuple-element.60, bf16[130,128,128]{2,1,0:T(8,128)(2,1)} %get-tuple-element.61, bf16[130,128,128]{2,1,0:T(8,128)(2,1)S(1)} %get-tuple-element.59), kind=kLoop, calls=%fused_computation.3 | loop fusion | flops 38338560 | bytes 25559040 | tf_op jit(solution)/shard_map/concatenate | solution.py:41
  196.3 15.9 %fusion.15 = (bf16[128,128,384]{2,1,0:T(8,128)(2,1)}, bf16[128,128,384]{2,1,0:T(8,128)(2,1)}, bf16[128,128,384]{2,1,0:T(8,128)(2,1)S(1)}) fusion(bf16[130,128,384]{2,1,0:T(8,128)(2,1)S(1)} %pad_maximum_fusion), kind=kLoop, calls=%fused_computation.43 | loop fusion | bytes 75497472 | tf_op jit(solution)/shard_map/slice | solution.py:46
  212.1 3.5 %fusion.22 = f32[16384,128]{1,0:T(8,128)S(1)} fusion(bf16[16384,384]{1,0:T(8,128)(2,1)S(1)} %bitcast.37, bf16[384,128]{1,0:T(8,128)(2,1)S(1)} %bitcast.52), kind=kOutput, calls=%fused_computation.50 | convolution fusion | flops 1610612736 | bytes 21069824 | tf_op jit(solution)/shard_map/dot_general | solution.py:49
  215.7 11.7 %convolution_add_fusion.1 = f32[16384,128]{1,0:T(8,128)} fusion(f32[16384,128]{1,0:T(8,128)S(1)} %fusion.22, bf16[16384,384]{1,0:T(8,128)(2,1)} %bitcast.41, bf16[384,128]{1,0:T(8,128)(2,1)S(1)} %bitcast.57), kind=kOutput, calls=%fused_computation.2 | convolution fusion | flops 1612709888 | bytes 29458432 | tf_op jit(solution)/shard_map/dot_general | solution.py:49
  227.4 6.3 %convolution_add_fusion = f32[16384,128]{1,0:T(8,128)S(1)} fusion(f32[16384,128]{1,0:T(8,128)} %convolution_add_fusion.1, bf16[16384,384]{1,0:T(8,128)(2,1)S(1)} %bitcast.40, bf16[384,128]{1,0:T(8,128)(2,1)S(1)} %bitcast.56), kind=kOutput, calls=%fused_computation.1 | convolution fusion | flops 1612709888 | bytes 29458432 | tf_op jit(solution)/shard_map/dot_general | solution.py:49
  237.7 5.0 %collective-permute-start.6 = (bf16[128,1,128]{2,1,0:T(2,128)(2,1)S(1)}, bf16[128,1,128]{2,1,0:T(2,128)(2,1)S(1)}, u32[]{:S(2)}, u32[]{:S(2)}) collective-permute-start(bf16[128,1,128]{2,1,0:T(2,128)(2,1)S(1)} %get-tuple-element.67), channel_id=1, source_target_pairs={{1,0},{2,1},{3,2},{4,3},{5,4},{6,5},{7,6},{8,7},{9,8},{10,9},{11,1... | collective-permute-start | bytes 98312 | tf_op jit(solution)/shard_map/ppermute | solution.py:15
  244.3 4.1 %collective-permute-start.7 = (bf16[1,130,128]{2,1,0:T(8,128)(2,1)S(1)}, bf16[1,130,128]{2,1,0:T(8,128)(2,1)S(1)}, u32[]{:S(2)}, u32[]{:S(2)}) collective-permute-start(bf16[1,130,128]{2,1,0:T(8,128)(2,1)S(1)} %get-tuple-element.62), channel_id=1, source_target_pairs={{0,32},{32,64},{64,96},{1,33},{33,65},{65,97},{2,34},{34,66},{66,9... | collective-permute-start | bytes 99848 | tf_op jit(solution)/shard_map/ppermute | solution.py:14
  250.5 4.7 %collective-permute-done.8 = bf16[1,130,128]{2,1,0:T(8,128)(2,1)S(1)} collective-permute-done((bf16[1,130,128]{2,1,0:T(8,128)(2,1)S(1)}, bf16[1,130,128]{2,1,0:T(8,128)(2,1)S(1)}, u32[]{:S(2)}, u32[]{:S(2)}) %collective-permute-start.8) | collective-permute-done | bytes 33312 | tf_op jit(solution)/shard_map/ppermute | solution.py:15
  255.2 5.3 %pad_maximum_fusion.3 = bf16[130,130,128]{2,1,0:T(8,128)(2,1)} fusion(bf16[1,130,128]{2,1,0:T(8,128)(2,1)S(1)} %collective-permute-done.8, bf16[128,1,128]{2,1,0:T(2,128)(2,1)S(1)} %collective-permute-done.6, bf16[128,128,128]{2,1,0:T(8,128)(2,1)S(1)} %fusion.7, bf16[128,1,128]{2,1,0:T(2,128)(2,1)S(1)} %collective-permute-done.5, ...), kind=kLoop, calls=%fused_computation.20 | loop fusion | flops 21632000 | bytes 8652800 | tf_op jit(solution)/shard_map/concatenate | solution.py:16
  261.7 16.7 %slice.204 = bf16[130,64,128]{2,1,0:T(8,128)(2,1)S(1)} slice(bf16[130,130,128]{2,1,0:T(8,128)(2,1)} %fusion.11), slice={[0:130:1], [0:128:2], [0:128:1]} | slice | bytes 4259840 | tf_op jit(solution)/shard_map/slice | solution.py:42
  278.4 18.3 %slice.205 = bf16[130,64,128]{2,1,0:T(8,128)(2,1)} slice(bf16[130,130,128]{2,1,0:T(8,128)(2,1)} %fusion.11), slice={[0:130:1], [1:129:2], [0:128:1]} | slice | bytes 4259840 | tf_op jit(solution)/shard_map/slice | solution.py:42
  296.6 18.3 %slice.206 = bf16[130,64,128]{2,1,0:T(8,128)(2,1)} slice(bf16[130,130,128]{2,1,0:T(8,128)(2,1)} %fusion.11), slice={[0:130:1], [2:130:2], [0:128:1]} | slice | bytes 4259840 | tf_op jit(solution)/shard_map/slice | solution.py:42
  318.4 6.0 %fusion.16 = (bf16[128,64,384]{2,1,0:T(8,128)(2,1)S(1)}, bf16[128,64,384]{2,1,0:T(8,128)(2,1)S(1)}, bf16[128,64,384]{2,1,0:T(8,128)(2,1)S(1)}) fusion(bf16[130,64,384]{2,1,0:T(8,128)(2,1)S(1)} %pad_maximum_fusion.1), kind=kLoop, calls=%fused_computation.44 | loop fusion | bytes 37748736 | tf_op jit(solution)/shard_map/slice | solution.py:46
  (62 shorter events, 33.4 us)
Async XLA Ops:
  2.4 21.0 %all-to-all-start = ((s32[128,1,96]{2,1,0:T(1,128)}), s32[128,1,96]{2,1,0:T(1,128)S(1)}, u32[]{:S(2)}, u32[]{:S(2)}) async-start(s32[128,1,96]{2,1,0:T(1,128)} %compare_select_fusion.1), calls=%async_computation | async-start | bytes 131072 | tf_op jit(solution)/shard_map/all_to_all | solution.py:74
  23.4 49.7 %all-to-all-start.1 = ((bf16[128,96,128]{2,1,0:T(8,128)(2,1)}), bf16[128,96,128]{2,1,0:T(8,128)(2,1)S(1)}, u32[]{:S(2)}, u32[]{:S(2)}) async-start(bf16[128,96,128]{2,1,0:T(8,128)(2,1)} %bitcast_select_fusion), calls=%async_computation.1 | async-start | bytes 6291456 | tf_op jit(solution)/shard_map/all_to_all | solution.py:73
  150.3 15.1 %copy-start.2 = (bf16[3,3,128,128]{3,2,1,0:T(8,128)(2,1)S(1)}, bf16[3,3,128,128]{3,2,1,0:T(8,128)(2,1)}, u32[]{:S(2)}) copy-start(bf16[3,3,128,128]{3,2,1,0:T(8,128)(2,1)} %param.20) | copy-start | bytes 884740
  156.2 2.0 copy-start
  158.3 8.4 %collective-permute-start = (bf16[128,1,128]{2,1,0:T(2,128)(2,1)S(1)}, bf16[128,1,128]{2,1,0:T(2,128)(2,1)S(1)}, u32[]{:S(2)}, u32[]{:S(2)}) collective-permute-start(bf16[128,1,128]{2,1,0:T(2,128)(2,1)S(1)} %get-tuple-element.68), channel_id=1, source_target_pairs={{0,1},{1,2},{2,3},{3,4},{4,5},{5,6},{6,7},{7,8},{8,9},{9,10},{10,1... | collective-permute-start | bytes 98312 | tf_op jit(solution)/shard_map/ppermute | solution.py:14
  165.4 4.0 %collective-permute-start.1 = (bf16[128,1,128]{2,1,0:T(2,128)(2,1)S(1)}, bf16[128,1,128]{2,1,0:T(2,128)(2,1)S(1)}, u32[]{:S(2)}, u32[]{:S(2)}) collective-permute-start(bf16[128,1,128]{2,1,0:T(2,128)(2,1)S(1)} %get-tuple-element.69), channel_id=1, source_target_pairs={{1,0},{2,1},{3,2},{4,3},{5,4},{6,5},{7,6},{8,7},{9,8},{10,9},{11,1... | collective-permute-start | bytes 98312 | tf_op jit(solution)/shard_map/ppermute | solution.py:15
  165.4 16.3 %copy-start.1 = (bf16[128,128,128]{2,1,0:T(8,128)(2,1)S(1)}, bf16[128,128,128]{2,1,0:T(8,128)(2,1)}, u32[]{:S(2)}) copy-start(bf16[128,128,128]{2,1,0:T(8,128)(2,1)} %copy-done) | copy-start | bytes 12582916
  170.2 7.0 %collective-permute-start.2 = (bf16[1,130,128]{2,1,0:T(8,128)(2,1)S(1)}, bf16[1,130,128]{2,1,0:T(8,128)(2,1)S(1)}, u32[]{:S(2)}, u32[]{:S(2)}) collective-permute-start(bf16[1,130,128]{2,1,0:T(8,128)(2,1)S(1)} %get-tuple-element.64), channel_id=1, source_target_pairs={{0,32},{32,64},{64,96},{1,33},{33,65},{65,97},{2,34},{34,66},{66,9... | collective-permute-start | bytes 99848 | tf_op jit(solution)/shard_map/ppermute | solution.py:14
  174.9 6.8 %collective-permute-start.3 = (bf16[1,130,128]{2,1,0:T(8,128)(2,1)S(1)}, bf16[1,130,128]{2,1,0:T(8,128)(2,1)S(1)}, u32[]{:S(2)}, u32[]{:S(2)}) collective-permute-start(bf16[1,130,128]{2,1,0:T(8,128)(2,1)S(1)} %get-tuple-element.65), channel_id=1, source_target_pairs={{32,0},{64,32},{96,64},{33,1},{65,33},{97,65},{34,2},{66,34},{98,6... | collective-permute-start | bytes 99848 | tf_op jit(solution)/shard_map/ppermute | solution.py:15
  176.9 8.7 %collective-permute-start.4 = (bf16[2,130,128]{2,1,0:T(8,128)(2,1)S(1)}, bf16[2,130,128]{2,1,0:T(8,128)(2,1)S(1)}, u32[]{:S(2)}, u32[]{:S(2)}) collective-permute-start(bf16[2,130,128]{2,1,0:T(8,128)(2,1)S(1)} %pad_maximum_fusion.4), channel_id=1, source_target_pairs={{0,16},{1,17},{2,18},{3,19},{4,20},{5,21},{6,22},{7,23},{8,24},{9,... | collective-permute-start | bytes 199688 | tf_op jit(solution)/shard_map/ppermute | solution.py:23
  215.6 11.7 %slice-start = ((s8[12582912]{0:T(1024)(128)(4,1)}), s8[4194304]{0:T(1024)(128)(4,1)S(1)}, s32[]{:S(2)}) async-start(s8[12582912]{0:T(1024)(128)(4,1)} %bitcast.38), calls=%async_computation.2 | async-start | bytes 8388608
  215.6 11.7 %slice-start.1 = ((s8[12582912]{0:T(1024)(128)(4,1)}), s8[4194304]{0:T(1024)(128)(4,1)S(1)}, s32[]{:S(2)}) async-start(s8[12582912]{0:T(1024)(128)(4,1)} %bitcast.38), calls=%async_computation.3 | async-start | bytes 8388608
  215.7 11.7 %slice-start.2 = ((s8[12582912]{0:T(1024)(128)(4,1)}), s8[4194304]{0:T(1024)(128)(4,1)S(1)}, s32[]{:S(2)}) async-start(s8[12582912]{0:T(1024)(128)(4,1)} %bitcast.38), calls=%async_computation.4 | async-start | bytes 8388608
  227.3 6.4 %copy-start.4 = (f32[128]{0:T(128)S(1)}, f32[128]{0:T(128)}, u32[]{:S(2)}) copy-start(f32[128]{0:T(128)} %param.21) | copy-start | bytes 1540
  233.7 8.9 %copy-start.3 = (bf16[3,3,128,128]{3,2,1,0:T(8,128)(2,1)S(1)}, bf16[3,3,128,128]{3,2,1,0:T(8,128)(2,1)}, u32[]{:S(2)}) copy-start(bf16[3,3,128,128]{3,2,1,0:T(8,128)(2,1)} %param.22) | copy-start | bytes 884740
  236.9 7.4 %collective-permute-start.5 = (bf16[128,1,128]{2,1,0:T(2,128)(2,1)S(1)}, bf16[128,1,128]{2,1,0:T(2,128)(2,1)S(1)}, u32[]{:S(2)}, u32[]{:S(2)}) collective-permute-start(bf16[128,1,128]{2,1,0:T(2,128)(2,1)S(1)} %get-tuple-element.66), channel_id=1, source_target_pairs={{0,1},{1,2},{2,3},{3,4},{4,5},{5,6},{6,7},{7,8},{8,9},{9,10},{10,1... | collective-permute-start | bytes 98312 | tf_op jit(solution)/shard_map/ppermute | solution.py:14
  237.7 6.6 %collective-permute-start.6 = (bf16[128,1,128]{2,1,0:T(2,128)(2,1)S(1)}, bf16[128,1,128]{2,1,0:T(2,128)(2,1)S(1)}, u32[]{:S(2)}, u32[]{:S(2)}) collective-permute-start(bf16[128,1,128]{2,1,0:T(2,128)(2,1)S(1)} %get-tuple-element.67), channel_id=1, source_target_pairs={{1,0},{2,1},{3,2},{4,3},{5,4},{6,5},{7,6},{8,7},{9,8},{10,9},{11,1... | collective-permute-start | bytes 98312 | tf_op jit(solution)/shard_map/ppermute | solution.py:15
  244.3 6.1 %collective-permute-start.7 = (bf16[1,130,128]{2,1,0:T(8,128)(2,1)S(1)}, bf16[1,130,128]{2,1,0:T(8,128)(2,1)S(1)}, u32[]{:S(2)}, u32[]{:S(2)}) collective-permute-start(bf16[1,130,128]{2,1,0:T(8,128)(2,1)S(1)} %get-tuple-element.62), channel_id=1, source_target_pairs={{0,32},{32,64},{64,96},{1,33},{33,65},{65,97},{2,34},{34,66},{66,9... | collective-permute-start | bytes 99848 | tf_op jit(solution)/shard_map/ppermute | solution.py:14
  248.4 6.8 %collective-permute-start.8 = (bf16[1,130,128]{2,1,0:T(8,128)(2,1)S(1)}, bf16[1,130,128]{2,1,0:T(8,128)(2,1)S(1)}, u32[]{:S(2)}, u32[]{:S(2)}) collective-permute-start(bf16[1,130,128]{2,1,0:T(8,128)(2,1)S(1)} %get-tuple-element.63), channel_id=1, source_target_pairs={{32,0},{64,32},{96,64},{33,1},{65,33},{97,65},{34,2},{66,34},{98,6... | collective-permute-start | bytes 99848 | tf_op jit(solution)/shard_map/ppermute | solution.py:15
  250.3 10.1 %collective-permute-start.9 = (bf16[2,130,128]{2,1,0:T(8,128)(2,1)S(1)}, bf16[2,130,128]{2,1,0:T(8,128)(2,1)S(1)}, u32[]{:S(2)}, u32[]{:S(2)}) collective-permute-start(bf16[2,130,128]{2,1,0:T(8,128)(2,1)S(1)} %pad_maximum_fusion.5), channel_id=1, source_target_pairs={{0,16},{1,17},{2,18},{3,19},{4,20},{5,21},{6,22},{7,23},{8,24},{9,... | collective-permute-start | bytes 199688 | tf_op jit(solution)/shard_map/ppermute | solution.py:23
  327.7 1.0 copy-start.5
where the time goes:
time: 332 us; the launch traced here: 330 us
  other arithmetic  118 us (36%)
  local copies, waits for them, and re-layouts  85.2 us (26%)
  waiting for transfers between devices  56.9 us (17%)
  starting transfers between devices  45.2 us (14%)
  matrix products  24.5 us (7%)
    scatter-add x1, other arithmetic, shards(): jnp.zeros((rows * cols, chans), jnp.float32).at[flat_cells].add(flat_values)  77.2 us
    slice x4, local copies, waits for them, and re-layouts, convolve(): padded[:, dj:dj + cols * stride:stride]  58.2 us
    all_to_all x1, waiting for transfers between devices, shards(): lax.all_to_all(sent, ('lat', 'lon'), split_axis=0, concat_axis=0, tiled=T...  40.2 us
    dot_general x6, matrix products, convolve(): jnp.dot(window.reshape(rows * cols, 3 * chans), weight[di].reshape(3 * ch...  24.5 us
    slice x2, local copies, waits for them, and re-layouts, convolve(): window = widened[di:di + rows * stride]  21.8 us
    ppermute x4, starting transfers between devices, padded_2(): before = lax.ppermute(last, axis, up)  16.6 us
    ppermute x4, waiting for transfers between devices, padded_2(): after = lax.ppermute(leading, axis, down)  11.9 us
    all_to_all x1, starting transfers between devices, shards(): lax.all_to_all(places, ('lat', 'lon'), split_axis=0, concat_axis=0, tiled...  11.5 us
  transfers between devices with their start and end apart: 12, of which 7 were waited for; matrix products, arithmetic and copies ran while one was open for 6% of the time, Pallas kernels for 0%

commit v1 on v0

v1 whole, which is shorter than its diff:
```python
import functools

import jax
import jax.numpy as jnp
from jax import lax
from jax.experimental import pallas as pl
from jax.experimental.pallas import tpu as pltpu
from jax.sharding import PartitionSpec as P

PITCH, ODD, EVEN = 152, 8, 80
SLABS = 138
NACC = 4
META = 8
GELU_A, GELU_B = 0.7978845608028654, 0.044715
VMEM = pl.BlockSpec(memory_space=pltpu.VMEM)
SMEM = pl.BlockSpec(memory_space=pltpu.SMEM)
ANY = pl.BlockSpec(memory_space=pl.ANY)


def on_chip(x):
    return pltpu.with_memory_space_constraint(x, pltpu.VMEM)


def gelu(x):
    return 0.5 * x * (1.0 + jnp.tanh(GELU_A * (x + GELU_B * (x * x * x))))


def pack_kernel(values_ref, cells_ref, counts_ref, out_ref, meta_ref, sem):
    slots = values_ref.shape[1]
    body = pltpu.make_async_copy(values_ref, out_ref.at[:, pl.ds(0, slots), :], sem.at[0])
    body.start()
    cells = cells_ref[...]
    live = lax.broadcasted_iota(jnp.int32, cells.shape, 1) < counts_ref[...]
    row = cells >> 7
    col = cells & 127
    high = jnp.where(live, row + 2, 0).astype(jnp.float32)
    low = jnp.where(live, (col >> 1) + jnp.where((col & 1) == 1, ODD, EVEN), 0).astype(jnp.float32)
    both = jnp.concatenate(
        [high[:, None, :], low[:, None, :], jnp.zeros((cells.shape[0], META - 2, 128), jnp.float32)], axis=1
    )
    meta_ref[...] = both.astype(jnp.bfloat16)
    tail = pltpu.make_async_copy(meta_ref, out_ref.at[:, pl.ds(slots, META), :], sem.at[1])
    tail.start()
    body.wait()
    tail.wait()


def pack(values, cells, counts):
    owners, slots, chans = values.shape
    return pl.pallas_call(
        pack_kernel,
        out_shape=jax.ShapeDtypeStruct((owners, slots + META, chans), jnp.bfloat16),
        in_specs=[ANY, VMEM, VMEM],
        out_specs=ANY,
        scratch_shapes=[
            pltpu.VMEM((owners, META, chans), jnp.bfloat16),
            pltpu.SemaphoreType.DMA((2,)),
        ],
        compiler_params=pltpu.CompilerParams(vmem_limit_bytes=8 << 20),
        name="pack",
    )(values, jnp.pad(cells, ((0, 0), (0, 128 - slots))), counts)


def spread_kernel(field_ref, acc_ref, wide_ref):
    def step(r, carry):
        wide_ref[...] = field_ref[r].astype(jnp.float32)
        base = pl.multiple_of((r + 2) * PITCH, 8)
        acc_ref[pl.ds(base + ODD, 64), :] = wide_ref[pl.ds(1, 64, stride=2), :]
        acc_ref[pl.ds(base + EVEN, 64), :] = wide_ref[pl.ds(0, 64, stride=2), :]
        return carry

    lax.fori_loop(0, field_ref.shape[0], step, 0)


def spread(field):
    return pl.pallas_call(
        spread_kernel,
        out_shape=pltpu.VMEM((SLABS * PITCH, 128), jnp.float32),
        in_specs=[VMEM],
        out_specs=VMEM,
        scratch_shapes=[pltpu.VMEM((128, 128), jnp.float32)],
        compiler_params=pltpu.CompilerParams(vmem_limit_bytes=12 << 20),
        name="spread",
    )(field)


def scatter_kernel(got_ref, start_ref, acc_ref, right_ref, left_ref, rows_ref, *rest):
    more = rest[: NACC - 1]
    wide_ref, meta_ref, index_ref, place_ref, sem = rest[NACC - 1 :]
    del start_ref
    sources, slots = got_ref.shape[0], got_ref.shape[1] - META

    def unpack(s, carry):
        meta_ref[pl.ds(pl.multiple_of(s * META, META), META), :] = got_ref[s, pl.ds(slots, META), :].astype(jnp.float32)
        return carry

    lax.fori_loop(0, sources, unpack, 0, unroll=8)
    high = meta_ref[pl.ds(0, sources, stride=META), :]
    low = meta_ref[pl.ds(1, sources, stride=META), :]
    index_ref[...] = (high * PITCH + low).astype(jnp.int32)
    copy = pltpu.make_async_copy(index_ref, place_ref, sem)
    copy.start()

    def clear(r, carry):
        base = pl.multiple_of((r + 2) * PITCH, 8)
        for acc in more:
            acc[pl.ds(base, PITCH), :] = jnp.zeros((PITCH, 128), jnp.float32)
        return carry

    lax.fori_loop(0, 128, clear, 0)
    copy.wait()
    accs = (acc_ref, *more)

    def add(s, carry):
        wide_ref[...] = got_ref[s, pl.ds(0, slots), :].astype(jnp.float32)
        for k in range(slots):
            acc = accs[k % NACC]
            i = place_ref[s, k]
            acc[pl.ds(i, 1), :] = acc[pl.ds(i, 1), :] + wide_ref[pl.ds(k, 1), :]
        return carry

    lax.fori_loop(0, sources, add, 0)

    def merge(r, carry):
        here = pl.ds(pl.multiple_of((r + 2) * PITCH, 8), PITCH)
        total = acc_ref[here, :]
        for acc in more:
            total = total + acc[here, :]
        acc_ref[here, :] = total
        return carry

    lax.fori_loop(0, 128, merge, 0)
    right_ref[0] = acc_ref[pl.ds(2 * PITCH + EVEN + 63, 128, stride=PITCH), :].astype(jnp.bfloat16)
    right_ref[1] = acc_ref[pl.ds(2 * PITCH + ODD + 63, 128, stride=PITCH), :].astype(jnp.bfloat16)
    left_ref[...] = acc_ref[pl.ds(2 * PITCH + EVEN, 128, stride=PITCH), :].astype(jnp.bfloat16)
    for n, r in enumerate((0, 1, 126, 127)):
        base = (r + 2) * PITCH
        rows_ref[n, pl.ds(0, 64), :] = acc_ref[pl.ds(base + ODD, 64), :].astype(jnp.bfloat16)
        rows_ref[n, pl.ds(64, 64), :] = acc_ref[pl.ds(base + EVEN, 64), :].astype(jnp.bfloat16)


def scatter(got, start):
    return pl.pallas_call(
        scatter_kernel,
        out_shape=[
            pltpu.VMEM(start.shape, jnp.float32),
            jax.ShapeDtypeStruct((2, 128, 128), jnp.bfloat16),
            jax.ShapeDtypeStruct((128, 128), jnp.bfloat16),
            jax.ShapeDtypeStruct((4, 128, 128), jnp.bfloat16),
        ],
        in_specs=[VMEM, VMEM],
        out_specs=[VMEM] * 4,
        scratch_shapes=[pltpu.VMEM((130 * PITCH, 128), jnp.float32)] * (NACC - 1)
        + [
            pltpu.VMEM((96, 128), jnp.float32),
            pltpu.VMEM((128 * META, 128), jnp.float32),
            pltpu.VMEM((128, 128), jnp.int32),
            pltpu.SMEM((128, 128), jnp.int32),
            pltpu.SemaphoreType.DMA,
        ],
        input_output_aliases={1: 0},
        compiler_params=pltpu.CompilerParams(vmem_limit_bytes=40 << 20),
        name="scatter",
    )(on_chip(got), on_chip(start))


def conv_kernel(
    band_ref,
    start_ref,
    west_ref,
    east_ref,
    down_ref,
    up_ref,
    across_ref,
    w1_ref,
    w1s_ref,
    b1_ref,
    w2_ref,
    b2_ref,
    acc_ref,
    out_ref,
    lhs_ref,
    col_ref,
    shift_ref,
    even_ref,
    odd_ref,
):
    del start_ref
    f32, bf16 = jnp.float32, jnp.bfloat16
    band = band_ref[0]
    dot = functools.partial(jnp.dot, preferred_element_type=f32)

    acc_ref[pl.ds(2 * PITCH + EVEN - 1, 128, stride=PITCH), :] = west_ref[0].astype(f32)
    acc_ref[pl.ds(2 * PITCH + ODD - 1, 128, stride=PITCH), :] = west_ref[1].astype(f32)
    acc_ref[pl.ds(2 * PITCH + EVEN + 64, 128, stride=PITCH), :] = east_ref[...].astype(f32)

    def put(slab, row):
        base = slab * PITCH
        acc_ref[pl.ds(base + ODD, 64), :] = row[0:64]
        acc_ref[pl.ds(base + EVEN, 64), :] = row[64:128]
        acc_ref[pl.ds(base + EVEN - 1, 1), :] = row[128:129]
        acc_ref[pl.ds(base + ODD - 1, 1), :] = row[129:130]
        acc_ref[pl.ds(base + EVEN + 64, 1), :] = row[130:131]

    north = band == 0
    south = band == 3
    put(0, jnp.where(north, across_ref[1].astype(f32), down_ref[0].astype(f32)))
    put(1, jnp.where(north, across_ref[0].astype(f32), down_ref[1].astype(f32)))
    put(130, jnp.where(south, across_ref[1].astype(f32), up_ref[0].astype(f32)))
    first = jnp.where(north, 2, 0)
    last = 2 - first
    flipped = (first, 1, last)

    def fill(slab):
        base = pl.multiple_of(slab * PITCH, 8)
        parts = [acc_ref[pl.ds(base + at, 64), :].astype(bf16) for at in (ODD - 1, EVEN, ODD, EVEN + 1)]
        lhs_ref[slab] = jnp.concatenate(parts, axis=-1)

    bias = b1_ref[...]
    total = jnp.zeros((136, 128), f32) + bias
    top = jnp.zeros((8, 128), f32) + bias
    for di in range(3):
        parts = [
            acc_ref[pl.ds(di * PITCH + at, 136, stride=PITCH), :].astype(bf16) for at in (EVEN - 1, ODD - 1, EVEN)
        ]
        window = jnp.concatenate(parts, axis=-1)
        total = total + dot(window, w1s_ref[di])
        top = top + dot(window[0:8], w1s_ref[flipped[di]])
    col_ref[pl.ds(0, 136), :] = gelu(total)
    col_ref[pl.ds(0, 1), :] = gelu(top)[0:1]

    bias2 = jnp.concatenate([bias, bias], axis=-1)

    def fill_step(slab, carry):
        fill(slab)
        return carry

    lax.fori_loop(0, 131, fill_step, 0)
    pre = bias2
    for di in range(3):
        pre = pre + dot(lhs_ref[di], w1_ref[flipped[di]])
    hid = gelu(pre)
    shift_ref[0, pl.ds(8, 64), :] = hid[:, 128:]
    shift_ref[0, pl.ds(7, 1), :] = col_ref[pl.ds(0, 1), :]
    odd_ref[0] = jnp.concatenate([shift_ref[0, pl.ds(7, 64), :], hid[:, :128], hid[:, 128:]], axis=-1).astype(bf16)

    def step(b, carry):
        pre = jnp.broadcast_to(bias2, (512, 256))
        for di in range(3):
            window = lhs_ref[pl.ds(b * 8 + 1 + di, 8)].reshape(512, 512)
            pre = pre + dot(window, w1_ref[di])
        hid = gelu(pre).reshape(8, 64, 256)
        shift_ref[:, pl.ds(8, 64), :] = hid[:, :, 128:]
        for n in range(8):
            shift_ref[n, pl.ds(7, 1), :] = col_ref[pl.ds(b * 8 + 1 + n, 1), :]
        wide = jnp.concatenate([shift_ref[:, pl.ds(7, 64), :], hid[:, :, :128], hid[:, :, 128:]], axis=-1)
        wide = wide.astype(bf16).reshape(4, 2, 64, 384)
        even_ref[pl.ds(b * 4, 4)] = wide[:, 0]
        odd_ref[pl.ds(b * 4 + 1, 4)] = wide[:, 1]
        return carry

    lax.fori_loop(0, 16, step, 0)

    def finish(b, carry):
        total = jnp.broadcast_to(b2_ref[...], (256, 128))
        total = total + dot(odd_ref[pl.ds(b * 4, 4)].reshape(256, 384), w2_ref[0])
        total = total + dot(even_ref[pl.ds(b * 4, 4)].reshape(256, 384), w2_ref[1])
        total = total + dot(odd_ref[pl.ds(b * 4 + 1, 4)].reshape(256, 384), w2_ref[2])
        out_ref[pl.ds(b * 4, 4)] = total.reshape(4, 64, 128).astype(bf16)
        return carry

    lax.fori_loop(0, 16, finish, 0)


def convolve(band, field, west, east, down, up, across, w1, w1s, b1, w2, b2):
    return pl.pallas_call(
        conv_kernel,
        out_shape=[
            pltpu.VMEM(field.shape, jnp.float32),
            jax.ShapeDtypeStruct((64, 64, 128), jnp.bfloat16),
        ],
        in_specs=[SMEM] + [VMEM] * 11,
        out_specs=[VMEM, VMEM],
        scratch_shapes=[
            pltpu.VMEM((131, 64, 512), jnp.bfloat16),
            pltpu.VMEM((136, 128), jnp.float32),
            pltpu.VMEM((8, 72, 128), jnp.float32),
            pltpu.VMEM((64, 64, 384), jnp.bfloat16),
            pltpu.VMEM((65, 64, 384), jnp.bfloat16),
        ],
        input_output_aliases={1: 0},
        compiler_params=pltpu.CompilerParams(vmem_limit_bytes=32 << 20),
        name="convolve",
    )(band, on_chip(field), west, east, down, up, across, w1, w1s, b1, w2, b2)[1]


def shards(background, values, cells, counts, w1, b1, w2, b2):
    lat, lon = lax.axis_size("lat"), lax.axis_size("lon")
    band = lax.axis_index("lat")
    east_pairs = [(i, (i + 1) % lon) for i in range(lon)]
    west_pairs = [(j, i) for i, j in east_pairs]
    down_pairs = [(i, i + 1) for i in range(lat - 1)]
    up_pairs = [(j, i) for i, j in down_pairs]
    pole_pairs = [(b * lon + i, b * lon + (i + lon // 2) % lon) for b in (0, lat - 1) for i in range(lon)]

    sent = pack(values[0], cells[0], counts[0][:, None])
    got = lax.all_to_all(sent, ("lat", "lon"), split_axis=0, concat_axis=0, tiled=True)
    field, right, left, rows = scatter(got, spread(background))

    west = lax.ppermute(right, "lon", east_pairs)
    east = lax.ppermute(left, "lon", west_pairs)
    cols = jnp.concatenate([west, east[None]], axis=0)
    sides = jnp.concatenate([cols[:, 0:2], cols[:, 126:128]], axis=1).transpose(1, 0, 2)
    rows = jnp.concatenate([rows, sides, jnp.zeros((4, 5, 128), jnp.bfloat16)], axis=1)
    down = lax.ppermute(rows[2:], "lat", down_pairs)
    up = lax.ppermute(rows[:2], "lat", up_pairs)
    across = lax.ppermute(jnp.where(band == 0, rows[:2], rows[2:]), ("lat", "lon"), pole_pairs)

    flat = w1.reshape(3, 384, 128)
    blank = jnp.zeros((3, 128, 128), jnp.bfloat16)
    paired = jnp.concatenate(
        [jnp.concatenate([flat, blank], axis=1), jnp.concatenate([blank, flat], axis=1)], axis=2
    )
    return convolve(
        band[None],
        field,
        west,
        east,
        down,
        up,
        across,
        paired,
        flat,
        b1[None],
        w2.reshape(3, 384, 128),
        b2[None],
    )


def solution(mesh):
    placed = (
        P("lat", "lon", None),
        P(("lat", "lon"), None, None, None),
        P(("lat", "lon"), None, None),
        P(("lat", "lon"), None),
        P(),
        P(),
        P(),
        P(),
    )
    return jax.shard_map(
        shards, mesh=mesh, in_specs=placed, out_specs=P("lat", "lon", None), check_vma=False
    )
```

time: 332 us -> 142 us (0.43)
  other arithmetic: 118 us -> 1.3 us
  local copies, waits for them, and re-layouts: 85.2 us -> 24.1 us
  Pallas kernels: 0 us -> 49.7 us
  matrix products: 24.5 us -> 0 us
  starting transfers between devices: 45.2 us -> 23.6 us
  waiting for transfers between devices: 56.9 us -> 42.1 us
    slice x13 -> x0, local copies, waits for them, and re-layouts: 81.7 us -> none  [the longest x4 58.2 us: convolve(): padded[:, dj:dj + cols * stride:stride]]
    scatter-add x1 -> x0, other arithmetic: 77.2 us -> none  [shards(): jnp.zeros((rows * cols, chans), jnp.float32).at[flat_cells].add(flat_values)]
    pallas_call x0 -> x4, Pallas kernels: none -> 49.7 us  [the longest x1 26.4 us: scatter(): pl.pallas_call(scatter_kernel, out_shape=[pltpu.VMEM(start.shape, jnp.flo...]
    dot_general x6 -> x0, matrix products: 24.5 us -> none  [convolve(): jnp.dot(window.reshape(rows * cols, 3 * chans), weight[di].reshape(3 * ch...]
    unnamed x19 -> x21, local copies, waits for them, and re-layouts: 2.88 us -> 23.1 us
    concatenate x4 -> x2, other arithmetic: 18.2 us -> 1.26 us  [the longest x1 1.17 us: shards(): jnp.concatenate([jnp.concatenate([flat, blank], axis=1), jnp.concatenate(...]
    ppermute x10 -> x5, starting transfers between devices: 25.8 us -> 12.1 us  [the longest x1 5.67 us: shards(): east = lax.ppermute(left, 'lon', west_pairs)]
    all_to_all x1 -> x0, starting transfers between devices: 11.5 us -> none  [shards(): lax.all_to_all(places, ('lat', 'lon'), split_axis=0, concat_axis=0, tiled...]
  transfers between devices with their start and end apart: 12 -> 6, of which waited for: 7 -> 4; matrix products, arithmetic and copies ran while one was open for 6% -> 1% of each run, Pallas kernels for 0% -> 1%
where the time goes in v1:
time: 142 us; the launch traced here: 141 us
  Pallas kernels  49.7 us (35%)
  waiting for transfers between devices  42.1 us (30%)
  local copies, waits for them, and re-layouts  24.1 us (17%)
  starting transfers between devices  23.6 us (17%)
    all_to_all x1, waiting for transfers between devices, shards(): lax.all_to_all(sent, ('lat', 'lon'), split_axis=0, concat_axis=0, tiled=T...  36.6 us
    pallas_call x1, Pallas kernels, scatter(): pl.pallas_call(scatter_kernel, out_shape=[pltpu.VMEM(start.shape, jnp.flo...  26.4 us
    unnamed x21, local copies, waits for them, and re-layouts  23.1 us
    pallas_call x1, Pallas kernels, convolve(): pl.pallas_call(conv_kernel, out_shape=[pltpu.VMEM(field.shape, jnp.float3...  19.6 us
    all_to_all x1, starting transfers between devices, shards(): lax.all_to_all(sent, ('lat', 'lon'), split_axis=0, concat_axis=0, tiled=T...  11.5 us
    ppermute x1, starting transfers between devices, shards(): east = lax.ppermute(left, 'lon', west_pairs)  5.67 us
    ppermute x1, starting transfers between devices, shards(): down = lax.ppermute(rows[2:], 'lat', down_pairs)  3.82 us
    ppermute x1, waiting for transfers between devices, shards(): up = lax.ppermute(rows[:2], 'lat', up_pairs)  3.57 us
  transfers between devices with their start and end apart: 6, of which 4 were waited for; matrix products, arithmetic and copies ran while one was open for 1% of the time, Pallas kernels for 1%

profile of v1, /device:TPU:1, one launch (start us, length us, event | category | flops | bytes accessed | tf_op | source)
XLA Modules:
  0.0 141.0 jit_solution(15333969680044583588)
XLA Ops:
  0.0 0.9 copy.15
  0.9 0.8 copy.16.counts_ref
  1.7 1.9 %copy-done.5 = bf16[1,128,96,128]{3,2,1,0:T(8,128)(2,1)S(1)} copy-done((bf16[1,128,96,128]{3,2,1,0:T(8,128)(2,1)S(1)}, bf16[1,128,96,128]{3,2,1,0:T(8,128)(2,1)}, u32[]{:S(2)}) %copy-start.5) | copy-done | bytes 3145752
  3.6 1.9 %pack.1 = bf16[128,104,128]{2,1,0:T(8,128)(2,1)} custom-call(bf16[128,96,128]{2,1,0:T(8,128)(2,1)S(1)} %bitcast.11, s32[128,128]{1,0:T(8,128)S(1)} %pad.6.cells_ref, s32[128,1]{1,0:T(8,128)S(1)} %copy.16.counts_ref), custom_call_target="tpu_custom_call" | custom-call | tf_op jit(solution)/shard_map/pack/pallas_call | solution.py:50
  5.5 11.5 %all-to-all-start = ((bf16[128,104,128]{2,1,0:T(8,128)(2,1)}), bf16[128,104,128]{2,1,0:T(8,128)(2,1)S(1)}, u32[]{:S(2)}, u32[]{:S(2)}) async-start(bf16[128,104,128]{2,1,0:T(8,128)(2,1)} %pack.1), calls=%async_computation | async-start | bytes 6815744 | tf_op jit(solution)/shard_map/all_to_all | solution.py:307
  17.0 2.2 %copy-done.4 = bf16[128,128,128]{2,1,0:T(8,128)(2,1)S(1)} copy-done((bf16[128,128,128]{2,1,0:T(8,128)(2,1)S(1)}, bf16[128,128,128]{2,1,0:T(8,128)(2,1)}, u32[]{:S(2)}) %copy-start.4) | copy-done | bytes 4194328
  19.2 1.8 %spread.1.start_ref = f32[20976,128]{1,0:T(8,128)S(1)} custom-call(bf16[128,128,128]{2,1,0:T(8,128)(2,1)S(1)} %copy-done.4), custom_call_target="tpu_custom_call" | custom-call | tf_op jit(solution)/shard_map/spread/pallas_call | solution.py:76
  21.0 4.1 %copy-done = f32[20976,128]{1,0:T(8,128)} copy-done((f32[20976,128]{1,0:T(8,128)}, f32[20976,128]{1,0:T(8,128)S(1)}, u32[]{:S(2)}) %copy-start) | copy-done | bytes 10739736
  25.1 36.6 %all-to-all-done.got_ref = bf16[128,104,128]{2,1,0:T(8,128)(2,1)S(1)} async-done(((bf16[128,104,128]{2,1,0:T(8,128)(2,1)}), bf16[128,104,128]{2,1,0:T(8,128)(2,1)S(1)}, u32[]{:S(2)}, u32[]{:S(2)}) %all-to-all-start) | async-done | bytes 3407904 | tf_op jit(solution)/shard_map/all_to_all | solution.py:307
  61.6 4.0 %copy-done.1 = f32[20976,128]{1,0:T(8,128)S(1)} copy-done((f32[20976,128]{1,0:T(8,128)S(1)}, f32[20976,128]{1,0:T(8,128)}, u32[]{:S(2)}) %copy-start.1) | copy-done | bytes 10739736
  65.7 26.4 %scatter.1 = (f32[20976,128]{1,0:T(8,128)S(1)}, bf16[2,128,128]{2,1,0:T(8,128)(2,1)S(1)}, bf16[128,128]{1,0:T(8,128)(2,1)}, bf16[4,128,128]{2,1,0:T(8,128)(2,1)S(1)}) custom-call(bf16[128,104,128]{2,1,0:T(8,128)(2,1)S(1)} %all-to-all-done.got_ref, f32[20976,128]{1,0:T(8,128)S(1)} %copy-done.1), custom_call_target="tpu_custom_call", output_to_operand_aliasing={{0}: (1, {})} | custom-call | tf_op jit(solution)/shard_map/scatter/pallas_call | solution.py:143
  92.0 4.1 %copy-done.2 = f32[20976,128]{1,0:T(8,128)} copy-done((f32[20976,128]{1,0:T(8,128)}, f32[20976,128]{1,0:T(8,128)S(1)}, u32[]{:S(2)}) %copy-start.2) | copy-done | bytes 10739736
  96.3 5.7 %collective-permute-start.1 = (bf16[128,128]{1,0:T(8,128)(2,1)}, bf16[128,128]{1,0:T(8,128)(2,1)S(1)}, u32[]{:S(2)}, u32[]{:S(2)}) collective-permute-start(bf16[128,128]{1,0:T(8,128)(2,1)} %get-tuple-element.12), channel_id=1, source_target_pairs={{1,0},{2,1},{3,2},{4,3},{5,4},{6,5},{7,6},{8,7},{9,8},{10,9},{11,1... | collective-permute-start | bytes 98312 | tf_op jit(solution)/shard_map/ppermute | solution.py:311
  102.0 1.3 collective-permute-done.1.east_ref
  103.4 0.7 collective-permute-done
  104.2 3.8 %collective-permute-start.2 = (bf16[2,136,128]{2,1,0:T(8,128)(2,1)S(1)}, bf16[2,136,128]{2,1,0:T(8,128)(2,1)S(1)}, u32[]{:S(2)}, u32[]{:S(2)}) collective-permute-start(bf16[2,136,128]{2,1,0:T(8,128)(2,1)S(1)} %get-tuple-element.17), channel_id=1, source_target_pairs={{0,32},{32,64},{64,96},{1,33},{33,65},{65,97},{2,34},{34,66},{66,9... | collective-permute-start | bytes 208904 | tf_op jit(solution)/shard_map/ppermute | solution.py:315
  108.0 1.9 %collective-permute-start.3 = (bf16[2,136,128]{2,1,0:T(8,128)(2,1)S(1)}, bf16[2,136,128]{2,1,0:T(8,128)(2,1)S(1)}, u32[]{:S(2)}, u32[]{:S(2)}) collective-permute-start(bf16[2,136,128]{2,1,0:T(8,128)(2,1)S(1)} %get-tuple-element.16), channel_id=1, source_target_pairs={{32,0},{64,32},{96,64},{33,1},{65,33},{97,65},{34,2},{66,34},{98,6... | collective-permute-start | bytes 208904 | tf_op jit(solution)/shard_map/ppermute | solution.py:316
  110.0 0.7 collective-permute-start.4
  110.6 1.2 fusion.2.w1_ref
  111.8 3.6 %collective-permute-done.3.up_ref = bf16[2,136,128]{2,1,0:T(8,128)(2,1)S(1)} collective-permute-done((bf16[2,136,128]{2,1,0:T(8,128)(2,1)S(1)}, bf16[2,136,128]{2,1,0:T(8,128)(2,1)S(1)}, u32[]{:S(2)}, u32[]{:S(2)}) %collective-permute-start.3) | collective-permute-done | bytes 69664 | tf_op jit(solution)/shard_map/ppermute | solution.py:316
  115.4 4.0 %copy-done.3 = f32[20976,128]{1,0:T(8,128)S(1)} copy-done((f32[20976,128]{1,0:T(8,128)S(1)}, f32[20976,128]{1,0:T(8,128)}, u32[]{:S(2)}) %copy-start.3) | copy-done | bytes 10739736
  119.5 1.0 copy-done.6
  120.4 1.0 copy-done.7
  121.4 19.6 %convolve.1 = (f32[20976,128]{1,0:T(8,128)S(1)}, bf16[64,64,128]{2,1,0:T(8,128)(2,1)}) custom-call(s32[1]{0:T(128)} %bitcast.band_ref, f32[20976,128]{1,0:T(8,128)S(1)} %copy-done.3, bf16[2,128,128]{2,1,0:T(8,128)(2,1)S(1)} %copy.19.west_ref, bf16[128,128]{1,0:T(8,128)(2,1)S(1)} %collective-permute-done.1.east_ref, ...), custom_call_target="tpu_custom_call", output_to_operand_aliasing={{0}: (1, {})} | custom-call | tf_op jit(solution)/shard_map/convolve/pallas_call | solution.py:276
  (24 shorter events, 0.5 us)
Async XLA Ops:
  1.7 1.9 %copy-start.5 = (bf16[1,128,96,128]{3,2,1,0:T(8,128)(2,1)S(1)}, bf16[1,128,96,128]{3,2,1,0:T(8,128)(2,1)}, u32[]{:S(2)}) copy-start(bf16[1,128,96,128]{3,2,1,0:T(8,128)(2,1)} %param.9) | copy-start | bytes 9437188
  5.5 56.2 %all-to-all-start = ((bf16[128,104,128]{2,1,0:T(8,128)(2,1)}), bf16[128,104,128]{2,1,0:T(8,128)(2,1)S(1)}, u32[]{:S(2)}, u32[]{:S(2)}) async-start(bf16[128,104,128]{2,1,0:T(8,128)(2,1)} %pack.1), calls=%async_computation | async-start | bytes 6815744 | tf_op jit(solution)/shard_map/all_to_all | solution.py:307
  17.0 2.2 %copy-start.4 = (bf16[128,128,128]{2,1,0:T(8,128)(2,1)S(1)}, bf16[128,128,128]{2,1,0:T(8,128)(2,1)}, u32[]{:S(2)}) copy-start(bf16[128,128,128]{2,1,0:T(8,128)(2,1)} %field_ref.1) | copy-start | bytes 12582916
  21.0 4.1 %copy-start = (f32[20976,128]{1,0:T(8,128)}, f32[20976,128]{1,0:T(8,128)S(1)}, u32[]{:S(2)}) copy-start(f32[20976,128]{1,0:T(8,128)S(1)} %spread.1.start_ref) | copy-start | bytes 32219140
  61.6 4.1 %copy-start.1 = (f32[20976,128]{1,0:T(8,128)S(1)}, f32[20976,128]{1,0:T(8,128)}, u32[]{:S(2)}) copy-start(f32[20976,128]{1,0:T(8,128)} %copy-done) | copy-start | bytes 32219140
  65.7 49.7 %copy-start.8 = (f32[128]{0:T(128)S(1)}, f32[128]{0:T(128)}, u32[]{:S(2)}) copy-start(f32[128]{0:T(128)} %param.13) | copy-start | bytes 1540
  65.7 49.7 %copy-start.9 = (f32[128]{0:T(128)S(1)}, f32[128]{0:T(128)}, u32[]{:S(2)}) copy-start(f32[128]{0:T(128)} %param.15) | copy-start | bytes 1540
  92.0 4.1 %copy-start.2 = (f32[20976,128]{1,0:T(8,128)}, f32[20976,128]{1,0:T(8,128)S(1)}, u32[]{:S(2)}) copy-start(f32[20976,128]{1,0:T(8,128)S(1)} %get-tuple-element.10.start_ref) | copy-start | bytes 32219140
  96.2 7.9 %collective-permute-start = (bf16[2,128,128]{2,0,1:T(2,128)(2,1)S(1)}, bf16[2,128,128]{2,0,1:T(2,128)(2,1)S(1)}, u32[]{:S(2)}, u32[]{:S(2)}) collective-permute-start(bf16[2,128,128]{2,0,1:T(2,128)(2,1)S(1)} %copy.17), channel_id=1, source_target_pairs={{0,1},{1,2},{2,3},{3,4},{4,5},{5,6},{6,7},{7,8},{8,9},{9,10},{10,1... | collective-permute-start | bytes 196616 | tf_op jit(solution)/shard_map/ppermute | solution.py:310
  96.3 7.0 %collective-permute-start.1 = (bf16[128,128]{1,0:T(8,128)(2,1)}, bf16[128,128]{1,0:T(8,128)(2,1)S(1)}, u32[]{:S(2)}, u32[]{:S(2)}) collective-permute-start(bf16[128,128]{1,0:T(8,128)(2,1)} %get-tuple-element.12), channel_id=1, source_target_pairs={{1,0},{2,1},{3,2},{4,3},{5,4},{6,5},{7,6},{8,7},{9,8},{10,9},{11,1... | collective-permute-start | bytes 98312 | tf_op jit(solution)/shard_map/ppermute | solution.py:311
  104.2 7.6 %collective-permute-start.2 = (bf16[2,136,128]{2,1,0:T(8,128)(2,1)S(1)}, bf16[2,136,128]{2,1,0:T(8,128)(2,1)S(1)}, u32[]{:S(2)}, u32[]{:S(2)}) collective-permute-start(bf16[2,136,128]{2,1,0:T(8,128)(2,1)S(1)} %get-tuple-element.17), channel_id=1, source_target_pairs={{0,32},{32,64},{64,96},{1,33},{33,65},{65,97},{2,34},{34,66},{66,9... | collective-permute-start | bytes 208904 | tf_op jit(solution)/shard_map/ppermute | solution.py:315
  108.0 7.4 %collective-permute-start.3 = (bf16[2,136,128]{2,1,0:T(8,128)(2,1)S(1)}, bf16[2,136,128]{2,1,0:T(8,128)(2,1)S(1)}, u32[]{:S(2)}, u32[]{:S(2)}) collective-permute-start(bf16[2,136,128]{2,1,0:T(8,128)(2,1)S(1)} %get-tuple-element.16), channel_id=1, source_target_pairs={{32,0},{64,32},{96,64},{33,1},{65,33},{97,65},{34,2},{66,34},{98,6... | collective-permute-start | bytes 208904 | tf_op jit(solution)/shard_map/ppermute | solution.py:316
  110.0 5.5 %collective-permute-start.4 = (bf16[2,136,128]{2,1,0:T(8,128)(2,1)S(1)}, bf16[2,136,128]{2,1,0:T(8,128)(2,1)S(1)}, u32[]{:S(2)}, u32[]{:S(2)}) collective-permute-start(bf16[2,136,128]{2,1,0:T(8,128)(2,1)S(1)} %get-tuple-element.15), channel_id=1, source_target_pairs={{0,16},{1,17},{2,18},{3,19},{4,20},{5,21},{6,22},{7,23},{8,24},{9,... | collective-permute-start | bytes 208904 | tf_op jit(solution)/shard_map/ppermute | solution.py:317
  115.4 4.1 %copy-start.3 = (f32[20976,128]{1,0:T(8,128)S(1)}, f32[20976,128]{1,0:T(8,128)}, u32[]{:S(2)}) copy-start(f32[20976,128]{1,0:T(8,128)} %copy-done.2) | copy-start | bytes 32219140
  119.5 1.0 copy-start.6
  120.4 1.0 copy-start.7

commit v2 on v1

v2 whole, which is shorter than its diff:
```python
import functools

import jax
import jax.numpy as jnp
from jax import lax
from jax.experimental import pallas as pl
from jax.experimental.pallas import tpu as pltpu
from jax.sharding import PartitionSpec as P

PITCH, ODD, EVEN = 152, 8, 80
SLABS = 131
NACC = 4
META = 8
GELU_A, GELU_B = 0.7978845608028654, 0.044715
VMEM = pl.BlockSpec(memory_space=pltpu.VMEM)
SMEM = pl.BlockSpec(memory_space=pltpu.SMEM)
ANY = pl.BlockSpec(memory_space=pl.ANY)


def on_chip(x):
    return pltpu.with_memory_space_constraint(x, pltpu.VMEM)


def gelu(x):
    return 0.5 * x * (1.0 + jnp.tanh(GELU_A * (x + GELU_B * (x * x * x))))


def pack_kernel(values_ref, cells_ref, counts_ref, out_ref, meta_ref, sem):
    slots = values_ref.shape[1]
    body = pltpu.make_async_copy(values_ref, out_ref.at[:, pl.ds(0, slots), :], sem.at[0])
    body.start()
    cells = cells_ref[...]
    live = lax.broadcasted_iota(jnp.int32, cells.shape, 1) < counts_ref[...]
    row = cells >> 7
    col = cells & 127
    high = jnp.where(live, row + 2, 0).astype(jnp.float32)
    low = jnp.where(live, (col >> 1) + jnp.where((col & 1) == 1, ODD, EVEN), 0).astype(jnp.float32)
    both = jnp.concatenate(
        [high[:, None, :], low[:, None, :], jnp.zeros((cells.shape[0], META - 2, 128), jnp.float32)], axis=1
    )
    meta_ref[...] = both.astype(jnp.bfloat16)
    tail = pltpu.make_async_copy(meta_ref, out_ref.at[:, pl.ds(slots, META), :], sem.at[1])
    tail.start()
    body.wait()
    tail.wait()


def pack(values, cells, counts):
    owners, slots, chans = values.shape
    return pl.pallas_call(
        pack_kernel,
        out_shape=jax.ShapeDtypeStruct((owners, slots + META, chans), jnp.bfloat16),
        in_specs=[ANY, VMEM, VMEM],
        out_specs=ANY,
        scratch_shapes=[
            pltpu.VMEM((owners, META, chans), jnp.bfloat16),
            pltpu.SemaphoreType.DMA((2,)),
        ],
        compiler_params=pltpu.CompilerParams(vmem_limit_bytes=8 << 20),
        name="pack",
    )(values, jnp.pad(cells, ((0, 0), (0, 128 - slots))), counts)


def spread_kernel(field_ref, acc_ref, wide_ref):
    def step(r, carry):
        wide_ref[...] = field_ref[r].astype(jnp.float32)
        base = pl.multiple_of((r + 2) * PITCH, 8)
        acc_ref[pl.ds(base + ODD, 64), :] = wide_ref[pl.ds(1, 64, stride=2), :]
        acc_ref[pl.ds(base + EVEN, 64), :] = wide_ref[pl.ds(0, 64, stride=2), :]
        for at in (0, EVEN - 8, EVEN + 64):
            acc_ref[pl.ds(base + at, 8), :] = jnp.zeros((8, 128), jnp.float32)
        return carry

    lax.fori_loop(0, field_ref.shape[0], step, 0)


def spread(field):
    return pl.pallas_call(
        spread_kernel,
        out_shape=jax.ShapeDtypeStruct((SLABS * PITCH, 128), jnp.float32),
        in_specs=[VMEM],
        out_specs=VMEM,
        scratch_shapes=[pltpu.VMEM((128, 128), jnp.float32)],
        compiler_params=pltpu.CompilerParams(vmem_limit_bytes=12 << 20),
        name="spread",
    )(field)


def scatter_kernel(band_ref, got_ref, start_ref, acc_ref, right_ref, left_ref, near_ref, rows_ref, *rest):
    more = rest[: NACC - 1]
    wide_ref, meta_ref, index_ref, place_ref, sem = rest[NACC - 1 :]
    del band_ref
    sources, slots = got_ref.shape[0], got_ref.shape[1] - META
    first = pltpu.make_async_copy(start_ref, acc_ref, sem.at[1])
    first.start()

    def unpack(s, carry):
        meta_ref[pl.ds(pl.multiple_of(s * META, META), META), :] = got_ref[s, pl.ds(slots, META), :].astype(jnp.float32)
        return carry

    lax.fori_loop(0, sources, unpack, 0, unroll=8)
    high = meta_ref[pl.ds(0, sources, stride=META), :]
    low = meta_ref[pl.ds(1, sources, stride=META), :]
    index_ref[...] = (high * PITCH + low).astype(jnp.int32)
    copy = pltpu.make_async_copy(index_ref, place_ref, sem.at[0])
    copy.start()

    def clear(r, carry):
        base = pl.multiple_of((r + 2) * PITCH, 8)
        for acc in more:
            acc[pl.ds(base, PITCH), :] = jnp.zeros((PITCH, 128), jnp.float32)
        return carry

    lax.fori_loop(0, 128, clear, 0)
    copy.wait()
    first.wait()
    accs = (acc_ref, *more)

    def add(s, carry):
        wide_ref[...] = got_ref[s, pl.ds(0, slots), :].astype(jnp.float32)
        for k in range(slots):
            acc = accs[k % NACC]
            i = place_ref[s, k]
            acc[pl.ds(i, 1), :] = acc[pl.ds(i, 1), :] + wide_ref[pl.ds(k, 1), :]
        return carry

    lax.fori_loop(0, sources, add, 0)

    def merge(r, carry):
        here = pl.ds(pl.multiple_of((r + 2) * PITCH, 8), PITCH)
        total = acc_ref[here, :]
        for acc in more:
            total = total + acc[here, :]
        acc_ref[here, :] = total
        return carry

    lax.fori_loop(0, 128, merge, 0)
    bf16 = jnp.bfloat16
    ends = (0, 1, 126, 127)
    for n, at in enumerate((EVEN + 63, ODD + 63)):
        right_ref[pl.ds(n * 128, 128), :] = acc_ref[pl.ds(2 * PITCH + at, 128, stride=PITCH), :].astype(bf16)
    left_ref[pl.ds(0, 128), :] = acc_ref[pl.ds(2 * PITCH + EVEN, 128, stride=PITCH), :].astype(bf16)
    near_ref[...] = acc_ref[pl.ds(2 * PITCH + ODD, 128, stride=PITCH), :].astype(bf16)
    east = [acc_ref[pl.ds((r + 2) * PITCH + at, 1), :] for r in ends for at in (EVEN + 63, ODD + 63)]
    west = [acc_ref[pl.ds((r + 2) * PITCH + EVEN, 1), :] for r in ends]
    right_ref[pl.ds(256, 8), :] = jnp.concatenate(east, axis=0).astype(bf16)
    left_ref[pl.ds(128, 8), :] = jnp.concatenate(west + west, axis=0).astype(bf16)
    for n, r in enumerate(ends):
        base = (r + 2) * PITCH
        rows_ref[n, pl.ds(0, 64), :] = acc_ref[pl.ds(base + ODD, 64), :].astype(bf16)
        rows_ref[n, pl.ds(64, 64), :] = acc_ref[pl.ds(base + EVEN, 64), :].astype(bf16)


def scatter(band, got, start):
    return pl.pallas_call(
        scatter_kernel,
        out_shape=[
            pltpu.VMEM(start.shape, jnp.float32),
            jax.ShapeDtypeStruct((264, 128), jnp.bfloat16),
            jax.ShapeDtypeStruct((136, 128), jnp.bfloat16),
            jax.ShapeDtypeStruct((128, 128), jnp.bfloat16),
            jax.ShapeDtypeStruct((4, 128, 128), jnp.bfloat16),
        ],
        in_specs=[SMEM, VMEM, ANY],
        out_specs=[VMEM] * 5,
        scratch_shapes=[pltpu.VMEM((130 * PITCH, 128), jnp.float32)] * (NACC - 1)
        + [
            pltpu.VMEM((96, 128), jnp.float32),
            pltpu.VMEM((128 * META, 128), jnp.float32),
            pltpu.VMEM((128, 128), jnp.int32),
            pltpu.SMEM((128, 128), jnp.int32),
            pltpu.SemaphoreType.DMA((2,)),
        ],
        compiler_params=pltpu.CompilerParams(vmem_limit_bytes=40 << 20),
        name="scatter",
    )(band, on_chip(got), start)


def frame_kernel(after_ref, rows_ref, west_ref, east_ref, down_ref, up_ref, all_ref):
    del after_ref
    f32, bf16 = jnp.float32, jnp.bfloat16
    west = west_ref[pl.ds(256, 8), :].astype(f32)
    east = east_ref[pl.ds(128, 8), :].astype(f32)
    for n in range(4):
        tail = jnp.concatenate([west[2 * n : 2 * n + 2], east[n : n + 1], jnp.zeros((5, 128), f32)], axis=0)
        for ref, at in ((all_ref, n), (up_ref, n) if n < 2 else (down_ref, n - 2)):
            ref[at, pl.ds(0, 128), :] = rows_ref[n]
            ref[at, pl.ds(128, 8), :] = tail.astype(bf16)


def frame(after, rows, west, east):
    return pl.pallas_call(
        frame_kernel,
        out_shape=[
            jax.ShapeDtypeStruct((2, 136, 128), jnp.bfloat16),
            jax.ShapeDtypeStruct((2, 136, 128), jnp.bfloat16),
            jax.ShapeDtypeStruct((4, 136, 128), jnp.bfloat16),
        ],
        in_specs=[ANY] + [VMEM] * 3,
        out_specs=[VMEM] * 3,
        compiler_params=pltpu.CompilerParams(vmem_limit_bytes=4 << 20),
        name="frame",
    )(after, rows, west, east)


def inner_kernel(low, field_ref, w1_ref, b1_ref, even_ref, odd_ref, mark_ref, lhs_ref, shift_ref):
    f32, bf16 = jnp.float32, jnp.bfloat16

    def fill(t, carry):
        base = pl.multiple_of((low + 1 + t) * PITCH, 8)
        parts = [field_ref[pl.ds(base + at, 64), :].astype(bf16) for at in (ODD - 1, EVEN, ODD, EVEN + 1)]
        lhs_ref[t] = jnp.concatenate(parts, axis=-1)
        return carry

    lax.fori_loop(0, 66, fill, 0)
    bias = jnp.concatenate([b1_ref[...], b1_ref[...]], axis=-1)

    def step(b, carry):
        pre = jnp.broadcast_to(bias, (512, 256))
        for di in range(3):
            window = lhs_ref[pl.ds(b * 8 + di, 8)].reshape(512, 512)
            pre = pre + jnp.dot(window, w1_ref[di], preferred_element_type=f32)
        hid = gelu(pre).reshape(8, 64, 256)
        shift_ref[:, pl.ds(8, 64), :] = hid[:, :, 128:]
        wide = jnp.concatenate([shift_ref[:, pl.ds(7, 64), :], hid[:, :, :128], hid[:, :, 128:]], axis=-1)
        wide = wide.astype(bf16).reshape(4, 2, 64, 384)
        even_ref[pl.ds(b * 4, 4)] = wide[:, 0]
        odd_ref[pl.ds(b * 4 + 1, 4)] = wide[:, 1]
        return carry

    lax.fori_loop(0, 8, step, 0)
    mark_ref[...] = jnp.zeros(mark_ref.shape, mark_ref.dtype)


def inner(low, field, w1, b1):
    return pl.pallas_call(
        functools.partial(inner_kernel, low),
        out_shape=[
            pltpu.VMEM((32, 64, 384), jnp.bfloat16),
            pltpu.VMEM((33, 64, 384), jnp.bfloat16),
            jax.ShapeDtypeStruct((8, 128), jnp.float32),
        ],
        in_specs=[VMEM] * 3,
        out_specs=[VMEM] * 3,
        scratch_shapes=[pltpu.VMEM((66, 64, 512), jnp.bfloat16), pltpu.VMEM((8, 72, 128), jnp.float32)],
        compiler_params=pltpu.CompilerParams(vmem_limit_bytes=24 << 20),
        name="inner",
    )(on_chip(field), w1, b1)


def rim_kernel(
    band_ref,
    even0_in,
    odd0_in,
    even1_in,
    odd1_in,
    right_ref,
    left_ref,
    near_ref,
    west_ref,
    east_ref,
    own_ref,
    down_ref,
    up_ref,
    across_ref,
    w1_ref,
    w1s_ref,
    b1_ref,
    w2_ref,
    b2_ref,
    even0_ref,
    odd0_ref,
    even1_ref,
    odd1_ref,
    out_ref,
    cols_ref,
    strip_ref,
    shift_ref,
    side_ref,
):
    del even0_in, odd0_in, even1_in, odd1_in
    f32, bf16 = jnp.float32, jnp.bfloat16
    band = band_ref[0]
    north, south = band == 0, band == 3
    first = jnp.where(north, 2, 0)
    flipped = (first, 1, 2 - first)
    dot = functools.partial(jnp.dot, preferred_element_type=f32)
    bias = b1_ref[...]
    bias2 = jnp.concatenate([bias, bias], axis=-1)

    body = (
        west_ref[pl.ds(0, 128), :],
        west_ref[pl.ds(128, 128), :],
        left_ref[pl.ds(0, 128), :],
        near_ref[...],
        right_ref[pl.ds(0, 128), :],
        right_ref[pl.ds(128, 128), :],
        east_ref[pl.ds(0, 128), :],
    )
    for n, col in enumerate(body):
        cols_ref[n, pl.ds(2, 128), :] = col.astype(f32)

    def wide(ref, n):
        return ref[n].astype(f32)

    rows = (
        jnp.where(north, wide(across_ref, 1), wide(down_ref, 0)),
        jnp.where(north, wide(across_ref, 0), wide(down_ref, 1)),
        wide(own_ref, 0),
        wide(own_ref, 1),
        wide(own_ref, 2),
        wide(own_ref, 3),
        jnp.where(south, wide(across_ref, 3), wide(up_ref, 0)),
    )
    where = (128, 129, 64, 0, 127, 63, 130)
    lhs = []
    for n, row in enumerate(rows):
        strip_ref[n, pl.ds(ODD, 64), :] = row[0:64]
        strip_ref[n, pl.ds(EVEN, 64), :] = row[64:128]
        strip_ref[n, pl.ds(ODD - 1, 1), :] = row[129:130]
        strip_ref[n, pl.ds(EVEN + 64, 1), :] = row[130:131]
        if n in (0, 1, 6):
            slab = 130 if n == 6 else n
            for m, at in enumerate(where):
                cols_ref[m, pl.ds(slab, 1), :] = row[at : at + 1]
        parts = [strip_ref[n, pl.ds(at, 64), :].astype(bf16) for at in (ODD - 1, EVEN, ODD, EVEN + 1)]
        lhs.append(jnp.concatenate(parts, axis=-1))

    for n, at in enumerate((0, 1, 4)):
        total = jnp.zeros((136, 128), f32) + bias
        top = jnp.zeros((8, 128), f32) + bias
        for di in range(3):
            window = jnp.concatenate(
                [cols_ref[at + m, pl.ds(di, 136), :].astype(bf16) for m in range(3)], axis=-1
            )
            total = total + dot(window, w1s_ref[di])
            if n == 0:
                top = top + dot(window[0:8], w1s_ref[flipped[di]])
        side_ref[n, pl.ds(0, 136), :] = gelu(total)
        if n == 0:
            side_ref[n, pl.ds(0, 1), :] = gelu(top)[0:1]

    odd1_ref[0] = odd0_ref[32]
    for r, at, taps in ((-1, 0, flipped), (0, 1, (0, 1, 2)), (127, 4, (0, 1, 2))):
        pre = bias2
        for di in range(3):
            pre = pre + dot(lhs[at + di], w1_ref[taps[di]])
        hid = gelu(pre)
        shift_ref[pl.ds(8, 64), :] = hid[:, 128:]
        shift_ref[pl.ds(7, 1), :] = side_ref[0, pl.ds(r + 1, 1), :]
        line = jnp.concatenate([shift_ref[pl.ds(7, 64), :], hid[:, :128], hid[:, 128:]], axis=-1).astype(bf16)
        if r == -1:
            odd0_ref[0] = line
        elif r == 0:
            even0_ref[0] = line
        else:
            odd1_ref[32] = line

    head = lax.broadcasted_iota(jnp.int32, (16, 256), 0) == 0
    foot = lax.broadcasted_iota(jnp.int32, (16, 128), 0) == 15

    def mend(ref, p, r):
        here = pl.ds(r + 1, 1)
        new = jnp.concatenate([side_ref[0, here, :], side_ref[1, here, :]], axis=-1)
        old = ref[p, pl.ds(0, 16), pl.ds(0, 256)].astype(f32)
        ref[p, pl.ds(0, 16), pl.ds(0, 256)] = jnp.where(head, new, old).astype(bf16)
        old = ref[p, pl.ds(48, 16), pl.ds(256, 128)].astype(f32)
        ref[p, pl.ds(48, 16), pl.ds(256, 128)] = jnp.where(foot, side_ref[2, here, :], old).astype(bf16)

    def mend_step(p, carry):
        mend(even0_ref, p, 2 * p)
        mend(odd0_ref, p + 1, 2 * p + 1)
        mend(even1_ref, p, 2 * p + 64)
        mend(odd1_ref, p + 1, 2 * p + 65)
        return carry

    lax.fori_loop(0, 32, mend_step, 0, unroll=2)
    odd1_ref[0] = odd0_ref[32]

    for half, (even_ref, odd_ref) in enumerate(((even0_ref, odd0_ref), (even1_ref, odd1_ref))):

        def finish(b, carry):
            total = jnp.broadcast_to(b2_ref[...], (256, 128))
            total = total + dot(odd_ref[pl.ds(b * 4, 4)].reshape(256, 384), w2_ref[0])
            total = total + dot(even_ref[pl.ds(b * 4, 4)].reshape(256, 384), w2_ref[1])
            total = total + dot(odd_ref[pl.ds(b * 4 + 1, 4)].reshape(256, 384), w2_ref[2])
            out_ref[pl.ds(half * 32 + b * 4, 4)] = total.reshape(4, 64, 128).astype(bf16)
            return carry

        lax.fori_loop(0, 8, finish, 0)


def rim(band, blocks, *rest):
    return pl.pallas_call(
        rim_kernel,
        out_shape=[pltpu.VMEM(b.shape, b.dtype) for b in blocks] + [jax.ShapeDtypeStruct((64, 64, 128), jnp.bfloat16)],
        in_specs=[SMEM] + [VMEM] * 18,
        out_specs=[VMEM] * 5,
        scratch_shapes=[
            pltpu.VMEM((7, 144, 128), jnp.float32),
            pltpu.VMEM((7, PITCH, 128), jnp.float32),
            pltpu.VMEM((72, 128), jnp.float32),
            pltpu.VMEM((3, 136, 128), jnp.float32),
        ],
        input_output_aliases={1: 0, 2: 1, 3: 2, 4: 3},
        compiler_params=pltpu.CompilerParams(vmem_limit_bytes=16 << 20),
        name="rim",
    )(band, *map(on_chip, blocks), *rest)[4]


def shards(background, values, cells, counts, w1, b1, w2, b2):
    lat, lon = lax.axis_size("lat"), lax.axis_size("lon")
    band = lax.axis_index("lat")[None]
    east_pairs = [(i, (i + 1) % lon) for i in range(lon)]
    west_pairs = [(j, i) for i, j in east_pairs]
    down_pairs = [(i, i + 1) for i in range(lat - 1)]
    up_pairs = [(j, i) for i, j in down_pairs]
    pole_pairs = [(b * lon + i, b * lon + (i + lon // 2) % lon) for b in (0, lat - 1) for i in range(lon)]

    sent = pack(values[0], cells[0], counts[0][:, None])
    got = lax.all_to_all(sent, ("lat", "lon"), split_axis=0, concat_axis=0, tiled=True)
    field, right, left, near, rows = scatter(band, got, spread(background))

    flat = w1.reshape(3, 384, 128)
    blank = jnp.zeros((3, 128, 128), jnp.bfloat16)
    paired = jnp.concatenate(
        [jnp.concatenate([flat, blank], axis=1), jnp.concatenate([blank, flat], axis=1)], axis=2
    )
    west = lax.ppermute(right, "lon", east_pairs)
    east = lax.ppermute(left, "lon", west_pairs)
    *upper, mark = inner(0, field, paired, b1[None])
    lower_rows, upper_rows, own = frame(mark, rows, west, east)
    down = lax.ppermute(lower_rows, "lat", down_pairs)
    up = lax.ppermute(upper_rows, "lat", up_pairs)
    across = lax.ppermute(own, ("lat", "lon"), pole_pairs)
    *lower, _ = inner(64, field, paired, b1[None])
    return rim(
        band,
        (*upper, *lower),
        right,
        left,
        near,
        west,
        east,
        own,
        down,
        up,
        across,
        paired,
        flat,
        b1[None],
        w2.reshape(3, 384, 128),
        b2[None],
    )


def solution(mesh):
    placed = (
        P("lat", "lon", None),
        P(("lat", "lon"), None, None, None),
        P(("lat", "lon"), None, None),
        P(("lat", "lon"), None),
        P(),
        P(),
        P(),
        P(),
    )
    return jax.shard_map(
        shards, mesh=mesh, in_specs=placed, out_specs=P("lat", "lon", None), check_vma=False
    )
```

time: 142 us -> 123 us (0.87)
  local copies, waits for them, and re-layouts: 24.1 us -> 9.63 us
  waiting for transfers between devices: 42.1 us -> 36.8 us
  starting transfers between devices: 23.6 us -> 25.9 us
    unnamed x21 -> x15, local copies, waits for them, and re-layouts: 23.1 us -> 8.86 us
    ppermute x3, waiting for transfers between devices: 3.58 us -> 0.01 us  [the longest x1 0.01 us: shards(): down = lax.ppermute(lower_rows, 'lat', down_pairs)]
    ppermute x3, starting transfers between devices: 6.4 us -> 8.62 us  [the longest x1 5.9 us: shards(): down = lax.ppermute(lower_rows, 'lat', down_pairs)]
    pallas_call x2 -> x5, Pallas kernels: 21.4 us -> 22.5 us  [the longest x2 13.4 us: inner(): pl.pallas_call(functools.partial(inner_kernel, low), out_shape=[pltpu.VME...]
  transfers between devices with their start and end apart: 6 -> 6, of which waited for: 4 -> 1; matrix products, arithmetic and copies ran while one was open for 1% -> 0% of each run, Pallas kernels for 1% -> 12%
where the time goes in v2:
time: 123 us
  Pallas kernels  50.5 us (41%)
  waiting for transfers between devices  36.8 us (30%)
  starting transfers between devices  25.9 us (21%)
  local copies, waits for them, and re-layouts  9.63 us (8%)
    all_to_all x1, waiting for transfers between devices, shards(): lax.all_to_all(sent, ('lat', 'lon'), split_axis=0, concat_axis=0, tiled=T...  36.7 us
    pallas_call x1, Pallas kernels, scatter(): pl.pallas_call(scatter_kernel, out_shape=[pltpu.VMEM(start.shape, jnp.flo...  26.1 us
    pallas_call x2, Pallas kernels, inner(): pl.pallas_call(functools.partial(inner_kernel, low), out_shape=[pltpu.VME...  13.4 us
    all_to_all x1, starting transfers between devices, shards(): lax.all_to_all(sent, ('lat', 'lon'), split_axis=0, concat_axis=0, tiled=T...  11.5 us
    unnamed x15, local copies, waits for them, and re-layouts  8.86 us
    pallas_call x1, Pallas kernels, rim(): pl.pallas_call(rim_kernel, out_shape=[pltpu.VMEM(b.shape, b.dtype) for b...  7.19 us
    ppermute x1, starting transfers between devices, shards(): down = lax.ppermute(lower_rows, 'lat', down_pairs)  5.9 us
    ppermute x1, starting transfers between devices, shards(): east = lax.ppermute(left, 'lon', west_pairs)  5.52 us
  transfers between devices with their start and end apart: 6, of which 1 were waited for; matrix products, arithmetic and copies ran while one was open for 0% of the time, Pallas kernels for 12%

profile of v2, /device:TPU:1, one launch (start us, length us, event | category | flops | bytes accessed | tf_op | source)
XLA Modules:
  0.0 123.0 jit_solution(11528893093174739237)
XLA Ops:
  0.0 0.9 copy.13
  0.9 0.8 copy.14.counts_ref
  1.7 0.0 copy-start.2
  1.7 1.9 %copy-done.2 = bf16[1,128,96,128]{3,2,1,0:T(8,128)(2,1)S(1)} copy-done((bf16[1,128,96,128]{3,2,1,0:T(8,128)(2,1)S(1)}, bf16[1,128,96,128]{3,2,1,0:T(8,128)(2,1)}, u32[]{:S(2)}) %copy-start.2) | copy-done | bytes 3145752
  3.6 1.9 %pack.1 = bf16[128,104,128]{2,1,0:T(8,128)(2,1)} custom-call(bf16[128,96,128]{2,1,0:T(8,128)(2,1)S(1)} %bitcast.8, s32[128,128]{1,0:T(8,128)S(1)} %pad.6.cells_ref, s32[128,1]{1,0:T(8,128)S(1)} %copy.14.counts_ref), custom_call_target="tpu_custom_call" | custom-call | tf_op jit(solution)/shard_map/pack/pallas_call | solution.py:50
  5.4 11.5 %all-to-all-start = ((bf16[128,104,128]{2,1,0:T(8,128)(2,1)}), bf16[128,104,128]{2,1,0:T(8,128)(2,1)S(1)}, u32[]{:S(2)}, u32[]{:S(2)}) async-start(bf16[128,104,128]{2,1,0:T(8,128)(2,1)} %pack.1), calls=%async_computation | async-start | bytes 6815744 | tf_op jit(solution)/shard_map/all_to_all | solution.py:421
  16.9 0.0 copy-start.1
  17.0 2.2 %copy-done.1 = bf16[128,128,128]{2,1,0:T(8,128)(2,1)S(1)} copy-done((bf16[128,128,128]{2,1,0:T(8,128)(2,1)S(1)}, bf16[128,128,128]{2,1,0:T(8,128)(2,1)}, u32[]{:S(2)}) %copy-start.1) | copy-done | bytes 4194328
  19.1 1.8 %spread.1.start_ref = f32[19912,128]{1,0:T(8,128)S(1)} custom-call(bf16[128,128,128]{2,1,0:T(8,128)(2,1)S(1)} %copy-done.1), custom_call_target="tpu_custom_call" | custom-call | tf_op jit(solution)/shard_map/spread/pallas_call | solution.py:78
  21.0 3.9 %copy-done = f32[19912,128]{1,0:T(8,128)} copy-done((f32[19912,128]{1,0:T(8,128)}, f32[19912,128]{1,0:T(8,128)S(1)}, u32[]{:S(2)}) %copy-start) | copy-done | bytes 10194968
  24.8 36.7 %all-to-all-done.got_ref = bf16[128,104,128]{2,1,0:T(8,128)(2,1)S(1)} async-done(((bf16[128,104,128]{2,1,0:T(8,128)(2,1)}), bf16[128,104,128]{2,1,0:T(8,128)(2,1)S(1)}, u32[]{:S(2)}, u32[]{:S(2)}) %all-to-all-start) | async-done | bytes 3407904 | tf_op jit(solution)/shard_map/all_to_all | solution.py:421
  61.6 26.1 %scatter.1 = (f32[19912,128]{1,0:T(8,128)S(1)}, bf16[264,128]{1,0:T(8,128)(2,1)S(1)}, bf16[136,128]{1,0:T(8,128)(2,1)S(1)}, bf16[128,128]{1,0:T(8,128)(2,1)S(1)}, bf16[4,128,128]{2,1,0:T(8,128)(2,1)S(1)}) custom-call(s32[1]{0:T(128)} %bitcast.band_ref, bf16[128,104,128]{2,1,0:T(8,128)(2,1)S(1)} %all-to-all-done.got_ref, f32[19912,128]{1,0:T(8,128)} %copy-done), custom_call_target="tpu_custom_call" | custom-call | tf_op jit(solution)/shard_map/scatter/pallas_call | solution.py:155
  87.7 0.2 collective-permute-start
  88.0 5.5 %collective-permute-start.1 = (bf16[136,128]{1,0:T(8,128)(2,1)S(1)}, bf16[136,128]{1,0:T(8,128)(2,1)S(1)}, u32[]{:S(2)}, u32[]{:S(2)}) collective-permute-start(bf16[136,128]{1,0:T(8,128)(2,1)S(1)} %get-tuple-element.25.left_ref), channel_id=1, source_target_pairs={{1,0},{2,1},{3,2},{4,3},{5,4},{6,5},{7,6},{8,7},{9,8},{10,9},{11,1... | collective-permute-start | bytes 104456 | tf_op jit(solution)/shard_map/ppermute | solution.py:430
  93.5 0.1 fusion.2.w1_ref
  93.6 6.4 %inner.2 = (bf16[32,64,384]{2,1,0:T(8,128)(2,1)S(1)}, bf16[33,64,384]{2,1,0:T(8,128)(2,1)S(1)}, f32[8,128]{1,0:T(8,128)S(1)}) custom-call(f32[19912,128]{1,0:T(8,128)S(1)} %get-tuple-element.19.field_ref, bf16[3,512,256]{2,1,0:T(8,128)(2,1)S(1)} %fusion.2.w1_ref, f32[1,128]{1,0:T(1,128)S(1)} %bitcast.12), custom_call_target="tpu_custom_call" | custom-call | tf_op jit(solution)/shard_map/inner/pallas_call | solution.py:236
  100.0 0.0 collective-permute-done.1.east_ref
  100.1 0.7 collective-permute-start.4
  100.8 5.9 %collective-permute-start.2 = (bf16[2,136,128]{2,1,0:T(8,128)(2,1)S(1)}, bf16[2,136,128]{2,1,0:T(8,128)(2,1)S(1)}, u32[]{:S(2)}, u32[]{:S(2)}) collective-permute-start(bf16[2,136,128]{2,1,0:T(8,128)(2,1)S(1)} %get-tuple-element.30), channel_id=1, source_target_pairs={{0,32},{32,64},{64,96},{1,33},{33,65},{65,97},{2,34},{34,66},{66,9... | collective-permute-start | bytes 208904 | tf_op jit(solution)/shard_map/ppermute | solution.py:433
  106.7 0.0 copy-start.4
  106.7 0.0 copy-start.6
  106.7 2.1 %collective-permute-start.3 = (bf16[2,136,128]{2,1,0:T(8,128)(2,1)S(1)}, bf16[2,136,128]{2,1,0:T(8,128)(2,1)S(1)}, u32[]{:S(2)}, u32[]{:S(2)}) collective-permute-start(bf16[2,136,128]{2,1,0:T(8,128)(2,1)S(1)} %get-tuple-element.31), channel_id=1, source_target_pairs={{32,0},{64,32},{96,64},{33,1},{65,33},{97,65},{34,2},{66,34},{98,6... | collective-permute-start | bytes 208904 | tf_op jit(solution)/shard_map/ppermute | solution.py:434
  108.8 7.0 %inner.3 = (bf16[32,64,384]{2,1,0:T(8,128)(2,1)S(1)}, bf16[33,64,384]{2,1,0:T(8,128)(2,1)S(1)}, f32[8,128]{1,0:T(8,128)}) custom-call(f32[19912,128]{1,0:T(8,128)S(1)} %get-tuple-element.19.field_ref, bf16[3,512,256]{2,1,0:T(8,128)(2,1)S(1)} %fusion.2.w1_ref, f32[1,128]{1,0:T(1,128)S(1)} %bitcast.13), custom_call_target="tpu_custom_call" | custom-call | tf_op jit(solution)/shard_map/inner/pallas_call | solution.py:236
  115.8 7.2 %rim.1 = (bf16[32,64,384]{2,1,0:T(8,128)(2,1)S(1)}, bf16[33,64,384]{2,1,0:T(8,128)(2,1)S(1)}, bf16[32,64,384]{2,1,0:T(8,128)(2,1)S(1)}, bf16[33,64,384]{2,1,0:T(8,128)(2,1)S(1)}, bf16[64,64,128]{2,1,0:T(8,128)(2,1)}) custom-call(s32[1]{0:T(128)} %bitcast.band_ref, ...), custom_call_target="tpu_custom_call", output_to_operand_aliasing={{0}: (1, {}), {1}: (2, {}), {2}: (3, {}), {3}: (4, {})} | custom-call | tf_op jit(solution)/shard_map/rim/pallas_call | solution.py:394
  (13 shorter events, 0.1 us)
Async XLA Ops:
  1.7 1.9 %copy-start.2 = (bf16[1,128,96,128]{3,2,1,0:T(8,128)(2,1)S(1)}, bf16[1,128,96,128]{3,2,1,0:T(8,128)(2,1)}, u32[]{:S(2)}) copy-start(bf16[1,128,96,128]{3,2,1,0:T(8,128)(2,1)} %param.9) | copy-start | bytes 9437188
  5.4 56.2 %all-to-all-start = ((bf16[128,104,128]{2,1,0:T(8,128)(2,1)}), bf16[128,104,128]{2,1,0:T(8,128)(2,1)S(1)}, u32[]{:S(2)}, u32[]{:S(2)}) async-start(bf16[128,104,128]{2,1,0:T(8,128)(2,1)} %pack.1), calls=%async_computation | async-start | bytes 6815744 | tf_op jit(solution)/shard_map/all_to_all | solution.py:421
  16.9 2.2 %copy-start.1 = (bf16[128,128,128]{2,1,0:T(8,128)(2,1)S(1)}, bf16[128,128,128]{2,1,0:T(8,128)(2,1)}, u32[]{:S(2)}) copy-start(bf16[128,128,128]{2,1,0:T(8,128)(2,1)} %field_ref.1) | copy-start | bytes 12582916
  21.0 3.9 %copy-start = (f32[19912,128]{1,0:T(8,128)}, f32[19912,128]{1,0:T(8,128)S(1)}, u32[]{:S(2)}) copy-start(f32[19912,128]{1,0:T(8,128)S(1)} %spread.1.start_ref) | copy-start | bytes 30584836
  61.6 31.9 %copy-start.3 = (bf16[3,3,128,128]{3,2,1,0:T(8,128)(2,1)S(1)}, bf16[3,3,128,128]{3,2,1,0:T(8,128)(2,1)}, u32[]{:S(2)}) copy-start(bf16[3,3,128,128]{3,2,1,0:T(8,128)(2,1)} %param.12) | copy-start | bytes 884740
  61.6 32.0 %copy-start.5 = (f32[128]{0:T(128)S(1)}, f32[128]{0:T(128)}, u32[]{:S(2)}) copy-start(f32[128]{0:T(128)} %param.13) | copy-start | bytes 1540
  87.7 12.3 %collective-permute-start = (bf16[264,128]{1,0:T(8,128)(2,1)S(1)}, bf16[264,128]{1,0:T(8,128)(2,1)S(1)}, u32[]{:S(2)}, u32[]{:S(2)}) collective-permute-start(bf16[264,128]{1,0:T(8,128)(2,1)S(1)} %get-tuple-element.24.right_ref), channel_id=1, source_target_pairs={{0,1},{1,2},{2,3},{3,4},{4,5},{5,6},{6,7},{7,8},{8,9},{9,10},{10,1... | collective-permute-start | bytes 202760 | tf_op jit(solution)/shard_map/ppermute | solution.py:429
  88.0 12.1 %collective-permute-start.1 = (bf16[136,128]{1,0:T(8,128)(2,1)S(1)}, bf16[136,128]{1,0:T(8,128)(2,1)S(1)}, u32[]{:S(2)}, u32[]{:S(2)}) collective-permute-start(bf16[136,128]{1,0:T(8,128)(2,1)S(1)} %get-tuple-element.25.left_ref), channel_id=1, source_target_pairs={{1,0},{2,1},{3,2},{4,3},{5,4},{6,5},{7,6},{8,7},{9,8},{10,9},{11,1... | collective-permute-start | bytes 104456 | tf_op jit(solution)/shard_map/ppermute | solution.py:430
  100.1 15.7 %collective-permute-start.4 = (bf16[4,136,128]{2,1,0:T(8,128)(2,1)S(1)}, bf16[4,136,128]{2,1,0:T(8,128)(2,1)S(1)}, u32[]{:S(2)}, u32[]{:S(2)}) collective-permute-start(bf16[4,136,128]{2,1,0:T(8,128)(2,1)S(1)} %get-tuple-element.29.own_ref), channel_id=1, source_target_pairs={{0,16},{1,17},{2,18},{3,19},{4,20},{5,21},{6,22},{7,23},{8,24},{9,... | collective-permute-start | bytes 417800 | tf_op jit(solution)/shard_map/ppermute | solution.py:435
  100.8 15.0 %collective-permute-start.2 = (bf16[2,136,128]{2,1,0:T(8,128)(2,1)S(1)}, bf16[2,136,128]{2,1,0:T(8,128)(2,1)S(1)}, u32[]{:S(2)}, u32[]{:S(2)}) collective-permute-start(bf16[2,136,128]{2,1,0:T(8,128)(2,1)S(1)} %get-tuple-element.30), channel_id=1, source_target_pairs={{0,32},{32,64},{64,96},{1,33},{33,65},{65,97},{2,34},{34,66},{66,9... | collective-permute-start | bytes 208904 | tf_op jit(solution)/shard_map/ppermute | solution.py:433
  106.7 9.1 %copy-start.4 = (bf16[3,3,128,128]{3,2,1,0:T(8,128)(2,1)S(1)}, bf16[3,3,128,128]{3,2,1,0:T(8,128)(2,1)}, u32[]{:S(2)}) copy-start(bf16[3,3,128,128]{3,2,1,0:T(8,128)(2,1)} %param.14) | copy-start | bytes 884740
  106.7 9.1 %copy-start.6 = (f32[128]{0:T(128)S(1)}, f32[128]{0:T(128)}, u32[]{:S(2)}) copy-start(f32[128]{0:T(128)} %param.15) | copy-start | bytes 1540
  106.7 9.1 %collective-permute-start.3 = (bf16[2,136,128]{2,1,0:T(8,128)(2,1)S(1)}, bf16[2,136,128]{2,1,0:T(8,128)(2,1)S(1)}, u32[]{:S(2)}, u32[]{:S(2)}) collective-permute-start(bf16[2,136,128]{2,1,0:T(8,128)(2,1)S(1)} %get-tuple-element.31), channel_id=1, source_target_pairs={{32,0},{64,32},{96,64},{33,1},{65,33},{97,65},{34,2},{66,34},{98,6... | collective-permute-start | bytes 208904 | tf_op jit(solution)/shard_map/ppermute | solution.py:434

commit v3 on v2

--- a/solution.py
+++ b/solution.py
@@ -9,7 +9,8 @@
 
 PITCH, ODD, EVEN = 152, 8, 80
 SLABS = 131
-NACC = 4
+BATCH = 8
+GROUP = 8
 META = 8
 GELU_A, GELU_B = 0.7978845608028654, 0.044715
 VMEM = pl.BlockSpec(memory_space=pltpu.VMEM)
@@ -35,8 +36,20 @@
     col = cells & 127
     high = jnp.where(live, row + 2, 0).astype(jnp.float32)
     low = jnp.where(live, (col >> 1) + jnp.where((col & 1) == 1, ODD, EVEN), 0).astype(jnp.float32)
+    again = jnp.zeros(cells.shape, jnp.float32)
+    place = lax.broadcasted_iota(jnp.int32, cells.shape, 1) % BATCH
+    marked = jnp.where(live, cells, -1)
+    for back in range(1, BATCH):
+        same = (pltpu.roll(marked, back, 1) == marked) & live & (place >= back)
+        again = jnp.where(same, 1.0, again)
     both = jnp.concatenate(
-        [high[:, None, :], low[:, None, :], jnp.zeros((cells.shape[0], META - 2, 128), jnp.float32)], axis=1
+        [
+            high[:, None, :],
+            low[:, None, :],
+            again[:, None, :],
+            jnp.zeros((cells.shape[0], META - 3, 128), jnp.float32),
+        ],
+        axis=1,
     )
     meta_ref[...] = both.astype(jnp.bfloat16)
     tail = pltpu.make_async_copy(meta_ref, out_ref.at[:, pl.ds(slots, META), :], sem.at[1])
@@ -87,11 +100,10 @@
 
 
 def scatter_kernel(band_ref, got_ref, start_ref, acc_ref, right_ref, left_ref, near_ref, rows_ref, *rest):
-    more = rest[: NACC - 1]
-    wide_ref, meta_ref, index_ref, place_ref, sem = rest[NACC - 1 :]
+    other_ref, wide_ref, meta_ref, index_ref, late_ref, cells0_ref, cells1_ref, list_ref, sem = rest
     del band_ref
     sources, slots = got_ref.shape[0], got_ref.shape[1] - META
-    first = pltpu.make_async_copy(start_ref, acc_ref, sem.at[1])
+    first = pltpu.make_async_copy(start_ref, acc_ref, sem.at[0])
     first.start()
 
     def unpack(s, carry):
@@ -101,37 +113,79 @@
     lax.fori_loop(0, sources, unpack, 0, unroll=8)
     high = meta_ref[pl.ds(0, sources, stride=META), :]
     low = meta_ref[pl.ds(1, sources, stride=META), :]
-    index_ref[...] = (high * PITCH + low).astype(jnp.int32)
-    copy = pltpu.make_async_copy(index_ref, place_ref, sem.at[0])
-    copy.start()
+    again = meta_ref[pl.ds(2, sources, stride=META), :]
+    spot = high * PITCH + low
+    index_ref[...] = jnp.where(again > 0, 0.0, spot).astype(jnp.int32)
+    lane = lax.broadcasted_iota(jnp.int32, again.shape, 1)
+    inside = lane < slots
+    count = jnp.sum(jnp.where(inside, again, 0.0), axis=1, keepdims=True)
+    late = jnp.where(inside, again * spot, jnp.broadcast_to(count, again.shape))
+    late_ref[...] = late.astype(jnp.int32)
+
+    cells = (cells0_ref, cells1_ref)
+
+    def fetch(group, half):
+        return pltpu.make_async_copy(index_ref.at[pl.ds(group * GROUP, GROUP), :], cells[half], sem.at[1 + half])
+
+    fetch(0, 0).start()
+    fetch(1, 1).start()
+    listed = pltpu.make_async_copy(late_ref, list_ref, sem.at[3])
+    listed.start()
 
     def clear(r, carry):
-        base = pl.multiple_of((r + 2) * PITCH, 8)
-        for acc in more:
-            acc[pl.ds(base, PITCH), :] = jnp.zeros((PITCH, 128), jnp.float32)
+        other_ref[pl.ds(pl.multiple_of((r + 2) * PITCH, 8), PITCH), :] = jnp.zeros((PITCH, 128), jnp.float32)
         return carry
 
     lax.fori_loop(0, 128, clear, 0)
-    copy.wait()
     first.wait()
-    accs = (acc_ref, *more)
-
-    def add(s, carry):
-        wide_ref[...] = got_ref[s, pl.ds(0, slots), :].astype(jnp.float32)
-        for k in range(slots):
-            acc = accs[k % NACC]
-            i = place_ref[s, k]
-            acc[pl.ds(i, 1), :] = acc[pl.ds(i, 1), :] + wide_ref[pl.ds(k, 1), :]
-        return carry
-
-    lax.fori_loop(0, sources, add, 0)
+    accs = (acc_ref, other_ref)
+
+    def add(step, carry):
+        for half in range(2):
+            group = step * 2 + half
+            fetch(group, half).wait()
+            for t in range(GROUP):
+                wide = wide_ref.at[t % 2]
+                wide[...] = got_ref[group * GROUP + t, pl.ds(0, slots), :].astype(jnp.float32)
+                for n, k in enumerate(range(0, slots, BATCH)):
+                    acc = accs[n % 2]
+                    where = [cells[half][t, k + m] for m in range(BATCH)]
+                    sums = [acc[pl.ds(i, 1), :] + wide[pl.ds(k + m, 1), :] for m, i in enumerate(where)]
+                    for i, total in zip(where, sums):
+                        acc[pl.ds(i, 1), :] = total
+
+            @pl.when(group + 2 < sources // GROUP)
+            def _():
+                fetch(group + 2, half).start()
+
+        return carry
+
+    lax.fori_loop(0, sources // (2 * GROUP), add, 0)
+    listed.wait()
+
+    def rest_of(s, carry):
+        @pl.when(list_ref[s, slots] > 0)
+        def _():
+            wide_ref[0] = got_ref[s, pl.ds(0, slots), :].astype(jnp.float32)
+
+            def one(k, carry):
+                i = list_ref[s, k]
+
+                @pl.when(i > 0)
+                def _():
+                    acc_ref[pl.ds(i, 1), :] = acc_ref[pl.ds(i, 1), :] + wide_ref[0, pl.ds(k, 1), :]
+
+                return carry
+
+            lax.fori_loop(0, slots, one, 0)
+
+        return carry
+
+    lax.fori_loop(0, sources, rest_of, 0)
 
     def merge(r, carry):
         here = pl.ds(pl.multiple_of((r + 2) * PITCH, 8), PITCH)
-        total = acc_ref[here, :]
-        for acc in more:
-            total = total + acc[here, :]
-        acc_ref[here, :] = total
+        acc_ref[here, :] = acc_ref[here, :] + other_ref[here, :]
         return carry
 
     lax.fori_loop(0, 128, merge, 0)
@@ -163,15 +217,18 @@
         ],
         in_specs=[SMEM, VMEM, ANY],
         out_specs=[VMEM] * 5,
-        scratch_shapes=[pltpu.VMEM((130 * PITCH, 128), jnp.float32)] * (NACC - 1)
-        + [
-            pltpu.VMEM((96, 128), jnp.float32),
+        scratch_shapes=[
+            pltpu.VMEM((130 * PITCH, 128), jnp.float32),
+            pltpu.VMEM((2, 96, 128), jnp.float32),
             pltpu.VMEM((128 * META, 128), jnp.float32),
             pltpu.VMEM((128, 128), jnp.int32),
+            pltpu.VMEM((128, 128), jnp.int32),
+            pltpu.SMEM((GROUP, 128), jnp.int32),
+            pltpu.SMEM((GROUP, 128), jnp.int32),
             pltpu.SMEM((128, 128), jnp.int32),
-            pltpu.SemaphoreType.DMA((2,)),
-        ],
-        compiler_params=pltpu.CompilerParams(vmem_limit_bytes=40 << 20),
+            pltpu.SemaphoreType.DMA((4,)),
+        ],
+        compiler_params=pltpu.CompilerParams(vmem_limit_bytes=24 << 20),
         name="scatter",
     )(band, on_chip(got), start)
 

time: 123 us -> 118 us (0.959)
  Pallas kernels: 50.5 us -> 41.7 us
  local copies, waits for them, and re-layouts: 9.63 us -> 13.5 us
    pallas_call x1, Pallas kernels: 26.1 us -> 17.3 us  [scatter(): pl.pallas_call(scatter_kernel, out_shape=[pltpu.VMEM(start.shape, jnp.flo...]
    unnamed x15 -> x17, local copies, waits for them, and re-layouts: 8.86 us -> 12.8 us
    ppermute x1, starting transfers between devices: 5.9 us -> 3.95 us  [shards(): down = lax.ppermute(lower_rows, 'lat', down_pairs)]
    ppermute x1, starting transfers between devices: 2.05 us -> 3.32 us  [shards(): up = lax.ppermute(upper_rows, 'lat', up_pairs)]
  transfers between devices with their start and end apart: 6 -> 6, of which waited for: 1 -> 1; matrix products, arithmetic and copies ran while one was open for 0% -> 0% of each run, Pallas kernels for 12% -> 13%
where the time goes in v3:
time: 118 us; the launch traced here: 117 us
  Pallas kernels  41.7 us (35%)
  waiting for transfers between devices  36.8 us (31%)
  starting transfers between devices  25.2 us (21%)
  local copies, waits for them, and re-layouts  13.5 us (11%)
    all_to_all x1, waiting for transfers between devices, shards(): lax.all_to_all(sent, ('lat', 'lon'), split_axis=0, concat_axis=0, tiled=T...  36.8 us
    pallas_call x1, Pallas kernels, scatter(): pl.pallas_call(scatter_kernel, out_shape=[pltpu.VMEM(start.shape, jnp.flo...  17.3 us
    pallas_call x2, Pallas kernels, inner(): pl.pallas_call(functools.partial(inner_kernel, low), out_shape=[pltpu.VME...  13.4 us
    unnamed x17, local copies, waits for them, and re-layouts  12.8 us
    all_to_all x1, starting transfers between devices, shards(): lax.all_to_all(sent, ('lat', 'lon'), split_axis=0, concat_axis=0, tiled=T...  11.5 us
    pallas_call x1, Pallas kernels, rim(): pl.pallas_call(rim_kernel, out_shape=[pltpu.VMEM(b.shape, b.dtype) for b...  7.19 us
    ppermute x1, starting transfers between devices, shards(): east = lax.ppermute(left, 'lon', west_pairs)  5.67 us
    ppermute x1, starting transfers between devices, shards(): down = lax.ppermute(lower_rows, 'lat', down_pairs)  3.95 us
  transfers between devices with their start and end apart: 6, of which 1 were waited for; matrix products, arithmetic and copies ran while one was open for 0% of the time, Pallas kernels for 13%

profile of v3, /device:TPU:1, one launch (start us, length us, event | category | flops | bytes accessed | tf_op | source)
XLA Modules:
  0.0 117.4 jit_solution(7881069137434852054)
XLA Ops:
  0.0 0.9 copy.13
  0.9 0.8 copy.14.counts_ref
  1.7 0.0 copy-start.3
  1.7 1.9 %copy-done.3 = bf16[1,128,96,128]{3,2,1,0:T(8,128)(2,1)S(1)} copy-done((bf16[1,128,96,128]{3,2,1,0:T(8,128)(2,1)S(1)}, bf16[1,128,96,128]{3,2,1,0:T(8,128)(2,1)}, u32[]{:S(2)}) %copy-start.3) | copy-done | bytes 3145752
  3.6 1.9 %pack.1 = bf16[128,104,128]{2,1,0:T(8,128)(2,1)} custom-call(bf16[128,96,128]{2,1,0:T(8,128)(2,1)S(1)} %bitcast.8, s32[128,128]{1,0:T(8,128)S(1)} %pad.6.cells_ref, s32[128,1]{1,0:T(8,128)S(1)} %copy.14.counts_ref), custom_call_target="tpu_custom_call" | custom-call | tf_op jit(solution)/shard_map/pack/pallas_call | solution.py:63
  5.5 11.5 %all-to-all-start = ((bf16[128,104,128]{2,1,0:T(8,128)(2,1)}), bf16[128,104,128]{2,1,0:T(8,128)(2,1)S(1)}, u32[]{:S(2)}, u32[]{:S(2)}) async-start(bf16[128,104,128]{2,1,0:T(8,128)(2,1)} %pack.1), calls=%async_computation | async-start | bytes 6815744 | tf_op jit(solution)/shard_map/all_to_all | solution.py:478
  17.0 0.0 copy-start.2
  17.0 2.2 %copy-done.2 = bf16[128,128,128]{2,1,0:T(8,128)(2,1)S(1)} copy-done((bf16[128,128,128]{2,1,0:T(8,128)(2,1)S(1)}, bf16[128,128,128]{2,1,0:T(8,128)(2,1)}, u32[]{:S(2)}) %copy-start.2) | copy-done | bytes 4194328
  19.2 1.8 %spread.1.start_ref = f32[19912,128]{1,0:T(8,128)S(1)} custom-call(bf16[128,128,128]{2,1,0:T(8,128)(2,1)S(1)} %copy-done.2), custom_call_target="tpu_custom_call" | custom-call | tf_op jit(solution)/shard_map/spread/pallas_call | solution.py:91
  21.0 3.9 %copy-done = f32[19912,128]{1,0:T(8,128)} copy-done((f32[19912,128]{1,0:T(8,128)}, f32[19912,128]{1,0:T(8,128)S(1)}, u32[]{:S(2)}) %copy-start) | copy-done | bytes 10194968
  24.9 36.8 %all-to-all-done.got_ref = bf16[128,104,128]{2,1,0:T(8,128)(2,1)S(1)} async-done(((bf16[128,104,128]{2,1,0:T(8,128)(2,1)}), bf16[128,104,128]{2,1,0:T(8,128)(2,1)S(1)}, u32[]{:S(2)}, u32[]{:S(2)}) %all-to-all-start) | async-done | bytes 3407904 | tf_op jit(solution)/shard_map/all_to_all | solution.py:478
  61.6 3.9 %copy-done.1 = f32[19912,128]{1,0:T(8,128)S(1)} copy-done((f32[19912,128]{1,0:T(8,128)S(1)}, f32[19912,128]{1,0:T(8,128)}, u32[]{:S(2)}) %copy-start.1) | copy-done | bytes 10194968
  65.5 17.3 %scatter.1 = (f32[19912,128]{1,0:T(8,128)S(1)}, bf16[264,128]{1,0:T(8,128)(2,1)S(1)}, bf16[136,128]{1,0:T(8,128)(2,1)S(1)}, bf16[128,128]{1,0:T(8,128)(2,1)S(1)}, bf16[4,128,128]{2,1,0:T(8,128)(2,1)S(1)}) custom-call(s32[1]{0:T(128)} %bitcast.band_ref, bf16[128,104,128]{2,1,0:T(8,128)(2,1)S(1)} %all-to-all-done.got_ref, f32[19912,128]{1,0:T(8,128)S(1)} %copy-done.1), custom_call_target="tpu_custom_call" | custom-call | tf_op jit(solution)/shard_map/scatter/pallas_call | solution.py:209
  82.9 0.1 collective-permute-start
  83.0 5.7 %collective-permute-start.1 = (bf16[136,128]{1,0:T(8,128)(2,1)S(1)}, bf16[136,128]{1,0:T(8,128)(2,1)S(1)}, u32[]{:S(2)}, u32[]{:S(2)}) collective-permute-start(bf16[136,128]{1,0:T(8,128)(2,1)S(1)} %get-tuple-element.25.left_ref), channel_id=1, source_target_pairs={{1,0},{2,1},{3,2},{4,3},{5,4},{6,5},{7,6},{8,7},{9,8},{10,9},{11,1... | collective-permute-start | bytes 104456 | tf_op jit(solution)/shard_map/ppermute | solution.py:487
  88.6 0.1 fusion.2.w1_ref
  88.7 6.4 %inner.2 = (bf16[32,64,384]{2,1,0:T(8,128)(2,1)S(1)}, bf16[33,64,384]{2,1,0:T(8,128)(2,1)S(1)}, f32[8,128]{1,0:T(8,128)S(1)}) custom-call(f32[19912,128]{1,0:T(8,128)S(1)} %get-tuple-element.19.field_ref, bf16[3,512,256]{2,1,0:T(8,128)(2,1)S(1)} %fusion.2.w1_ref, f32[1,128]{1,0:T(1,128)S(1)} %bitcast.12), custom_call_target="tpu_custom_call" | custom-call | tf_op jit(solution)/shard_map/inner/pallas_call | solution.py:293
  95.2 0.7 collective-permute-start.4
  95.9 4.0 %collective-permute-start.2 = (bf16[2,136,128]{2,1,0:T(8,128)(2,1)S(1)}, bf16[2,136,128]{2,1,0:T(8,128)(2,1)S(1)}, u32[]{:S(2)}, u32[]{:S(2)}) collective-permute-start(bf16[2,136,128]{2,1,0:T(8,128)(2,1)S(1)} %get-tuple-element.30), channel_id=1, source_target_pairs={{0,32},{32,64},{64,96},{1,33},{33,65},{65,97},{2,34},{34,66},{66,9... | collective-permute-start | bytes 208904 | tf_op jit(solution)/shard_map/ppermute | solution.py:490
  99.9 0.0 copy-start.5
  99.9 0.0 copy-start.7
  99.9 3.3 %collective-permute-start.3 = (bf16[2,136,128]{2,1,0:T(8,128)(2,1)S(1)}, bf16[2,136,128]{2,1,0:T(8,128)(2,1)S(1)}, u32[]{:S(2)}, u32[]{:S(2)}) collective-permute-start(bf16[2,136,128]{2,1,0:T(8,128)(2,1)S(1)} %get-tuple-element.31), channel_id=1, source_target_pairs={{32,0},{64,32},{96,64},{33,1},{65,33},{97,65},{34,2},{66,34},{98,6... | collective-permute-start | bytes 208904 | tf_op jit(solution)/shard_map/ppermute | solution.py:491
  103.2 7.0 %inner.3 = (bf16[32,64,384]{2,1,0:T(8,128)(2,1)S(1)}, bf16[33,64,384]{2,1,0:T(8,128)(2,1)S(1)}, f32[8,128]{1,0:T(8,128)}) custom-call(f32[19912,128]{1,0:T(8,128)S(1)} %get-tuple-element.19.field_ref, bf16[3,512,256]{2,1,0:T(8,128)(2,1)S(1)} %fusion.2.w1_ref, f32[1,128]{1,0:T(1,128)S(1)} %bitcast.13), custom_call_target="tpu_custom_call" | custom-call | tf_op jit(solution)/shard_map/inner/pallas_call | solution.py:293
  110.3 7.2 %rim.1 = (bf16[32,64,384]{2,1,0:T(8,128)(2,1)S(1)}, bf16[33,64,384]{2,1,0:T(8,128)(2,1)S(1)}, bf16[32,64,384]{2,1,0:T(8,128)(2,1)S(1)}, bf16[33,64,384]{2,1,0:T(8,128)(2,1)S(1)}, bf16[64,64,128]{2,1,0:T(8,128)(2,1)}) custom-call(s32[1]{0:T(128)} %bitcast.band_ref, ...), custom_call_target="tpu_custom_call", output_to_operand_aliasing={{0}: (1, {}), {1}: (2, {}), {2}: (3, {}), {3}: (4, {})} | custom-call | tf_op jit(solution)/shard_map/rim/pallas_call | solution.py:451
  (15 shorter events, 0.1 us)
Async XLA Ops:
  1.7 1.9 %copy-start.3 = (bf16[1,128,96,128]{3,2,1,0:T(8,128)(2,1)S(1)}, bf16[1,128,96,128]{3,2,1,0:T(8,128)(2,1)}, u32[]{:S(2)}) copy-start(bf16[1,128,96,128]{3,2,1,0:T(8,128)(2,1)} %param.9) | copy-start | bytes 9437188
  5.5 56.2 %all-to-all-start = ((bf16[128,104,128]{2,1,0:T(8,128)(2,1)}), bf16[128,104,128]{2,1,0:T(8,128)(2,1)S(1)}, u32[]{:S(2)}, u32[]{:S(2)}) async-start(bf16[128,104,128]{2,1,0:T(8,128)(2,1)} %pack.1), calls=%async_computation | async-start | bytes 6815744 | tf_op jit(solution)/shard_map/all_to_all | solution.py:478
  17.0 2.2 %copy-start.2 = (bf16[128,128,128]{2,1,0:T(8,128)(2,1)S(1)}, bf16[128,128,128]{2,1,0:T(8,128)(2,1)}, u32[]{:S(2)}) copy-start(bf16[128,128,128]{2,1,0:T(8,128)(2,1)} %field_ref.1) | copy-start | bytes 12582916
  21.0 3.9 %copy-start = (f32[19912,128]{1,0:T(8,128)}, f32[19912,128]{1,0:T(8,128)S(1)}, u32[]{:S(2)}) copy-start(f32[19912,128]{1,0:T(8,128)S(1)} %spread.1.start_ref) | copy-start | bytes 30584836
  61.6 3.9 %copy-start.1 = (f32[19912,128]{1,0:T(8,128)S(1)}, f32[19912,128]{1,0:T(8,128)}, u32[]{:S(2)}) copy-start(f32[19912,128]{1,0:T(8,128)} %copy-done) | copy-start | bytes 30584836
  65.5 23.1 %copy-start.4 = (bf16[3,3,128,128]{3,2,1,0:T(8,128)(2,1)S(1)}, bf16[3,3,128,128]{3,2,1,0:T(8,128)(2,1)}, u32[]{:S(2)}) copy-start(bf16[3,3,128,128]{3,2,1,0:T(8,128)(2,1)} %param.12) | copy-start | bytes 884740
  65.5 23.2 %copy-start.6 = (f32[128]{0:T(128)S(1)}, f32[128]{0:T(128)}, u32[]{:S(2)}) copy-start(f32[128]{0:T(128)} %param.13) | copy-start | bytes 1540
  82.9 12.3 %collective-permute-start = (bf16[264,128]{1,0:T(8,128)(2,1)S(1)}, bf16[264,128]{1,0:T(8,128)(2,1)S(1)}, u32[]{:S(2)}, u32[]{:S(2)}) collective-permute-start(bf16[264,128]{1,0:T(8,128)(2,1)S(1)} %get-tuple-element.24.right_ref), channel_id=1, source_target_pairs={{0,1},{1,2},{2,3},{3,4},{4,5},{5,6},{6,7},{7,8},{8,9},{9,10},{10,1... | collective-permute-start | bytes 202760 | tf_op jit(solution)/shard_map/ppermute | solution.py:486
  83.0 12.2 %collective-permute-start.1 = (bf16[136,128]{1,0:T(8,128)(2,1)S(1)}, bf16[136,128]{1,0:T(8,128)(2,1)S(1)}, u32[]{:S(2)}, u32[]{:S(2)}) collective-permute-start(bf16[136,128]{1,0:T(8,128)(2,1)S(1)} %get-tuple-element.25.left_ref), channel_id=1, source_target_pairs={{1,0},{2,1},{3,2},{4,3},{5,4},{6,5},{7,6},{8,7},{9,8},{10,9},{11,1... | collective-permute-start | bytes 104456 | tf_op jit(solution)/shard_map/ppermute | solution.py:487
  95.2 15.0 %collective-permute-start.4 = (bf16[4,136,128]{2,1,0:T(8,128)(2,1)S(1)}, bf16[4,136,128]{2,1,0:T(8,128)(2,1)S(1)}, u32[]{:S(2)}, u32[]{:S(2)}) collective-permute-start(bf16[4,136,128]{2,1,0:T(8,128)(2,1)S(1)} %get-tuple-element.29.own_ref), channel_id=1, source_target_pairs={{0,16},{1,17},{2,18},{3,19},{4,20},{5,21},{6,22},{7,23},{8,24},{9,... | collective-permute-start | bytes 417800 | tf_op jit(solution)/shard_map/ppermute | solution.py:492
  95.9 14.3 %collective-permute-start.2 = (bf16[2,136,128]{2,1,0:T(8,128)(2,1)S(1)}, bf16[2,136,128]{2,1,0:T(8,128)(2,1)S(1)}, u32[]{:S(2)}, u32[]{:S(2)}) collective-permute-start(bf16[2,136,128]{2,1,0:T(8,128)(2,1)S(1)} %get-tuple-element.30), channel_id=1, source_target_pairs={{0,32},{32,64},{64,96},{1,33},{33,65},{65,97},{2,34},{34,66},{66,9... | collective-permute-start | bytes 208904 | tf_op jit(solution)/shard_map/ppermute | solution.py:490
  99.9 10.4 %copy-start.5 = (bf16[3,3,128,128]{3,2,1,0:T(8,128)(2,1)S(1)}, bf16[3,3,128,128]{3,2,1,0:T(8,128)(2,1)}, u32[]{:S(2)}) copy-start(bf16[3,3,128,128]{3,2,1,0:T(8,128)(2,1)} %param.14) | copy-start | bytes 884740
  99.9 10.4 %copy-start.7 = (f32[128]{0:T(128)S(1)}, f32[128]{0:T(128)}, u32[]{:S(2)}) copy-start(f32[128]{0:T(128)} %param.15) | copy-start | bytes 1540
  99.9 10.3 %collective-permute-start.3 = (bf16[2,136,128]{2,1,0:T(8,128)(2,1)S(1)}, bf16[2,136,128]{2,1,0:T(8,128)(2,1)S(1)}, u32[]{:S(2)}, u32[]{:S(2)}) collective-permute-start(bf16[2,136,128]{2,1,0:T(8,128)(2,1)S(1)} %get-tuple-element.31), channel_id=1, source_target_pairs={{32,0},{64,32},{96,64},{33,1},{65,33},{97,65},{34,2},{66,34},{98,6... | collective-permute-start | bytes 208904 | tf_op jit(solution)/shard_map/ppermute | solution.py:491

commit v4 on v3

--- a/solution.py
+++ b/solution.py
@@ -10,8 +10,10 @@
 PITCH, ODD, EVEN = 152, 8, 80
 SLABS = 131
 BATCH = 8
+CHUNKS = 4
 GROUP = 8
 META = 8
+ROWS = 16
 GELU_A, GELU_B = 0.7978845608028654, 0.044715
 VMEM = pl.BlockSpec(memory_space=pltpu.VMEM)
 SMEM = pl.BlockSpec(memory_space=pltpu.SMEM)
@@ -22,56 +24,79 @@
     return pltpu.with_memory_space_constraint(x, pltpu.VMEM)
 
 
+def off_chip(x):
+    return pltpu.with_memory_space_constraint(x, pltpu.HBM)
+
+
 def gelu(x):
     return 0.5 * x * (1.0 + jnp.tanh(GELU_A * (x + GELU_B * (x * x * x))))
 
 
-def pack_kernel(values_ref, cells_ref, counts_ref, out_ref, meta_ref, sem):
-    slots = values_ref.shape[1]
-    body = pltpu.make_async_copy(values_ref, out_ref.at[:, pl.ds(0, slots), :], sem.at[0])
-    body.start()
-    cells = cells_ref[...]
-    live = lax.broadcasted_iota(jnp.int32, cells.shape, 1) < counts_ref[...]
+def pack_kernel(values_ref, cells_ref, counts_ref, out_ref, held_ref, where_ref, live_ref, meta_ref, sem):
+    owners, slots = values_ref.shape[0], values_ref.shape[1]
+    part = owners // CHUNKS
+    numbers = pltpu.make_async_copy(cells_ref, where_ref, sem.at[2 * CHUNKS])
+    numbers.start()
+    totals = pltpu.make_async_copy(counts_ref, live_ref, sem.at[2 * CHUNKS + 1])
+    totals.start()
+    arrive, leave = [], []
+    for n in range(CHUNKS):
+        here = pl.ds(n * part, part)
+        arrive.append(
+            pltpu.make_async_copy(values_ref.at[here], held_ref.at[here, pl.ds(0, slots), :], sem.at[n])
+        )
+        leave.append(pltpu.make_async_copy(held_ref.at[here], out_ref.at[here], sem.at[CHUNKS + n]))
+        arrive[-1].start()
+    numbers.wait()
+    totals.wait()
+    cells = where_ref[...]
+    across = jnp.broadcast_to(live_ref[...], (owners, owners))
+    down = lax.broadcasted_iota(jnp.int32, (owners, owners), 0)
+    lane = lax.broadcasted_iota(jnp.int32, (owners, owners), 1)
+    counts = jnp.sum(jnp.where(down == lane, across, 0).astype(jnp.float32), axis=1, keepdims=True)
+    place = lax.broadcasted_iota(jnp.int32, cells.shape, 1)
+    live = place.astype(jnp.float32) < counts
     row = cells >> 7
     col = cells & 127
     high = jnp.where(live, row + 2, 0).astype(jnp.float32)
     low = jnp.where(live, (col >> 1) + jnp.where((col & 1) == 1, ODD, EVEN), 0).astype(jnp.float32)
-    again = jnp.zeros(cells.shape, jnp.float32)
-    place = lax.broadcasted_iota(jnp.int32, cells.shape, 1) % BATCH
-    marked = jnp.where(live, cells, -1)
+    blank = jnp.zeros((owners, 128 - slots), jnp.int32)
+    marked = jnp.concatenate([jnp.where(live, cells, -1), blank - 1], axis=1)
+    again = jnp.zeros(marked.shape, jnp.float32)
     for back in range(1, BATCH):
-        same = (pltpu.roll(marked, back, 1) == marked) & live & (place >= back)
+        same = (pltpu.roll(marked, back, 1) == marked) & (marked >= 0) & (lane % BATCH >= back)
         again = jnp.where(same, 1.0, again)
-    both = jnp.concatenate(
-        [
-            high[:, None, :],
-            low[:, None, :],
-            again[:, None, :],
-            jnp.zeros((cells.shape[0], META - 3, 128), jnp.float32),
-        ],
-        axis=1,
-    )
-    meta_ref[...] = both.astype(jnp.bfloat16)
-    tail = pltpu.make_async_copy(meta_ref, out_ref.at[:, pl.ds(slots, META), :], sem.at[1])
-    tail.start()
-    body.wait()
-    tail.wait()
+    blank = blank.astype(jnp.float32)
+    meta_ref[pl.ds(0, owners, stride=META), :] = jnp.concatenate([high, blank], axis=1)
+    meta_ref[pl.ds(1, owners, stride=META), :] = jnp.concatenate([low, blank], axis=1)
+    meta_ref[pl.ds(2, owners, stride=META), :] = again
+    for m in range(3, META):
+        meta_ref[pl.ds(m, owners, stride=META), :] = jnp.zeros((owners, 128), jnp.float32)
+    held_ref[:, pl.ds(slots, META), :] = meta_ref[...].reshape(owners, META, 128).astype(jnp.bfloat16)
+    for came, goes in zip(arrive, leave):
+        came.wait()
+        goes.start()
+    for goes in leave:
+        goes.wait()
 
 
 def pack(values, cells, counts):
     owners, slots, chans = values.shape
     return pl.pallas_call(
         pack_kernel,
-        out_shape=jax.ShapeDtypeStruct((owners, slots + META, chans), jnp.bfloat16),
-        in_specs=[ANY, VMEM, VMEM],
+        out_shape=pltpu.HBM((owners, slots + META, chans), jnp.bfloat16),
+        in_specs=[ANY] * 3,
         out_specs=ANY,
         scratch_shapes=[
-            pltpu.VMEM((owners, META, chans), jnp.bfloat16),
-            pltpu.SemaphoreType.DMA((2,)),
+            pltpu.VMEM((owners, slots + META, chans), jnp.bfloat16),
+            pltpu.VMEM((owners, slots), jnp.int32),
+            pltpu.VMEM((1, owners), jnp.int32),
+            pltpu.VMEM((owners * META, chans), jnp.float32),
+            pltpu.SemaphoreType.DMA((2 * CHUNKS + 2,)),
         ],
-        compiler_params=pltpu.CompilerParams(vmem_limit_bytes=8 << 20),
+        compiler_params=pltpu.CompilerParams(vmem_limit_bytes=12 << 20),
         name="pack",
-    )(values, jnp.pad(cells, ((0, 0), (0, 128 - slots))), counts)
+    )(off_chip(values), off_chip(cells), off_chip(counts))
 
 
 def spread_kernel(field_ref, acc_ref, wide_ref):
@@ -90,7 +115,7 @@
 def spread(field):
     return pl.pallas_call(
         spread_kernel,
-        out_shape=jax.ShapeDtypeStruct((SLABS * PITCH, 128), jnp.float32),
+        out_shape=pltpu.HBM((SLABS * PITCH, 128), jnp.float32),
         in_specs=[VMEM],
         out_specs=VMEM,
         scratch_shapes=[pltpu.VMEM((128, 128), jnp.float32)],
@@ -119,7 +144,9 @@
     lane = lax.broadcasted_iota(jnp.int32, again.shape, 1)
     inside = lane < slots
     count = jnp.sum(jnp.where(inside, again, 0.0), axis=1, keepdims=True)
-    late = jnp.where(inside, again * spot, jnp.broadcast_to(count, again.shape))
+    furthest = jnp.max(jnp.where(inside & (again > 0), lane, 0).astype(jnp.float32), axis=1, keepdims=True)
+    notes = jnp.where(lane == slots, count, furthest)
+    late = jnp.where(inside, again * spot, notes)
     late_ref[...] = late.astype(jnp.int32)
 
     cells = (cells0_ref, cells1_ref)
@@ -164,7 +191,10 @@
     listed.wait()
 
     def rest_of(s, carry):
-        @pl.when(list_ref[s, slots] > 0)
+        repeats = list_ref[s, slots]
+        furthest = list_ref[s, slots + 1]
+
+        @pl.when(repeats > 0)
         def _():
             wide_ref[0] = got_ref[s, pl.ds(0, slots), :].astype(jnp.float32)
 
@@ -177,7 +207,7 @@
 
                 return carry
 
-            lax.fori_loop(0, slots, one, 0)
+            lax.fori_loop(jnp.where(repeats > 1, 0, furthest), furthest + 1, one, 0)
 
         return carry
 
@@ -230,7 +260,7 @@
         ],
         compiler_params=pltpu.CompilerParams(vmem_limit_bytes=24 << 20),
         name="scatter",
-    )(band, on_chip(got), start)
+    )(band, on_chip(got), off_chip(start))
 
 
 def frame_kernel(after_ref, rows_ref, west_ref, east_ref, down_ref, up_ref, all_ref):
@@ -262,30 +292,24 @@
 
 def inner_kernel(low, field_ref, w1_ref, b1_ref, even_ref, odd_ref, mark_ref, lhs_ref, shift_ref):
     f32, bf16 = jnp.float32, jnp.bfloat16
-
-    def fill(t, carry):
-        base = pl.multiple_of((low + 1 + t) * PITCH, 8)
-        parts = [field_ref[pl.ds(base + at, 64), :].astype(bf16) for at in (ODD - 1, EVEN, ODD, EVEN + 1)]
-        lhs_ref[t] = jnp.concatenate(parts, axis=-1)
-        return carry
-
-    lax.fori_loop(0, 66, fill, 0)
     bias = jnp.concatenate([b1_ref[...], b1_ref[...]], axis=-1)
+    weight = w1_ref[...].reshape(1536, 256)
 
     def step(b, carry):
-        pre = jnp.broadcast_to(bias, (512, 256))
-        for di in range(3):
-            window = lhs_ref[pl.ds(b * 8 + di, 8)].reshape(512, 512)
-            pre = pre + jnp.dot(window, w1_ref[di], preferred_element_type=f32)
-        hid = gelu(pre).reshape(8, 64, 256)
+        for n in range(ROWS + 2):
+            base = pl.multiple_of((low + 1 + b * ROWS + n) * PITCH, 8)
+            parts = [field_ref[pl.ds(base + at, 64), :].astype(bf16) for at in (ODD - 1, EVEN, ODD, EVEN + 1)]
+            lhs_ref[n] = jnp.concatenate(parts, axis=-1)
+        window = jnp.concatenate([lhs_ref[pl.ds(di, ROWS)].reshape(ROWS * 64, 512) for di in range(3)], axis=-1)
+        hid = gelu(jnp.dot(window, weight, preferred_element_type=f32) + bias).reshape(ROWS, 64, 256)
         shift_ref[:, pl.ds(8, 64), :] = hid[:, :, 128:]
         wide = jnp.concatenate([shift_ref[:, pl.ds(7, 64), :], hid[:, :, :128], hid[:, :, 128:]], axis=-1)
-        wide = wide.astype(bf16).reshape(4, 2, 64, 384)
-        even_ref[pl.ds(b * 4, 4)] = wide[:, 0]
-        odd_ref[pl.ds(b * 4 + 1, 4)] = wide[:, 1]
-        return carry
-
-    lax.fori_loop(0, 8, step, 0)
+        wide = wide.astype(bf16).reshape(ROWS // 2, 2, 64, 384)
+        even_ref[pl.ds(b * (ROWS // 2), ROWS // 2)] = wide[:, 0]
+        odd_ref[pl.ds(b * (ROWS // 2) + 1, ROWS // 2)] = wide[:, 1]
+        return carry
+
+    lax.fori_loop(0, 64 // ROWS, step, 0)
     mark_ref[...] = jnp.zeros(mark_ref.shape, mark_ref.dtype)
 
 
@@ -299,7 +323,7 @@
         ],
         in_specs=[VMEM] * 3,
         out_specs=[VMEM] * 3,
-        scratch_shapes=[pltpu.VMEM((66, 64, 512), jnp.bfloat16), pltpu.VMEM((8, 72, 128), jnp.float32)],
+        scratch_shapes=[pltpu.VMEM((ROWS + 2, 64, 512), jnp.bfloat16), pltpu.VMEM((ROWS, 72, 128), jnp.float32)],
         compiler_params=pltpu.CompilerParams(vmem_limit_bytes=24 << 20),
         name="inner",
     )(on_chip(field), w1, b1)
@@ -474,7 +498,7 @@
     up_pairs = [(j, i) for i, j in down_pairs]
     pole_pairs = [(b * lon + i, b * lon + (i + lon // 2) % lon) for b in (0, lat - 1) for i in range(lon)]
 
-    sent = pack(values[0], cells[0], counts[0][:, None])
+    sent = pack(values[0], cells[0], counts)
     got = lax.all_to_all(sent, ("lat", "lon"), split_axis=0, concat_axis=0, tiled=True)
     field, right, left, near, rows = scatter(band, got, spread(background))
 

time: 118 us -> 111 us (0.941)
  local copies, waits for them, and re-layouts: 13.5 us -> 3.73 us
  Pallas kernels: 41.7 us -> 45.1 us
    unnamed x17 -> x11, local copies, waits for them, and re-layouts: 12.8 us -> 3.73 us
    pallas_call x2, Pallas kernels: 3.72 us -> 8.93 us  [the longest x1 5.78 us: spread(): pl.pallas_call(spread_kernel, out_shape=pltpu.HBM((SLABS * PITCH, 128), j...]
    pallas_call x2, Pallas kernels: 13.4 us -> 10.8 us  [inner(): pl.pallas_call(functools.partial(inner_kernel, low), out_shape=[pltpu.VME...]
  transfers between devices with their start and end apart: 6 -> 6, of which waited for: 1 -> 1; matrix products, arithmetic and copies ran while one was open for 0% -> 0% of each run, Pallas kernels for 13% -> 15%
where the time goes in v4:
time: 111 us; the launch traced here: 110 us
  Pallas kernels  45.1 us (41%)
  waiting for transfers between devices  36.7 us (33%)
  starting transfers between devices  24.6 us (22%)
  local copies, waits for them, and re-layouts  3.73 us (3%)
    all_to_all x1, waiting for transfers between devices, shards(): lax.all_to_all(sent, ('lat', 'lon'), split_axis=0, concat_axis=0, tiled=T...  36.7 us
    pallas_call x1, Pallas kernels, scatter(): pl.pallas_call(scatter_kernel, out_shape=[pltpu.VMEM(start.shape, jnp.flo...  18.1 us
    all_to_all x1, starting transfers between devices, shards(): lax.all_to_all(sent, ('lat', 'lon'), split_axis=0, concat_axis=0, tiled=T...  11.5 us
    pallas_call x2, Pallas kernels, inner(): pl.pallas_call(functools.partial(inner_kernel, low), out_shape=[pltpu.VME...  10.8 us
    pallas_call x1, Pallas kernels, rim(): pl.pallas_call(rim_kernel, out_shape=[pltpu.VMEM(b.shape, b.dtype) for b...  7.21 us
    pallas_call x1, Pallas kernels, spread(): pl.pallas_call(spread_kernel, out_shape=pltpu.HBM((SLABS * PITCH, 128), j...  5.78 us
    ppermute x1, starting transfers between devices, shards(): east = lax.ppermute(left, 'lon', west_pairs)  5.12 us
    ppermute x1, starting transfers between devices, shards(): down = lax.ppermute(lower_rows, 'lat', down_pairs)  4.11 us
  transfers between devices with their start and end apart: 6, of which 1 were waited for; matrix products, arithmetic and copies ran while one was open for 0% of the time, Pallas kernels for 15%

profile of v4, /device:TPU:1, one launch (start us, length us, event | category | flops | bytes accessed | tf_op | source)
XLA Modules:
  0.0 110.4 jit_solution(7794575774562188405)
XLA Ops:
  0.0 1.5 %copy.13 = s32[1,128,96]{2,1,0:T(8,128)} copy(s32[1,128,96]{1,2,0:T(8,128)} %param.10) | data formatting | bytes 98304 | tf_op args[2]
  1.5 3.1 %pack.1 = bf16[128,104,128]{2,1,0:T(8,128)(2,1)} custom-call(bf16[128,96,128]{2,1,0:T(8,128)(2,1)} %bitcast.14, s32[128,96]{1,0:T(8,128)} %bitcast.15, s32[1,128]{1,0:T(1,128)} %counts_ref.1), custom_call_target="tpu_custom_call" | custom-call | tf_op jit(solution)/shard_map/pack/pallas_call | solution.py:85
  4.7 11.5 %all-to-all-start = ((bf16[128,104,128]{2,1,0:T(8,128)(2,1)}), bf16[128,104,128]{2,1,0:T(8,128)(2,1)S(1)}, u32[]{:S(2)}, u32[]{:S(2)}) async-start(bf16[128,104,128]{2,1,0:T(8,128)(2,1)} %pack.1), calls=%async_computation | async-start | bytes 6815744 | tf_op jit(solution)/shard_map/all_to_all | solution.py:502
  16.2 0.0 copy-start
  16.2 2.2 %copy-done = bf16[128,128,128]{2,1,0:T(8,128)(2,1)S(1)} copy-done((bf16[128,128,128]{2,1,0:T(8,128)(2,1)S(1)}, bf16[128,128,128]{2,1,0:T(8,128)(2,1)}, u32[]{:S(2)}) %copy-start) | copy-done | bytes 4194328
  18.4 5.8 %spread.1.start_ref = f32[19912,128]{1,0:T(8,128)} custom-call(bf16[128,128,128]{2,1,0:T(8,128)(2,1)S(1)} %copy-done), custom_call_target="tpu_custom_call" | custom-call | tf_op jit(solution)/shard_map/spread/pallas_call | solution.py:116
  24.2 36.7 %all-to-all-done.got_ref = bf16[128,104,128]{2,1,0:T(8,128)(2,1)S(1)} async-done(((bf16[128,104,128]{2,1,0:T(8,128)(2,1)}), bf16[128,104,128]{2,1,0:T(8,128)(2,1)S(1)}, u32[]{:S(2)}, u32[]{:S(2)}) %all-to-all-start) | async-done | bytes 3407904 | tf_op jit(solution)/shard_map/all_to_all | solution.py:502
  60.8 18.1 %scatter.1 = (f32[19912,128]{1,0:T(8,128)S(1)}, bf16[264,128]{1,0:T(8,128)(2,1)S(1)}, bf16[136,128]{1,0:T(8,128)(2,1)S(1)}, bf16[128,128]{1,0:T(8,128)(2,1)S(1)}, bf16[4,128,128]{2,1,0:T(8,128)(2,1)S(1)}) custom-call(s32[1]{0:T(128)} %bitcast.band_ref, bf16[128,104,128]{2,1,0:T(8,128)(2,1)S(1)} %all-to-all-done.got_ref, f32[19912,128]{1,0:T(8,128)} %spread.1.start_ref), custom_call_target="tpu_custom_call" | custom-call | tf_op jit(solution)/shard_map/scatter/pallas_call | solution.py:239
  79.0 0.6 collective-permute-start
  79.6 5.1 %collective-permute-start.1 = (bf16[136,128]{1,0:T(8,128)(2,1)S(1)}, bf16[136,128]{1,0:T(8,128)(2,1)S(1)}, u32[]{:S(2)}, u32[]{:S(2)}) collective-permute-start(bf16[136,128]{1,0:T(8,128)(2,1)S(1)} %get-tuple-element.25.left_ref), channel_id=1, source_target_pairs={{1,0},{2,1},{3,2},{4,3},{5,4},{6,5},{7,6},{8,7},{9,8},{10,9},{11,1... | collective-permute-start | bytes 104456 | tf_op jit(solution)/shard_map/ppermute | solution.py:511
  84.8 0.1 fusion.2.w1_ref
  84.8 5.1 %inner.2 = (bf16[32,64,384]{2,1,0:T(8,128)(2,1)S(1)}, bf16[33,64,384]{2,1,0:T(8,128)(2,1)S(1)}, f32[8,128]{1,0:T(8,128)S(1)}) custom-call(f32[19912,128]{1,0:T(8,128)S(1)} %get-tuple-element.19.field_ref, bf16[3,512,256]{2,1,0:T(8,128)(2,1)S(1)} %fusion.2.w1_ref, f32[1,128]{1,0:T(1,128)S(1)} %bitcast.10), custom_call_target="tpu_custom_call" | custom-call | tf_op jit(solution)/shard_map/inner/pallas_call | solution.py:317
  90.0 0.0 collective-permute-done.1.east_ref
  90.0 0.0 collective-permute-done.west_ref
  90.0 0.7 collective-permute-start.4
  90.7 4.1 %collective-permute-start.2 = (bf16[2,136,128]{2,1,0:T(8,128)(2,1)S(1)}, bf16[2,136,128]{2,1,0:T(8,128)(2,1)S(1)}, u32[]{:S(2)}, u32[]{:S(2)}) collective-permute-start(bf16[2,136,128]{2,1,0:T(8,128)(2,1)S(1)} %get-tuple-element.30), channel_id=1, source_target_pairs={{0,32},{32,64},{64,96},{1,33},{33,65},{65,97},{2,34},{34,66},{66,9... | collective-permute-start | bytes 208904 | tf_op jit(solution)/shard_map/ppermute | solution.py:514
  94.8 0.0 copy-start.2
  94.8 0.0 copy-start.4
  94.8 2.6 %collective-permute-start.3 = (bf16[2,136,128]{2,1,0:T(8,128)(2,1)S(1)}, bf16[2,136,128]{2,1,0:T(8,128)(2,1)S(1)}, u32[]{:S(2)}, u32[]{:S(2)}) collective-permute-start(bf16[2,136,128]{2,1,0:T(8,128)(2,1)S(1)} %get-tuple-element.31), channel_id=1, source_target_pairs={{32,0},{64,32},{96,64},{33,1},{65,33},{97,65},{34,2},{66,34},{98,6... | collective-permute-start | bytes 208904 | tf_op jit(solution)/shard_map/ppermute | solution.py:515
  97.5 5.7 %inner.3 = (bf16[32,64,384]{2,1,0:T(8,128)(2,1)S(1)}, bf16[33,64,384]{2,1,0:T(8,128)(2,1)S(1)}, f32[8,128]{1,0:T(8,128)}) custom-call(f32[19912,128]{1,0:T(8,128)S(1)} %get-tuple-element.19.field_ref, bf16[3,512,256]{2,1,0:T(8,128)(2,1)S(1)} %fusion.2.w1_ref, f32[1,128]{1,0:T(1,128)S(1)} %bitcast.11), custom_call_target="tpu_custom_call" | custom-call | tf_op jit(solution)/shard_map/inner/pallas_call | solution.py:317
  103.2 0.0 collective-permute-done.2.down_ref
  103.2 0.0 collective-permute-done.3.up_ref
  103.2 0.0 collective-permute-done.4.across_ref
  103.2 7.2 %rim.1 = (bf16[32,64,384]{2,1,0:T(8,128)(2,1)S(1)}, bf16[33,64,384]{2,1,0:T(8,128)(2,1)S(1)}, bf16[32,64,384]{2,1,0:T(8,128)(2,1)S(1)}, bf16[33,64,384]{2,1,0:T(8,128)(2,1)S(1)}, bf16[64,64,128]{2,1,0:T(8,128)(2,1)}) custom-call(s32[1]{0:T(128)} %bitcast.band_ref, ...), custom_call_target="tpu_custom_call", output_to_operand_aliasing={{0}: (1, {}), {1}: (2, {}), {2}: (3, {}), {3}: (4, {})} | custom-call | tf_op jit(solution)/shard_map/rim/pallas_call | solution.py:475
  (7 shorter events, 0.1 us)
Async XLA Ops:
  4.7 56.2 %all-to-all-start = ((bf16[128,104,128]{2,1,0:T(8,128)(2,1)}), bf16[128,104,128]{2,1,0:T(8,128)(2,1)S(1)}, u32[]{:S(2)}, u32[]{:S(2)}) async-start(bf16[128,104,128]{2,1,0:T(8,128)(2,1)} %pack.1), calls=%async_computation | async-start | bytes 6815744 | tf_op jit(solution)/shard_map/all_to_all | solution.py:502
  16.2 2.2 %copy-start = (bf16[128,128,128]{2,1,0:T(8,128)(2,1)S(1)}, bf16[128,128,128]{2,1,0:T(8,128)(2,1)}, u32[]{:S(2)}) copy-start(bf16[128,128,128]{2,1,0:T(8,128)(2,1)} %field_ref.1) | copy-start | bytes 12582916
  60.8 23.9 %copy-start.1 = (bf16[3,3,128,128]{3,2,1,0:T(8,128)(2,1)S(1)}, bf16[3,3,128,128]{3,2,1,0:T(8,128)(2,1)}, u32[]{:S(2)}) copy-start(bf16[3,3,128,128]{3,2,1,0:T(8,128)(2,1)} %param.12) | copy-start | bytes 884740
  60.8 24.0 %copy-start.3 = (f32[128]{0:T(128)S(1)}, f32[128]{0:T(128)}, u32[]{:S(2)}) copy-start(f32[128]{0:T(128)} %param.13) | copy-start | bytes 1540
  79.0 11.0 %collective-permute-start = (bf16[264,128]{1,0:T(8,128)(2,1)S(1)}, bf16[264,128]{1,0:T(8,128)(2,1)S(1)}, u32[]{:S(2)}, u32[]{:S(2)}) collective-permute-start(bf16[264,128]{1,0:T(8,128)(2,1)S(1)} %get-tuple-element.24.right_ref), channel_id=1, source_target_pairs={{0,1},{1,2},{2,3},{3,4},{4,5},{5,6},{6,7},{7,8},{8,9},{9,10},{10,1... | collective-permute-start | bytes 202760 | tf_op jit(solution)/shard_map/ppermute | solution.py:510
  79.6 10.3 %collective-permute-start.1 = (bf16[136,128]{1,0:T(8,128)(2,1)S(1)}, bf16[136,128]{1,0:T(8,128)(2,1)S(1)}, u32[]{:S(2)}, u32[]{:S(2)}) collective-permute-start(bf16[136,128]{1,0:T(8,128)(2,1)S(1)} %get-tuple-element.25.left_ref), channel_id=1, source_target_pairs={{1,0},{2,1},{3,2},{4,3},{5,4},{6,5},{7,6},{8,7},{9,8},{10,9},{11,1... | collective-permute-start | bytes 104456 | tf_op jit(solution)/shard_map/ppermute | solution.py:511
  90.0 13.1 %collective-permute-start.4 = (bf16[4,136,128]{2,1,0:T(8,128)(2,1)S(1)}, bf16[4,136,128]{2,1,0:T(8,128)(2,1)S(1)}, u32[]{:S(2)}, u32[]{:S(2)}) collective-permute-start(bf16[4,136,128]{2,1,0:T(8,128)(2,1)S(1)} %get-tuple-element.29.own_ref), channel_id=1, source_target_pairs={{0,16},{1,17},{2,18},{3,19},{4,20},{5,21},{6,22},{7,23},{8,24},{9,... | collective-permute-start | bytes 417800 | tf_op jit(solution)/shard_map/ppermute | solution.py:516
  90.7 12.5 %collective-permute-start.2 = (bf16[2,136,128]{2,1,0:T(8,128)(2,1)S(1)}, bf16[2,136,128]{2,1,0:T(8,128)(2,1)S(1)}, u32[]{:S(2)}, u32[]{:S(2)}) collective-permute-start(bf16[2,136,128]{2,1,0:T(8,128)(2,1)S(1)} %get-tuple-element.30), channel_id=1, source_target_pairs={{0,32},{32,64},{64,96},{1,33},{33,65},{65,97},{2,34},{34,66},{66,9... | collective-permute-start | bytes 208904 | tf_op jit(solution)/shard_map/ppermute | solution.py:514
  94.8 8.3 %copy-start.2 = (bf16[3,3,128,128]{3,2,1,0:T(8,128)(2,1)S(1)}, bf16[3,3,128,128]{3,2,1,0:T(8,128)(2,1)}, u32[]{:S(2)}) copy-start(bf16[3,3,128,128]{3,2,1,0:T(8,128)(2,1)} %param.14) | copy-start | bytes 884740
  94.8 8.3 %copy-start.4 = (f32[128]{0:T(128)S(1)}, f32[128]{0:T(128)}, u32[]{:S(2)}) copy-start(f32[128]{0:T(128)} %param.15) | copy-start | bytes 1540
  94.8 8.3 %collective-permute-start.3 = (bf16[2,136,128]{2,1,0:T(8,128)(2,1)S(1)}, bf16[2,136,128]{2,1,0:T(8,128)(2,1)S(1)}, u32[]{:S(2)}, u32[]{:S(2)}) collective-permute-start(bf16[2,136,128]{2,1,0:T(8,128)(2,1)S(1)} %get-tuple-element.31), channel_id=1, source_target_pairs={{32,0},{64,32},{96,64},{33,1},{65,33},{97,65},{34,2},{66,34},{98,6... | collective-permute-start | bytes 208904 | tf_op jit(solution)/shard_map/ppermute | solution.py:515

commit v5 on v4

--- a/solution.py
+++ b/solution.py
@@ -50,26 +50,25 @@
     numbers.wait()
     totals.wait()
     cells = where_ref[...]
-    across = jnp.broadcast_to(live_ref[...], (owners, owners))
-    down = lax.broadcasted_iota(jnp.int32, (owners, owners), 0)
-    lane = lax.broadcasted_iota(jnp.int32, (owners, owners), 1)
-    counts = jnp.sum(jnp.where(down == lane, across, 0).astype(jnp.float32), axis=1, keepdims=True)
-    place = lax.broadcasted_iota(jnp.int32, cells.shape, 1)
-    live = place.astype(jnp.float32) < counts
+    place = lax.broadcasted_iota(jnp.int32, cells.shape, 0)
+    live = place < live_ref[...]
     row = cells >> 7
     col = cells & 127
-    high = jnp.where(live, row + 2, 0).astype(jnp.float32)
-    low = jnp.where(live, (col >> 1) + jnp.where((col & 1) == 1, ODD, EVEN), 0).astype(jnp.float32)
-    blank = jnp.zeros((owners, 128 - slots), jnp.int32)
-    marked = jnp.concatenate([jnp.where(live, cells, -1), blank - 1], axis=1)
-    again = jnp.zeros(marked.shape, jnp.float32)
+    high = jnp.where(live, row + 2, 0)
+    low = jnp.where(live, (col >> 1) + jnp.where((col & 1) == 1, ODD, EVEN), 0)
+    marked = jnp.where(live, cells, -1)
+    again = jnp.zeros(cells.shape, jnp.int32)
     for back in range(1, BATCH):
-        same = (pltpu.roll(marked, back, 1) == marked) & (marked >= 0) & (lane % BATCH >= back)
-        again = jnp.where(same, 1.0, again)
-    blank = blank.astype(jnp.float32)
-    meta_ref[pl.ds(0, owners, stride=META), :] = jnp.concatenate([high, blank], axis=1)
-    meta_ref[pl.ds(1, owners, stride=META), :] = jnp.concatenate([low, blank], axis=1)
-    meta_ref[pl.ds(2, owners, stride=META), :] = again
+        same = (pltpu.roll(marked, back, 0) == marked) & live & (place % BATCH >= back)
+        again = jnp.where(same, 1, again)
+    blank = jnp.zeros((128 - slots, owners), jnp.float32)
+
+    def turned(x):
+        return jnp.concatenate([x.astype(jnp.float32), blank], axis=0).T
+
+    meta_ref[pl.ds(0, owners, stride=META), :] = turned(high)
+    meta_ref[pl.ds(1, owners, stride=META), :] = turned(low)
+    meta_ref[pl.ds(2, owners, stride=META), :] = turned(again)
     for m in range(3, META):
         meta_ref[pl.ds(m, owners, stride=META), :] = jnp.zeros((owners, 128), jnp.float32)
     held_ref[:, pl.ds(slots, META), :] = meta_ref[...].reshape(owners, META, 128).astype(jnp.bfloat16)
@@ -89,7 +88,7 @@
         out_specs=ANY,
         scratch_shapes=[
             pltpu.VMEM((owners, slots + META, chans), jnp.bfloat16),
-            pltpu.VMEM((owners, slots), jnp.int32),
+            pltpu.VMEM((slots, owners), jnp.int32),
             pltpu.VMEM((1, owners), jnp.int32),
             pltpu.VMEM((owners * META, chans), jnp.float32),
             pltpu.SemaphoreType.DMA((2 * CHUNKS + 2,)),
@@ -99,14 +98,11 @@
     )(off_chip(values), off_chip(cells), off_chip(counts))
 
 
-def spread_kernel(field_ref, acc_ref, wide_ref):
+def spread_kernel(field_ref, parted_ref, wide_ref):
     def step(r, carry):
         wide_ref[...] = field_ref[r].astype(jnp.float32)
-        base = pl.multiple_of((r + 2) * PITCH, 8)
-        acc_ref[pl.ds(base + ODD, 64), :] = wide_ref[pl.ds(1, 64, stride=2), :]
-        acc_ref[pl.ds(base + EVEN, 64), :] = wide_ref[pl.ds(0, 64, stride=2), :]
-        for at in (0, EVEN - 8, EVEN + 64):
-            acc_ref[pl.ds(base + at, 8), :] = jnp.zeros((8, 128), jnp.float32)
+        parted_ref[r, pl.ds(0, 64), :] = wide_ref[pl.ds(1, 64, stride=2), :].astype(jnp.bfloat16)
+        parted_ref[r, pl.ds(64, 64), :] = wide_ref[pl.ds(0, 64, stride=2), :].astype(jnp.bfloat16)
         return carry
 
     lax.fori_loop(0, field_ref.shape[0], step, 0)
@@ -115,7 +111,7 @@
 def spread(field):
     return pl.pallas_call(
         spread_kernel,
-        out_shape=pltpu.HBM((SLABS * PITCH, 128), jnp.float32),
+        out_shape=pltpu.HBM(field.shape, field.dtype),
         in_specs=[VMEM],
         out_specs=VMEM,
         scratch_shapes=[pltpu.VMEM((128, 128), jnp.float32)],
@@ -124,12 +120,16 @@
     )(field)
 
 
-def scatter_kernel(band_ref, got_ref, start_ref, acc_ref, right_ref, left_ref, near_ref, rows_ref, *rest):
-    other_ref, wide_ref, meta_ref, index_ref, late_ref, cells0_ref, cells1_ref, list_ref, sem = rest
+def scatter_kernel(band_ref, got_ref, parted_ref, acc_ref, right_ref, left_ref, near_ref, rows_ref, *rest):
+    other_ref, start_ref, wide_ref, meta_ref, index_ref, late_ref, cells0_ref, cells1_ref, list_ref, sem = rest
     del band_ref
     sources, slots = got_ref.shape[0], got_ref.shape[1] - META
-    first = pltpu.make_async_copy(start_ref, acc_ref, sem.at[0])
-    first.start()
+    part = 128 // CHUNKS
+    pieces = []
+    for n in range(CHUNKS):
+        here = pl.ds(n * part, part)
+        pieces.append(pltpu.make_async_copy(parted_ref.at[here], start_ref.at[here], sem.at[3 + n]))
+        pieces[-1].start()
 
     def unpack(s, carry):
         meta_ref[pl.ds(pl.multiple_of(s * META, META), META), :] = got_ref[s, pl.ds(slots, META), :].astype(jnp.float32)
@@ -145,26 +145,41 @@
     inside = lane < slots
     count = jnp.sum(jnp.where(inside, again, 0.0), axis=1, keepdims=True)
     furthest = jnp.max(jnp.where(inside & (again > 0), lane, 0).astype(jnp.float32), axis=1, keepdims=True)
-    notes = jnp.where(lane == slots, count, furthest)
+    crowd = jnp.sum(count.reshape(sources // GROUP, GROUP, 1), axis=1, keepdims=True)
+    crowd = jnp.broadcast_to(crowd, (sources // GROUP, GROUP, 128)).reshape(sources, 128)
+    notes = jnp.where(lane == slots, count, jnp.where(lane == slots + 1, furthest, crowd))
     late = jnp.where(inside, again * spot, notes)
     late_ref[...] = late.astype(jnp.int32)
 
     cells = (cells0_ref, cells1_ref)
 
     def fetch(group, half):
-        return pltpu.make_async_copy(index_ref.at[pl.ds(group * GROUP, GROUP), :], cells[half], sem.at[1 + half])
+        return pltpu.make_async_copy(index_ref.at[pl.ds(group * GROUP, GROUP), :], cells[half], sem.at[half])
 
     fetch(0, 0).start()
     fetch(1, 1).start()
-    listed = pltpu.make_async_copy(late_ref, list_ref, sem.at[3])
+    listed = pltpu.make_async_copy(late_ref, list_ref, sem.at[2])
     listed.start()
 
     def clear(r, carry):
-        other_ref[pl.ds(pl.multiple_of((r + 2) * PITCH, 8), PITCH), :] = jnp.zeros((PITCH, 128), jnp.float32)
+        base = pl.multiple_of((r + 2) * PITCH, 8)
+        for at in (ODD, EVEN):
+            other_ref[pl.ds(base + at, 64), :] = jnp.zeros((64, 128), jnp.float32)
         return carry
 
     lax.fori_loop(0, 128, clear, 0)
-    first.wait()
+
+    def widen(r, carry):
+        base = pl.multiple_of((r + 2) * PITCH, 8)
+        for at in (0, EVEN - 8, EVEN + 64):
+            acc_ref[pl.ds(base + at, 8), :] = jnp.zeros((8, 128), jnp.float32)
+        acc_ref[pl.ds(base + ODD, 64), :] = start_ref[r, pl.ds(0, 64), :].astype(jnp.float32)
+        acc_ref[pl.ds(base + EVEN, 64), :] = start_ref[r, pl.ds(64, 64), :].astype(jnp.float32)
+        return carry
+
+    for n, piece in enumerate(pieces):
+        piece.wait()
+        lax.fori_loop(n * part, (n + 1) * part, widen, 0)
     accs = (acc_ref, other_ref)
 
     def add(step, carry):
@@ -211,11 +226,18 @@
 
         return carry
 
-    lax.fori_loop(0, sources, rest_of, 0)
+    for group in range(sources // GROUP):
+
+        @pl.when(list_ref[group * GROUP, slots + 2] > 0)
+        def _():
+            lax.fori_loop(group * GROUP, (group + 1) * GROUP, rest_of, 0)
+
 
     def merge(r, carry):
-        here = pl.ds(pl.multiple_of((r + 2) * PITCH, 8), PITCH)
-        acc_ref[here, :] = acc_ref[here, :] + other_ref[here, :]
+        base = pl.multiple_of((r + 2) * PITCH, 8)
+        for at in (ODD, EVEN):
+            here = pl.ds(base + at, 64)
+            acc_ref[here, :] = acc_ref[here, :] + other_ref[here, :]
         return carry
 
     lax.fori_loop(0, 128, merge, 0)
@@ -239,7 +261,7 @@
     return pl.pallas_call(
         scatter_kernel,
         out_shape=[
-            pltpu.VMEM(start.shape, jnp.float32),
+            pltpu.VMEM((SLABS * PITCH, 128), jnp.float32),
             jax.ShapeDtypeStruct((264, 128), jnp.bfloat16),
             jax.ShapeDtypeStruct((136, 128), jnp.bfloat16),
             jax.ShapeDtypeStruct((128, 128), jnp.bfloat16),
@@ -249,6 +271,7 @@
         out_specs=[VMEM] * 5,
         scratch_shapes=[
             pltpu.VMEM((130 * PITCH, 128), jnp.float32),
+            pltpu.VMEM((128, 128, 128), jnp.bfloat16),
             pltpu.VMEM((2, 96, 128), jnp.float32),
             pltpu.VMEM((128 * META, 128), jnp.float32),
             pltpu.VMEM((128, 128), jnp.int32),
@@ -256,7 +279,7 @@
             pltpu.SMEM((GROUP, 128), jnp.int32),
             pltpu.SMEM((GROUP, 128), jnp.int32),
             pltpu.SMEM((128, 128), jnp.int32),
-            pltpu.SemaphoreType.DMA((4,)),
+            pltpu.SemaphoreType.DMA((3 + CHUNKS,)),
         ],
         compiler_params=pltpu.CompilerParams(vmem_limit_bytes=24 << 20),
         name="scatter",
@@ -498,7 +521,7 @@
     up_pairs = [(j, i) for i, j in down_pairs]
     pole_pairs = [(b * lon + i, b * lon + (i + lon // 2) % lon) for b in (0, lat - 1) for i in range(lon)]
 
-    sent = pack(values[0], cells[0], counts)
+    sent = pack(values[0], cells[0].T, counts)
     got = lax.all_to_all(sent, ("lat", "lon"), split_axis=0, concat_axis=0, tiled=True)
     field, right, left, near, rows = scatter(band, got, spread(background))
 

time: 111 us -> 106 us (0.955)
  Pallas kernels: 45.1 us -> 39.9 us
  waiting for transfers between devices: 36.7 us -> 38.7 us
  local copies, waits for them, and re-layouts: 3.73 us -> 2.2 us
    pallas_call x2, Pallas kernels: 23.9 us -> 18.8 us  [the longest x1 15 us: scatter(): pl.pallas_call(scatter_kernel, out_shape=[pltpu.VMEM((SLABS * PITCH, 128)...]
    all_to_all x1, waiting for transfers between devices: 36.7 us -> 38.7 us  [shards(): lax.all_to_all(sent, ('lat', 'lon'), split_axis=0, concat_axis=0, tiled=T...]
    unnamed x11 -> x10, local copies, waits for them, and re-layouts: 3.73 us -> 2.2 us
  transfers between devices with their start and end apart: 6 -> 6, of which waited for: 1 -> 1; matrix products, arithmetic and copies ran while one was open for 0% -> 0% of each run, Pallas kernels for 15% -> 14%
where the time goes in v5:
time: 106 us; the launch traced here: 105 us
  Pallas kernels  39.9 us (38%)
  waiting for transfers between devices  38.7 us (37%)
  starting transfers between devices  24 us (23%)
  local copies, waits for them, and re-layouts  2.2 us (2%)
    all_to_all x1, waiting for transfers between devices, shards(): lax.all_to_all(sent, ('lat', 'lon'), split_axis=0, concat_axis=0, tiled=T...  38.7 us
    pallas_call x1, Pallas kernels, scatter(): pl.pallas_call(scatter_kernel, out_shape=[pltpu.VMEM((SLABS * PITCH, 128)...  15 us
    all_to_all x1, starting transfers between devices, shards(): lax.all_to_all(sent, ('lat', 'lon'), split_axis=0, concat_axis=0, tiled=T...  11.5 us
    pallas_call x2, Pallas kernels, inner(): pl.pallas_call(functools.partial(inner_kernel, low), out_shape=[pltpu.VME...  10.8 us
    pallas_call x1, Pallas kernels, rim(): pl.pallas_call(rim_kernel, out_shape=[pltpu.VMEM(b.shape, b.dtype) for b...  7.22 us
    ppermute x1, starting transfers between devices, shards(): east = lax.ppermute(left, 'lon', west_pairs)  5.07 us
    ppermute x1, starting transfers between devices, shards(): down = lax.ppermute(lower_rows, 'lat', down_pairs)  4.01 us
    pallas_call x1, Pallas kernels, spread(): pl.pallas_call(spread_kernel, out_shape=pltpu.HBM(field.shape, field.dtyp...  3.79 us
  transfers between devices with their start and end apart: 6, of which 1 were waited for; matrix products, arithmetic and copies ran while one was open for 0% of the time, Pallas kernels for 14%

profile of v5, /device:TPU:1, one launch (start us, length us, event | category | flops | bytes accessed | tf_op | source)
XLA Modules:
  0.0 104.9 jit_solution(8151322781284887592)
XLA Ops:
  0.0 3.0 %pack.1 = bf16[128,104,128]{2,1,0:T(8,128)(2,1)} custom-call(bf16[128,96,128]{2,1,0:T(8,128)(2,1)} %bitcast.16, s32[96,128]{1,0:T(8,128)} %bitcast.17, s32[1,128]{1,0:T(1,128)} %counts_ref.1), custom_call_target="tpu_custom_call" | custom-call | tf_op jit(solution)/shard_map/pack/pallas_call | solution.py:84
  3.0 11.5 %all-to-all-start = ((bf16[128,104,128]{2,1,0:T(8,128)(2,1)}), bf16[128,104,128]{2,1,0:T(8,128)(2,1)S(1)}, u32[]{:S(2)}, u32[]{:S(2)}) async-start(bf16[128,104,128]{2,1,0:T(8,128)(2,1)} %pack.1), calls=%async_computation | async-start | bytes 6815744 | tf_op jit(solution)/shard_map/all_to_all | solution.py:525
  14.5 0.0 copy-start
  14.5 2.2 %copy-done = bf16[128,128,128]{2,1,0:T(8,128)(2,1)S(1)} copy-done((bf16[128,128,128]{2,1,0:T(8,128)(2,1)S(1)}, bf16[128,128,128]{2,1,0:T(8,128)(2,1)}, u32[]{:S(2)}) %copy-start) | copy-done | bytes 4194328
  16.7 3.8 %spread.1.parted_ref = bf16[128,128,128]{2,1,0:T(8,128)(2,1)} custom-call(bf16[128,128,128]{2,1,0:T(8,128)(2,1)S(1)} %copy-done), custom_call_target="tpu_custom_call" | custom-call | tf_op jit(solution)/shard_map/spread/pallas_call | solution.py:112
  20.5 38.7 %all-to-all-done.got_ref = bf16[128,104,128]{2,1,0:T(8,128)(2,1)S(1)} async-done(((bf16[128,104,128]{2,1,0:T(8,128)(2,1)}), bf16[128,104,128]{2,1,0:T(8,128)(2,1)S(1)}, u32[]{:S(2)}, u32[]{:S(2)}) %all-to-all-start) | async-done | bytes 3407904 | tf_op jit(solution)/shard_map/all_to_all | solution.py:525
  59.2 15.0 %scatter.1 = (f32[19912,128]{1,0:T(8,128)S(1)}, bf16[264,128]{1,0:T(8,128)(2,1)S(1)}, bf16[136,128]{1,0:T(8,128)(2,1)S(1)}, bf16[128,128]{1,0:T(8,128)(2,1)S(1)}, bf16[4,128,128]{2,1,0:T(8,128)(2,1)S(1)}) custom-call(s32[1]{0:T(128)} %bitcast.band_ref, bf16[128,104,128]{2,1,0:T(8,128)(2,1)S(1)} %all-to-all-done.got_ref, bf16[128,128,128]{2,1,0:T(8,128)(2,1)} %spread.1.parted_ref), custom_call_target="tpu_custom_call" | custom-call | tf_op jit(solution)/shard_map/scatter/pallas_call | solution.py:261
  74.2 0.7 collective-permute-start
  74.9 5.1 %collective-permute-start.1 = (bf16[136,128]{1,0:T(8,128)(2,1)S(1)}, bf16[136,128]{1,0:T(8,128)(2,1)S(1)}, u32[]{:S(2)}, u32[]{:S(2)}) collective-permute-start(bf16[136,128]{1,0:T(8,128)(2,1)S(1)} %get-tuple-element.25.left_ref), channel_id=1, source_target_pairs={{1,0},{2,1},{3,2},{4,3},{5,4},{6,5},{7,6},{8,7},{9,8},{10,9},{11,1... | collective-permute-start | bytes 104456 | tf_op jit(solution)/shard_map/ppermute | solution.py:534
  79.9 0.0 copy-done.1
  79.9 0.1 fusion.2.w1_ref
  80.0 5.1 %inner.2 = (bf16[32,64,384]{2,1,0:T(8,128)(2,1)S(1)}, bf16[33,64,384]{2,1,0:T(8,128)(2,1)S(1)}, f32[8,128]{1,0:T(8,128)S(1)}) custom-call(f32[19912,128]{1,0:T(8,128)S(1)} %get-tuple-element.19.field_ref, bf16[3,512,256]{2,1,0:T(8,128)(2,1)S(1)} %fusion.2.w1_ref, f32[1,128]{1,0:T(1,128)S(1)} %bitcast.12), custom_call_target="tpu_custom_call" | custom-call | tf_op jit(solution)/shard_map/inner/pallas_call | solution.py:340
  85.1 0.0 collective-permute-done.1.east_ref
  85.2 0.0 collective-permute-done.west_ref
  85.2 0.7 collective-permute-start.4
  85.9 4.0 %collective-permute-start.2 = (bf16[2,136,128]{2,1,0:T(8,128)(2,1)S(1)}, bf16[2,136,128]{2,1,0:T(8,128)(2,1)S(1)}, u32[]{:S(2)}, u32[]{:S(2)}) collective-permute-start(bf16[2,136,128]{2,1,0:T(8,128)(2,1)S(1)} %get-tuple-element.30), channel_id=1, source_target_pairs={{0,32},{32,64},{64,96},{1,33},{33,65},{65,97},{2,34},{34,66},{66,9... | collective-permute-start | bytes 208904 | tf_op jit(solution)/shard_map/ppermute | solution.py:537
  89.9 0.0 copy-start.2
  89.9 0.0 copy-start.4
  89.9 2.1 %collective-permute-start.3 = (bf16[2,136,128]{2,1,0:T(8,128)(2,1)S(1)}, bf16[2,136,128]{2,1,0:T(8,128)(2,1)S(1)}, u32[]{:S(2)}, u32[]{:S(2)}) collective-permute-start(bf16[2,136,128]{2,1,0:T(8,128)(2,1)S(1)} %get-tuple-element.31), channel_id=1, source_target_pairs={{32,0},{64,32},{96,64},{33,1},{65,33},{97,65},{34,2},{66,34},{98,6... | collective-permute-start | bytes 208904 | tf_op jit(solution)/shard_map/ppermute | solution.py:538
  92.0 5.7 %inner.3 = (bf16[32,64,384]{2,1,0:T(8,128)(2,1)S(1)}, bf16[33,64,384]{2,1,0:T(8,128)(2,1)S(1)}, f32[8,128]{1,0:T(8,128)}) custom-call(f32[19912,128]{1,0:T(8,128)S(1)} %get-tuple-element.19.field_ref, bf16[3,512,256]{2,1,0:T(8,128)(2,1)S(1)} %fusion.2.w1_ref, f32[1,128]{1,0:T(1,128)S(1)} %bitcast.13), custom_call_target="tpu_custom_call" | custom-call | tf_op jit(solution)/shard_map/inner/pallas_call | solution.py:340
  97.7 0.0 collective-permute-done.2.down_ref
  97.7 0.0 collective-permute-done.3.up_ref
  97.7 0.0 collective-permute-done.4.across_ref
  97.7 7.2 %rim.1 = (bf16[32,64,384]{2,1,0:T(8,128)(2,1)S(1)}, bf16[33,64,384]{2,1,0:T(8,128)(2,1)S(1)}, bf16[32,64,384]{2,1,0:T(8,128)(2,1)S(1)}, bf16[33,64,384]{2,1,0:T(8,128)(2,1)S(1)}, bf16[64,64,128]{2,1,0:T(8,128)(2,1)}) custom-call(s32[1]{0:T(128)} %bitcast.band_ref, ...), custom_call_target="tpu_custom_call", output_to_operand_aliasing={{0}: (1, {}), {1}: (2, {}), {2}: (3, {}), {3}: (4, {})} | custom-call | tf_op jit(solution)/shard_map/rim/pallas_call | solution.py:498
  (6 shorter events, 0.0 us)
Async XLA Ops:
  3.0 56.2 %all-to-all-start = ((bf16[128,104,128]{2,1,0:T(8,128)(2,1)}), bf16[128,104,128]{2,1,0:T(8,128)(2,1)S(1)}, u32[]{:S(2)}, u32[]{:S(2)}) async-start(bf16[128,104,128]{2,1,0:T(8,128)(2,1)} %pack.1), calls=%async_computation | async-start | bytes 6815744 | tf_op jit(solution)/shard_map/all_to_all | solution.py:525
  14.5 2.2 %copy-start = (bf16[128,128,128]{2,1,0:T(8,128)(2,1)S(1)}, bf16[128,128,128]{2,1,0:T(8,128)(2,1)}, u32[]{:S(2)}) copy-start(bf16[128,128,128]{2,1,0:T(8,128)(2,1)} %field_ref.1) | copy-start | bytes 12582916
  59.2 20.8 %copy-start.1 = (bf16[3,3,128,128]{3,2,1,0:T(8,128)(2,1)S(1)}, bf16[3,3,128,128]{3,2,1,0:T(8,128)(2,1)}, u32[]{:S(2)}) copy-start(bf16[3,3,128,128]{3,2,1,0:T(8,128)(2,1)} %param.12) | copy-start | bytes 884740
  59.2 20.8 %copy-start.3 = (f32[128]{0:T(128)S(1)}, f32[128]{0:T(128)}, u32[]{:S(2)}) copy-start(f32[128]{0:T(128)} %param.13) | copy-start | bytes 1540
  74.2 11.0 %collective-permute-start = (bf16[264,128]{1,0:T(8,128)(2,1)S(1)}, bf16[264,128]{1,0:T(8,128)(2,1)S(1)}, u32[]{:S(2)}, u32[]{:S(2)}) collective-permute-start(bf16[264,128]{1,0:T(8,128)(2,1)S(1)} %get-tuple-element.24.right_ref), channel_id=1, source_target_pairs={{0,1},{1,2},{2,3},{3,4},{4,5},{5,6},{6,7},{7,8},{8,9},{9,10},{10,1... | collective-permute-start | bytes 202760 | tf_op jit(solution)/shard_map/ppermute | solution.py:533
  74.9 10.3 %collective-permute-start.1 = (bf16[136,128]{1,0:T(8,128)(2,1)S(1)}, bf16[136,128]{1,0:T(8,128)(2,1)S(1)}, u32[]{:S(2)}, u32[]{:S(2)}) collective-permute-start(bf16[136,128]{1,0:T(8,128)(2,1)S(1)} %get-tuple-element.25.left_ref), channel_id=1, source_target_pairs={{1,0},{2,1},{3,2},{4,3},{5,4},{6,5},{7,6},{8,7},{9,8},{10,9},{11,1... | collective-permute-start | bytes 104456 | tf_op jit(solution)/shard_map/ppermute | solution.py:534
  85.2 12.5 %collective-permute-start.4 = (bf16[4,136,128]{2,1,0:T(8,128)(2,1)S(1)}, bf16[4,136,128]{2,1,0:T(8,128)(2,1)S(1)}, u32[]{:S(2)}, u32[]{:S(2)}) collective-permute-start(bf16[4,136,128]{2,1,0:T(8,128)(2,1)S(1)} %get-tuple-element.29.own_ref), channel_id=1, source_target_pairs={{0,16},{1,17},{2,18},{3,19},{4,20},{5,21},{6,22},{7,23},{8,24},{9,... | collective-permute-start | bytes 417800 | tf_op jit(solution)/shard_map/ppermute | solution.py:539
  85.9 11.8 %collective-permute-start.2 = (bf16[2,136,128]{2,1,0:T(8,128)(2,1)S(1)}, bf16[2,136,128]{2,1,0:T(8,128)(2,1)S(1)}, u32[]{:S(2)}, u32[]{:S(2)}) collective-permute-start(bf16[2,136,128]{2,1,0:T(8,128)(2,1)S(1)} %get-tuple-element.30), channel_id=1, source_target_pairs={{0,32},{32,64},{64,96},{1,33},{33,65},{65,97},{2,34},{34,66},{66,9... | collective-permute-start | bytes 208904 | tf_op jit(solution)/shard_map/ppermute | solution.py:537
  89.9 7.8 %copy-start.2 = (bf16[3,3,128,128]{3,2,1,0:T(8,128)(2,1)S(1)}, bf16[3,3,128,128]{3,2,1,0:T(8,128)(2,1)}, u32[]{:S(2)}) copy-start(bf16[3,3,128,128]{3,2,1,0:T(8,128)(2,1)} %param.14) | copy-start | bytes 884740
  89.9 7.8 %copy-start.4 = (f32[128]{0:T(128)S(1)}, f32[128]{0:T(128)}, u32[]{:S(2)}) copy-start(f32[128]{0:T(128)} %param.15) | copy-start | bytes 1540
  89.9 7.8 %collective-permute-start.3 = (bf16[2,136,128]{2,1,0:T(8,128)(2,1)S(1)}, bf16[2,136,128]{2,1,0:T(8,128)(2,1)S(1)}, u32[]{:S(2)}, u32[]{:S(2)}) collective-permute-start(bf16[2,136,128]{2,1,0:T(8,128)(2,1)S(1)} %get-tuple-element.31), channel_id=1, source_target_pairs={{32,0},{64,32},{96,64},{33,1},{65,33},{97,65},{34,2},{66,34},{98,6... | collective-permute-start | bytes 208904 | tf_op jit(solution)/shard_map/ppermute | solution.py:538

commit v6 on v5

--- a/solution.py
+++ b/solution.py
@@ -313,7 +313,7 @@
     )(after, rows, west, east)
 
 
-def inner_kernel(low, field_ref, w1_ref, b1_ref, even_ref, odd_ref, mark_ref, lhs_ref, shift_ref):
+def inner_kernel(low, field_ref, w1_ref, b1_ref, even_ref, odd_ref, edge_ref, lhs_ref, shift_ref, tail_ref):
     f32, bf16 = jnp.float32, jnp.bfloat16
     bias = jnp.concatenate([b1_ref[...], b1_ref[...]], axis=-1)
     weight = w1_ref[...].reshape(1536, 256)
@@ -326,6 +326,12 @@
         window = jnp.concatenate([lhs_ref[pl.ds(di, ROWS)].reshape(ROWS * 64, 512) for di in range(3)], axis=-1)
         hid = gelu(jnp.dot(window, weight, preferred_element_type=f32) + bias).reshape(ROWS, 64, 256)
         shift_ref[:, pl.ds(8, 64), :] = hid[:, :, 128:]
+        tail_ref[...] = hid[:, 56:, :128]
+        for n in range(ROWS):
+            line = pl.ds(b * ROWS + n, 1)
+            edge_ref[0, line, :] = shift_ref[n, pl.ds(8, 1), :]
+            edge_ref[1, line, :] = shift_ref[n, pl.ds(70, 1), :]
+            edge_ref[2, line, :] = tail_ref[n, pl.ds(7, 1), :]
         wide = jnp.concatenate([shift_ref[:, pl.ds(7, 64), :], hid[:, :, :128], hid[:, :, 128:]], axis=-1)
         wide = wide.astype(bf16).reshape(ROWS // 2, 2, 64, 384)
         even_ref[pl.ds(b * (ROWS // 2), ROWS // 2)] = wide[:, 0]
@@ -333,7 +339,6 @@
         return carry
 
     lax.fori_loop(0, 64 // ROWS, step, 0)
-    mark_ref[...] = jnp.zeros(mark_ref.shape, mark_ref.dtype)
 
 
 def inner(low, field, w1, b1):
@@ -342,11 +347,11 @@
         out_shape=[
             pltpu.VMEM((32, 64, 384), jnp.bfloat16),
             pltpu.VMEM((33, 64, 384), jnp.bfloat16),
-            jax.ShapeDtypeStruct((8, 128), jnp.float32),
+            jax.ShapeDtypeStruct((3, 64, 128), jnp.float32),
         ],
         in_specs=[VMEM] * 3,
         out_specs=[VMEM] * 3,
-        scratch_shapes=[pltpu.VMEM((ROWS + 2, 64, 512), jnp.bfloat16), pltpu.VMEM((ROWS, 72, 128), jnp.float32)],
+        scratch_shapes=[pltpu.VMEM((ROWS + 2, 64, 512), jnp.bfloat16), pltpu.VMEM((ROWS, 72, 128), jnp.float32), pltpu.VMEM((ROWS, 8, 128), jnp.float32)],
         compiler_params=pltpu.CompilerParams(vmem_limit_bytes=24 << 20),
         name="inner",
     )(on_chip(field), w1, b1)
@@ -358,6 +363,8 @@
     odd0_in,
     even1_in,
     odd1_in,
+    edge0_ref,
+    edge1_ref,
     right_ref,
     left_ref,
     near_ref,
@@ -381,16 +388,19 @@
     strip_ref,
     shift_ref,
     side_ref,
+    ends_ref,
+    total_ref,
 ):
     del even0_in, odd0_in, even1_in, odd1_in
     f32, bf16 = jnp.float32, jnp.bfloat16
     band = band_ref[0]
     north, south = band == 0, band == 3
-    first = jnp.where(north, 2, 0)
-    flipped = (first, 1, 2 - first)
     dot = functools.partial(jnp.dot, preferred_element_type=f32)
     bias = b1_ref[...]
     bias2 = jnp.concatenate([bias, bias], axis=-1)
+    pairs = w1_ref[...].reshape(1536, 256)
+    taps1 = w1s_ref[...].reshape(1152, 128)
+    taps2 = w2_ref[...].reshape(1152, 128)
 
     body = (
         west_ref[pl.ds(0, 128), :],
@@ -407,107 +417,105 @@
     def wide(ref, n):
         return ref[n].astype(f32)
 
-    rows = (
-        jnp.where(north, wide(across_ref, 1), wide(down_ref, 0)),
-        jnp.where(north, wide(across_ref, 0), wide(down_ref, 1)),
-        wide(own_ref, 0),
-        wide(own_ref, 1),
-        wide(own_ref, 2),
-        wide(own_ref, 3),
-        jnp.where(south, wide(across_ref, 3), wide(up_ref, 0)),
-    )
-    where = (128, 129, 64, 0, 127, 63, 130)
-    lhs = []
-    for n, row in enumerate(rows):
+    second = jnp.where(north, wide(across_ref, 1), wide(down_ref, 0))
+    first = jnp.where(north, wide(across_ref, 0), wide(down_ref, 1))
+    own = [wide(own_ref, n) for n in range(4)]
+    below = jnp.where(south, wide(across_ref, 3), wide(up_ref, 0))
+    top = (jnp.where(north, own[0], second), first, jnp.where(north, second, own[0]))
+    for slab, row in ((0, second), (1, first), (130, below)):
+        for m, at in enumerate((128, 129, 64, 0, 127, 63, 130)):
+            cols_ref[m, pl.ds(slab, 1), :] = row[at : at + 1]
+
+    def lines(n, row):
         strip_ref[n, pl.ds(ODD, 64), :] = row[0:64]
         strip_ref[n, pl.ds(EVEN, 64), :] = row[64:128]
         strip_ref[n, pl.ds(ODD - 1, 1), :] = row[129:130]
         strip_ref[n, pl.ds(EVEN + 64, 1), :] = row[130:131]
-        if n in (0, 1, 6):
-            slab = 130 if n == 6 else n
-            for m, at in enumerate(where):
-                cols_ref[m, pl.ds(slab, 1), :] = row[at : at + 1]
         parts = [strip_ref[n, pl.ds(at, 64), :].astype(bf16) for at in (ODD - 1, EVEN, ODD, EVEN + 1)]
-        lhs.append(jnp.concatenate(parts, axis=-1))
-
-    for n, at in enumerate((0, 1, 4)):
-        total = jnp.zeros((136, 128), f32) + bias
-        top = jnp.zeros((8, 128), f32) + bias
-        for di in range(3):
-            window = jnp.concatenate(
-                [cols_ref[at + m, pl.ds(di, 136), :].astype(bf16) for m in range(3)], axis=-1
-            )
-            total = total + dot(window, w1s_ref[di])
-            if n == 0:
-                top = top + dot(window[0:8], w1s_ref[flipped[di]])
-        side_ref[n, pl.ds(0, 136), :] = gelu(total)
-        if n == 0:
-            side_ref[n, pl.ds(0, 1), :] = gelu(top)[0:1]
-
-    odd1_ref[0] = odd0_ref[32]
-    for r, at, taps in ((-1, 0, flipped), (0, 1, (0, 1, 2)), (127, 4, (0, 1, 2))):
-        pre = bias2
-        for di in range(3):
-            pre = pre + dot(lhs[at + di], w1_ref[taps[di]])
-        hid = gelu(pre)
-        shift_ref[pl.ds(8, 64), :] = hid[:, 128:]
-        shift_ref[pl.ds(7, 1), :] = side_ref[0, pl.ds(r + 1, 1), :]
-        line = jnp.concatenate([shift_ref[pl.ds(7, 64), :], hid[:, :128], hid[:, 128:]], axis=-1).astype(bf16)
+        return jnp.concatenate(parts, axis=-1)
+
+    lhs = [lines(n, row) for n, row in enumerate((top[0], first, top[2], *own, below))]
+    corner = []
+    for row in top:
+        corner.append(jnp.zeros((8, 128), f32))
+        corner.extend(jnp.broadcast_to(row[at : at + 1], (8, 128)) for at in (128, 129, 64))
+    corner = jnp.concatenate(corner, axis=-1).astype(bf16)
+    stack = [jnp.concatenate([lhs[n] for n in picks], axis=-1) for picks in ((0, 1, 2), (1, 3, 4), (5, 6, 7))]
+    hid = gelu(dot(jnp.concatenate([*stack, corner, corner], axis=0), pairs) + bias2)
+
+    windows = []
+    for at in (0, 1, 4):
+        parts = [cols_ref[at + m, pl.ds(di, 136), :] for di in range(3) for m in range(3)]
+        windows.append(jnp.concatenate(parts, axis=-1))
+    cols = gelu(dot(jnp.concatenate(windows, axis=0).astype(bf16), taps1) + bias)
+    for n, to in enumerate((0, 1, 5)):
+        side_ref[to] = cols[n * 136 : (n + 1) * 136]
+    for n in range(3):
+        side_ref[n + 2, pl.ds(1, 64), :] = edge0_ref[n]
+        side_ref[n + 2, pl.ds(65, 64), :] = edge1_ref[n]
+    for n, r in enumerate((-1, 0, 127)):
+        here = pl.ds(r + 1, 1)
+        even, odd = hid[n * 64 : n * 64 + 64, :128], hid[n * 64 : n * 64 + 64, 128:]
+        side_ref[1, here, :] = even[0:1]
+        side_ref[2, here, :] = odd[0:1]
+        side_ref[3, here, :] = odd[62:63]
+        side_ref[4, here, :] = even[63:64]
+        side_ref[5, here, :] = odd[63:64]
+        shift_ref[pl.ds(8, 64), :] = odd
+        line = jnp.concatenate([shift_ref[pl.ds(7, 64), :], even, odd], axis=-1).astype(bf16)
         if r == -1:
             odd0_ref[0] = line
         elif r == 0:
             even0_ref[0] = line
         else:
             odd1_ref[32] = line
-
-    head = lax.broadcasted_iota(jnp.int32, (16, 256), 0) == 0
-    foot = lax.broadcasted_iota(jnp.int32, (16, 128), 0) == 15
-
-    def mend(ref, p, r):
-        here = pl.ds(r + 1, 1)
-        new = jnp.concatenate([side_ref[0, here, :], side_ref[1, here, :]], axis=-1)
-        old = ref[p, pl.ds(0, 16), pl.ds(0, 256)].astype(f32)
-        ref[p, pl.ds(0, 16), pl.ds(0, 256)] = jnp.where(head, new, old).astype(bf16)
-        old = ref[p, pl.ds(48, 16), pl.ds(256, 128)].astype(f32)
-        ref[p, pl.ds(48, 16), pl.ds(256, 128)] = jnp.where(foot, side_ref[2, here, :], old).astype(bf16)
-
-    def mend_step(p, carry):
-        mend(even0_ref, p, 2 * p)
-        mend(odd0_ref, p + 1, 2 * p + 1)
-        mend(even1_ref, p, 2 * p + 64)
-        mend(odd1_ref, p + 1, 2 * p + 65)
-        return carry
-
-    lax.fori_loop(0, 32, mend_step, 0, unroll=2)
+    side_ref[0, pl.ds(0, 1), :] = hid[192:193, 128:]
     odd1_ref[0] = odd0_ref[32]
 
+    windows = []
+    for at in (0, 3):
+        parts = [side_ref[at + m, pl.ds(a, 64, stride=2), :] for a in range(3) for m in range(3)]
+        windows.append(jnp.concatenate(parts, axis=-1))
+    ends_ref[...] = dot(jnp.concatenate(windows, axis=0).astype(bf16), taps2) + b2_ref[...]
+
     for half, (even_ref, odd_ref) in enumerate(((even0_ref, odd0_ref), (even1_ref, odd1_ref))):
 
         def finish(b, carry):
-            total = jnp.broadcast_to(b2_ref[...], (256, 128))
-            total = total + dot(odd_ref[pl.ds(b * 4, 4)].reshape(256, 384), w2_ref[0])
-            total = total + dot(even_ref[pl.ds(b * 4, 4)].reshape(256, 384), w2_ref[1])
-            total = total + dot(odd_ref[pl.ds(b * 4 + 1, 4)].reshape(256, 384), w2_ref[2])
-            out_ref[pl.ds(half * 32 + b * 4, 4)] = total.reshape(4, 64, 128).astype(bf16)
+            p = b * 8
+            window = jnp.concatenate(
+                [
+                    odd_ref[pl.ds(p, 8)].reshape(512, 384),
+                    even_ref[pl.ds(p, 8)].reshape(512, 384),
+                    odd_ref[pl.ds(p + 1, 8)].reshape(512, 384),
+                ],
+                axis=-1,
+            )
+            total_ref[...] = (dot(window, taps2) + b2_ref[...]).reshape(8, 64, 128)
+            for n in range(8):
+                total_ref[n, pl.ds(0, 1), :] = ends_ref[pl.ds(half * 32 + p + n, 1), :]
+                total_ref[n, pl.ds(63, 1), :] = ends_ref[pl.ds(64 + half * 32 + p + n, 1), :]
+            out_ref[pl.ds(half * 32 + p, 8)] = total_ref[...].astype(bf16)
             return carry
 
-        lax.fori_loop(0, 8, finish, 0)
+        lax.fori_loop(0, 4, finish, 0)
 
 
 def rim(band, blocks, *rest):
     return pl.pallas_call(
         rim_kernel,
         out_shape=[pltpu.VMEM(b.shape, b.dtype) for b in blocks] + [jax.ShapeDtypeStruct((64, 64, 128), jnp.bfloat16)],
-        in_specs=[SMEM] + [VMEM] * 18,
+        in_specs=[SMEM] + [VMEM] * 20,
         out_specs=[VMEM] * 5,
         scratch_shapes=[
             pltpu.VMEM((7, 144, 128), jnp.float32),
-            pltpu.VMEM((7, PITCH, 128), jnp.float32),
+            pltpu.VMEM((8, PITCH, 128), jnp.float32),
             pltpu.VMEM((72, 128), jnp.float32),
-            pltpu.VMEM((3, 136, 128), jnp.float32),
+            pltpu.VMEM((6, 136, 128), jnp.float32),
+            pltpu.VMEM((128, 128), jnp.float32),
+            pltpu.VMEM((8, 64, 128), jnp.float32),
         ],
         input_output_aliases={1: 0, 2: 1, 3: 2, 4: 3},
-        compiler_params=pltpu.CompilerParams(vmem_limit_bytes=16 << 20),
+        compiler_params=pltpu.CompilerParams(vmem_limit_bytes=20 << 20),
         name="rim",
     )(band, *map(on_chip, blocks), *rest)[4]
 
@@ -532,15 +540,17 @@
     )
     west = lax.ppermute(right, "lon", east_pairs)
     east = lax.ppermute(left, "lon", west_pairs)
-    *upper, mark = inner(0, field, paired, b1[None])
-    lower_rows, upper_rows, own = frame(mark, rows, west, east)
+    *upper, upper_edge = inner(0, field, paired, b1[None])
+    lower_rows, upper_rows, own = frame(upper_edge, rows, west, east)
     down = lax.ppermute(lower_rows, "lat", down_pairs)
     up = lax.ppermute(upper_rows, "lat", up_pairs)
     across = lax.ppermute(own, ("lat", "lon"), pole_pairs)
-    *lower, _ = inner(64, field, paired, b1[None])
+    *lower, lower_edge = inner(64, field, paired, b1[None])
     return rim(
         band,
         (*upper, *lower),
+        upper_edge,
+        lower_edge,
         right,
         left,
         near,

time: 106 us -> 104 us (0.981)
  Pallas kernels: 39.9 us -> 38.5 us
    pallas_call x1, Pallas kernels: 7.22 us -> 5.96 us  [rim(): pl.pallas_call(rim_kernel, out_shape=[pltpu.VMEM(b.shape, b.dtype) for b...]
where the time goes in v6:
time: 104 us
  waiting for transfers between devices  38.7 us (37%)
  Pallas kernels  38.5 us (37%)
  starting transfers between devices  24.1 us (23%)
  local copies, waits for them, and re-layouts  2.2 us (2%)
    all_to_all x1, waiting for transfers between devices, shards(): lax.all_to_all(sent, ('lat', 'lon'), split_axis=0, concat_axis=0, tiled=T...  38.7 us
    pallas_call x1, Pallas kernels, scatter(): pl.pallas_call(scatter_kernel, out_shape=[pltpu.VMEM((SLABS * PITCH, 128)...  15.4 us
    all_to_all x1, starting transfers between devices, shards(): lax.all_to_all(sent, ('lat', 'lon'), split_axis=0, concat_axis=0, tiled=T...  11.5 us
    pallas_call x2, Pallas kernels, inner(): pl.pallas_call(functools.partial(inner_kernel, low), out_shape=[pltpu.VME...  10.3 us
    pallas_call x1, Pallas kernels, rim(): pl.pallas_call(rim_kernel, out_shape=[pltpu.VMEM(b.shape, b.dtype) for b...  5.96 us
    ppermute x1, starting transfers between devices, shards(): east = lax.ppermute(left, 'lon', west_pairs)  5.67 us
    pallas_call x1, Pallas kernels, spread(): pl.pallas_call(spread_kernel, out_shape=pltpu.HBM(field.shape, field.dtyp...  3.79 us
    ppermute x1, starting transfers between devices, shards(): down = lax.ppermute(lower_rows, 'lat', down_pairs)  3.52 us
  transfers between devices with their start and end apart: 6, of which 1 were waited for; matrix products, arithmetic and copies ran while one was open for 0% of the time, Pallas kernels for 14%

profile of v6, /device:TPU:1, one launch (start us, length us, event | category | flops | bytes accessed | tf_op | source)
XLA Modules:
  0.0 103.7 jit_solution(9817208980669884107)
XLA Ops:
  0.0 3.0 %pack.1 = bf16[128,104,128]{2,1,0:T(8,128)(2,1)} custom-call(bf16[128,96,128]{2,1,0:T(8,128)(2,1)} %bitcast.16, s32[96,128]{1,0:T(8,128)} %bitcast.17, s32[1,128]{1,0:T(1,128)} %counts_ref.1), custom_call_target="tpu_custom_call" | custom-call | tf_op jit(solution)/shard_map/pack/pallas_call | solution.py:84
  3.0 11.5 %all-to-all-start = ((bf16[128,104,128]{2,1,0:T(8,128)(2,1)}), bf16[128,104,128]{2,1,0:T(8,128)(2,1)S(1)}, u32[]{:S(2)}, u32[]{:S(2)}) async-start(bf16[128,104,128]{2,1,0:T(8,128)(2,1)} %pack.1), calls=%async_computation | async-start | bytes 6815744 | tf_op jit(solution)/shard_map/all_to_all | solution.py:533
  14.5 0.0 copy-start
  14.5 2.2 %copy-done = bf16[128,128,128]{2,1,0:T(8,128)(2,1)S(1)} copy-done((bf16[128,128,128]{2,1,0:T(8,128)(2,1)S(1)}, bf16[128,128,128]{2,1,0:T(8,128)(2,1)}, u32[]{:S(2)}) %copy-start) | copy-done | bytes 4194328
  16.7 3.8 %spread.1.parted_ref = bf16[128,128,128]{2,1,0:T(8,128)(2,1)} custom-call(bf16[128,128,128]{2,1,0:T(8,128)(2,1)S(1)} %copy-done), custom_call_target="tpu_custom_call" | custom-call | tf_op jit(solution)/shard_map/spread/pallas_call | solution.py:112
  20.5 38.7 %all-to-all-done.got_ref = bf16[128,104,128]{2,1,0:T(8,128)(2,1)S(1)} async-done(((bf16[128,104,128]{2,1,0:T(8,128)(2,1)}), bf16[128,104,128]{2,1,0:T(8,128)(2,1)S(1)}, u32[]{:S(2)}, u32[]{:S(2)}) %all-to-all-start) | async-done | bytes 3407904 | tf_op jit(solution)/shard_map/all_to_all | solution.py:533
  59.2 15.4 %scatter.1 = (f32[19912,128]{1,0:T(8,128)S(1)}, bf16[264,128]{1,0:T(8,128)(2,1)S(1)}, bf16[136,128]{1,0:T(8,128)(2,1)S(1)}, bf16[128,128]{1,0:T(8,128)(2,1)S(1)}, bf16[4,128,128]{2,1,0:T(8,128)(2,1)S(1)}) custom-call(s32[1]{0:T(128)} %bitcast.band_ref, bf16[128,104,128]{2,1,0:T(8,128)(2,1)S(1)} %all-to-all-done.got_ref, bf16[128,128,128]{2,1,0:T(8,128)(2,1)} %spread.1.parted_ref), custom_call_target="tpu_custom_call" | custom-call | tf_op jit(solution)/shard_map/scatter/pallas_call | solution.py:261
  74.5 0.1 collective-permute-start
  74.6 5.7 %collective-permute-start.1 = (bf16[136,128]{1,0:T(8,128)(2,1)S(1)}, bf16[136,128]{1,0:T(8,128)(2,1)S(1)}, u32[]{:S(2)}, u32[]{:S(2)}) collective-permute-start(bf16[136,128]{1,0:T(8,128)(2,1)S(1)} %get-tuple-element.28.left_ref), channel_id=1, source_target_pairs={{1,0},{2,1},{3,2},{4,3},{5,4},{6,5},{7,6},{8,7},{9,8},{10,9},{11,1... | collective-permute-start | bytes 104456 | tf_op jit(solution)/shard_map/ppermute | solution.py:542
  80.3 0.0 copy-done.1
  80.3 0.1 fusion.2.w1_ref
  80.4 5.2 %inner.2 = (bf16[32,64,384]{2,1,0:T(8,128)(2,1)S(1)}, bf16[33,64,384]{2,1,0:T(8,128)(2,1)S(1)}, f32[3,64,128]{2,1,0:T(8,128)S(1)}) custom-call(f32[19912,128]{1,0:T(8,128)S(1)} %get-tuple-element.20.field_ref, bf16[3,512,256]{2,1,0:T(8,128)(2,1)S(1)} %fusion.2.w1_ref, f32[1,128]{1,0:T(1,128)S(1)} %bitcast.12), custom_call_target="tpu_custom_call" | custom-call | tf_op jit(solution)/shard_map/inner/pallas_call | solution.py:345
  85.6 0.0 collective-permute-done.1.east_ref
  85.6 0.0 collective-permute-done.west_ref
  85.6 0.7 collective-permute-start.4
  86.3 3.5 %collective-permute-start.2 = (bf16[2,136,128]{2,1,0:T(8,128)(2,1)S(1)}, bf16[2,136,128]{2,1,0:T(8,128)(2,1)S(1)}, u32[]{:S(2)}, u32[]{:S(2)}) collective-permute-start(bf16[2,136,128]{2,1,0:T(8,128)(2,1)S(1)} %get-tuple-element.32), channel_id=1, source_target_pairs={{0,32},{32,64},{64,96},{1,33},{33,65},{65,97},{2,34},{34,66},{66,9... | collective-permute-start | bytes 208904 | tf_op jit(solution)/shard_map/ppermute | solution.py:545
  89.8 0.0 copy-start.2
  89.8 0.0 copy-start.4
  89.9 2.7 %collective-permute-start.3 = (bf16[2,136,128]{2,1,0:T(8,128)(2,1)S(1)}, bf16[2,136,128]{2,1,0:T(8,128)(2,1)S(1)}, u32[]{:S(2)}, u32[]{:S(2)}) collective-permute-start(bf16[2,136,128]{2,1,0:T(8,128)(2,1)S(1)} %get-tuple-element.33), channel_id=1, source_target_pairs={{32,0},{64,32},{96,64},{33,1},{65,33},{97,65},{34,2},{66,34},{98,6... | collective-permute-start | bytes 208904 | tf_op jit(solution)/shard_map/ppermute | solution.py:546
  92.6 5.2 %inner.3 = (bf16[32,64,384]{2,1,0:T(8,128)(2,1)S(1)}, bf16[33,64,384]{2,1,0:T(8,128)(2,1)S(1)}, f32[3,64,128]{2,1,0:T(8,128)S(1)}) custom-call(f32[19912,128]{1,0:T(8,128)S(1)} %get-tuple-element.20.field_ref, bf16[3,512,256]{2,1,0:T(8,128)(2,1)S(1)} %fusion.2.w1_ref, f32[1,128]{1,0:T(1,128)S(1)} %bitcast.13), custom_call_target="tpu_custom_call" | custom-call | tf_op jit(solution)/shard_map/inner/pallas_call | solution.py:345
  97.7 0.0 collective-permute-done.2.down_ref
  97.7 0.0 collective-permute-done.3.up_ref
  97.8 0.0 collective-permute-done.4.across_ref
  97.8 6.0 %rim.1 = (bf16[32,64,384]{2,1,0:T(8,128)(2,1)S(1)}, bf16[33,64,384]{2,1,0:T(8,128)(2,1)S(1)}, bf16[32,64,384]{2,1,0:T(8,128)(2,1)S(1)}, bf16[33,64,384]{2,1,0:T(8,128)(2,1)S(1)}, bf16[64,64,128]{2,1,0:T(8,128)(2,1)}) custom-call(s32[1]{0:T(128)} %bitcast.band_ref, ...), custom_call_target="tpu_custom_call", output_to_operand_aliasing={{0}: (1, {}), {1}: (2, {}), {2}: (3, {}), {3}: (4, {})} | custom-call | tf_op jit(solution)/shard_map/rim/pallas_call | solution.py:504
  (6 shorter events, 0.0 us)
Async XLA Ops:
  3.0 56.2 %all-to-all-start = ((bf16[128,104,128]{2,1,0:T(8,128)(2,1)}), bf16[128,104,128]{2,1,0:T(8,128)(2,1)S(1)}, u32[]{:S(2)}, u32[]{:S(2)}) async-start(bf16[128,104,128]{2,1,0:T(8,128)(2,1)} %pack.1), calls=%async_computation | async-start | bytes 6815744 | tf_op jit(solution)/shard_map/all_to_all | solution.py:533
  14.5 2.2 %copy-start = (bf16[128,128,128]{2,1,0:T(8,128)(2,1)S(1)}, bf16[128,128,128]{2,1,0:T(8,128)(2,1)}, u32[]{:S(2)}) copy-start(bf16[128,128,128]{2,1,0:T(8,128)(2,1)} %field_ref.1) | copy-start | bytes 12582916
  59.2 21.1 %copy-start.1 = (bf16[3,3,128,128]{3,2,1,0:T(8,128)(2,1)S(1)}, bf16[3,3,128,128]{3,2,1,0:T(8,128)(2,1)}, u32[]{:S(2)}) copy-start(bf16[3,3,128,128]{3,2,1,0:T(8,128)(2,1)} %param.12) | copy-start | bytes 884740
  59.2 21.2 %copy-start.3 = (f32[128]{0:T(128)S(1)}, f32[128]{0:T(128)}, u32[]{:S(2)}) copy-start(f32[128]{0:T(128)} %param.13) | copy-start | bytes 1540
  74.5 11.0 %collective-permute-start = (bf16[264,128]{1,0:T(8,128)(2,1)S(1)}, bf16[264,128]{1,0:T(8,128)(2,1)S(1)}, u32[]{:S(2)}, u32[]{:S(2)}) collective-permute-start(bf16[264,128]{1,0:T(8,128)(2,1)S(1)} %get-tuple-element.27.right_ref), channel_id=1, source_target_pairs={{0,1},{1,2},{2,3},{3,4},{4,5},{5,6},{6,7},{7,8},{8,9},{9,10},{10,1... | collective-permute-start | bytes 202760 | tf_op jit(solution)/shard_map/ppermute | solution.py:541
  74.6 10.9 %collective-permute-start.1 = (bf16[136,128]{1,0:T(8,128)(2,1)S(1)}, bf16[136,128]{1,0:T(8,128)(2,1)S(1)}, u32[]{:S(2)}, u32[]{:S(2)}) collective-permute-start(bf16[136,128]{1,0:T(8,128)(2,1)S(1)} %get-tuple-element.28.left_ref), channel_id=1, source_target_pairs={{1,0},{2,1},{3,2},{4,3},{5,4},{6,5},{7,6},{8,7},{9,8},{10,9},{11,1... | collective-permute-start | bytes 104456 | tf_op jit(solution)/shard_map/ppermute | solution.py:542
  85.6 12.1 %collective-permute-start.4 = (bf16[4,136,128]{2,1,0:T(8,128)(2,1)S(1)}, bf16[4,136,128]{2,1,0:T(8,128)(2,1)S(1)}, u32[]{:S(2)}, u32[]{:S(2)}) collective-permute-start(bf16[4,136,128]{2,1,0:T(8,128)(2,1)S(1)} %get-tuple-element.31.own_ref), channel_id=1, source_target_pairs={{0,16},{1,17},{2,18},{3,19},{4,20},{5,21},{6,22},{7,23},{8,24},{9,... | collective-permute-start | bytes 417800 | tf_op jit(solution)/shard_map/ppermute | solution.py:547
  86.3 11.4 %collective-permute-start.2 = (bf16[2,136,128]{2,1,0:T(8,128)(2,1)S(1)}, bf16[2,136,128]{2,1,0:T(8,128)(2,1)S(1)}, u32[]{:S(2)}, u32[]{:S(2)}) collective-permute-start(bf16[2,136,128]{2,1,0:T(8,128)(2,1)S(1)} %get-tuple-element.32), channel_id=1, source_target_pairs={{0,32},{32,64},{64,96},{1,33},{33,65},{65,97},{2,34},{34,66},{66,9... | collective-permute-start | bytes 208904 | tf_op jit(solution)/shard_map/ppermute | solution.py:545
  89.8 7.9 %copy-start.2 = (bf16[3,3,128,128]{3,2,1,0:T(8,128)(2,1)S(1)}, bf16[3,3,128,128]{3,2,1,0:T(8,128)(2,1)}, u32[]{:S(2)}) copy-start(bf16[3,3,128,128]{3,2,1,0:T(8,128)(2,1)} %param.14) | copy-start | bytes 884740
  89.8 7.9 %copy-start.4 = (f32[128]{0:T(128)S(1)}, f32[128]{0:T(128)}, u32[]{:S(2)}) copy-start(f32[128]{0:T(128)} %param.15) | copy-start | bytes 1540
  89.9 7.9 %collective-permute-start.3 = (bf16[2,136,128]{2,1,0:T(8,128)(2,1)S(1)}, bf16[2,136,128]{2,1,0:T(8,128)(2,1)S(1)}, u32[]{:S(2)}, u32[]{:S(2)}) collective-permute-start(bf16[2,136,128]{2,1,0:T(8,128)(2,1)S(1)} %get-tuple-element.33), channel_id=1, source_target_pairs={{32,0},{64,32},{96,64},{33,1},{65,33},{97,65},{34,2},{66,34},{98,6... | collective-permute-start | bytes 208904 | tf_op jit(solution)/shard_map/ppermute | solution.py:546

commit v7 on v6

--- a/solution.py
+++ b/solution.py
@@ -32,7 +32,7 @@
     return 0.5 * x * (1.0 + jnp.tanh(GELU_A * (x + GELU_B * (x * x * x))))
 
 
-def pack_kernel(values_ref, cells_ref, counts_ref, out_ref, held_ref, where_ref, live_ref, meta_ref, sem):
+def pack_kernel(values_ref, cells_ref, counts_ref, out_ref, held_ref, where_ref, live_ref, meta_ref, tail_ref, sem):
     owners, slots = values_ref.shape[0], values_ref.shape[1]
     part = owners // CHUNKS
     numbers = pltpu.make_async_copy(cells_ref, where_ref, sem.at[2 * CHUNKS])
@@ -43,10 +43,17 @@
     for n in range(CHUNKS):
         here = pl.ds(n * part, part)
         arrive.append(
-            pltpu.make_async_copy(values_ref.at[here], held_ref.at[here, pl.ds(0, slots), :], sem.at[n])
+            pltpu.make_async_copy(values_ref.at[here], held_ref.at[here], sem.at[n])
         )
-        leave.append(pltpu.make_async_copy(held_ref.at[here], out_ref.at[here], sem.at[CHUNKS + n]))
+        leave.append(
+            pltpu.make_async_copy(
+                held_ref.at[here], out_ref.at[here, pl.ds(0, slots), :], sem.at[CHUNKS + n]
+            )
+        )
         arrive[-1].start()
+    for came, goes in zip(arrive, leave):
+        came.wait()
+        goes.start()
     numbers.wait()
     totals.wait()
     cells = where_ref[...]
@@ -71,11 +78,10 @@
     meta_ref[pl.ds(2, owners, stride=META), :] = turned(again)
     for m in range(3, META):
         meta_ref[pl.ds(m, owners, stride=META), :] = jnp.zeros((owners, 128), jnp.float32)
-    held_ref[:, pl.ds(slots, META), :] = meta_ref[...].reshape(owners, META, 128).astype(jnp.bfloat16)
-    for came, goes in zip(arrive, leave):
-        came.wait()
-        goes.start()
-    for goes in leave:
+    tail_ref[...] = meta_ref[...].reshape(owners, META, 128).astype(jnp.bfloat16)
+    last = pltpu.make_async_copy(tail_ref, out_ref.at[:, pl.ds(slots, META), :], sem.at[2 * CHUNKS + 2])
+    last.start()
+    for goes in (*leave, last):
         goes.wait()
 
 
@@ -87,11 +93,12 @@
         in_specs=[ANY] * 3,
         out_specs=ANY,
         scratch_shapes=[
-            pltpu.VMEM((owners, slots + META, chans), jnp.bfloat16),
+            pltpu.VMEM((owners, slots, chans), jnp.bfloat16),
             pltpu.VMEM((slots, owners), jnp.int32),
             pltpu.VMEM((1, owners), jnp.int32),
             pltpu.VMEM((owners * META, chans), jnp.float32),
-            pltpu.SemaphoreType.DMA((2 * CHUNKS + 2,)),
+            pltpu.VMEM((owners, META, chans), jnp.bfloat16),
+            pltpu.SemaphoreType.DMA((2 * CHUNKS + 3,)),
         ],
         compiler_params=pltpu.CompilerParams(vmem_limit_bytes=12 << 20),
         name="pack",
@@ -120,9 +127,9 @@
     )(field)
 
 
-def scatter_kernel(band_ref, got_ref, parted_ref, acc_ref, right_ref, left_ref, near_ref, rows_ref, *rest):
+def scatter_kernel(place_ref, got_ref, parted_ref, acc_ref, right_ref, left_ref, near_ref, rows_ref, *rest):
     other_ref, start_ref, wide_ref, meta_ref, index_ref, late_ref, cells0_ref, cells1_ref, list_ref, sem = rest
-    del band_ref
+    del place_ref
     sources, slots = got_ref.shape[0], got_ref.shape[1] - META
     part = 128 // CHUNKS
     pieces = []
@@ -257,7 +264,7 @@
         rows_ref[n, pl.ds(64, 64), :] = acc_ref[pl.ds(base + EVEN, 64), :].astype(bf16)
 
 
-def scatter(band, got, start):
+def scatter(place, got, start):
     return pl.pallas_call(
         scatter_kernel,
         out_shape=[
@@ -283,22 +290,26 @@
         ],
         compiler_params=pltpu.CompilerParams(vmem_limit_bytes=24 << 20),
         name="scatter",
-    )(band, on_chip(got), off_chip(start))
-
-
-def frame_kernel(after_ref, rows_ref, west_ref, east_ref, down_ref, up_ref, all_ref):
+    )(place, on_chip(got), off_chip(start))
+
+
+def frame_kernel(place_ref, after_ref, rows_ref, west_ref, east_ref, round_ref, back_ref, own_ref):
     del after_ref
     f32, bf16 = jnp.float32, jnp.bfloat16
     west = west_ref[pl.ds(256, 8), :].astype(f32)
     east = east_ref[pl.ds(128, 8), :].astype(f32)
     for n in range(4):
         tail = jnp.concatenate([west[2 * n : 2 * n + 2], east[n : n + 1], jnp.zeros((5, 128), f32)], axis=0)
-        for ref, at in ((all_ref, n), (up_ref, n) if n < 2 else (down_ref, n - 2)):
-            ref[at, pl.ds(0, 128), :] = rows_ref[n]
-            ref[at, pl.ds(128, 8), :] = tail.astype(bf16)
-
-
-def frame(after, rows, west, east):
+        own_ref[n, pl.ds(0, 128), :] = rows_ref[n]
+        own_ref[n, pl.ds(128, 8), :] = tail.astype(bf16)
+    descends = place_ref[1] < place_ref[2]
+    for n in range(2):
+        top, bottom = own_ref[n].astype(f32), own_ref[n + 2].astype(f32)
+        round_ref[n] = jnp.where(descends, bottom, top).astype(bf16)
+        back_ref[n] = jnp.where(descends, top, bottom).astype(bf16)
+
+
+def frame(place, after, rows, west, east):
     return pl.pallas_call(
         frame_kernel,
         out_shape=[
@@ -306,11 +317,11 @@
             jax.ShapeDtypeStruct((2, 136, 128), jnp.bfloat16),
             jax.ShapeDtypeStruct((4, 136, 128), jnp.bfloat16),
         ],
-        in_specs=[ANY] + [VMEM] * 3,
+        in_specs=[SMEM, ANY] + [VMEM] * 3,
         out_specs=[VMEM] * 3,
         compiler_params=pltpu.CompilerParams(vmem_limit_bytes=4 << 20),
         name="frame",
-    )(after, rows, west, east)
+    )(place, after, rows, west, east)
 
 
 def inner_kernel(low, field_ref, w1_ref, b1_ref, even_ref, odd_ref, edge_ref, lhs_ref, shift_ref, tail_ref):
@@ -358,7 +369,7 @@
 
 
 def rim_kernel(
-    band_ref,
+    place_ref,
     even0_in,
     odd0_in,
     even1_in,
@@ -371,9 +382,8 @@
     west_ref,
     east_ref,
     own_ref,
-    down_ref,
-    up_ref,
-    across_ref,
+    round_ref,
+    back_ref,
     w1_ref,
     w1s_ref,
     b1_ref,
@@ -393,8 +403,8 @@
 ):
     del even0_in, odd0_in, even1_in, odd1_in
     f32, bf16 = jnp.float32, jnp.bfloat16
-    band = band_ref[0]
-    north, south = band == 0, band == 3
+    north, south = place_ref[0] == 0, place_ref[0] == 3
+    descends = place_ref[1] < place_ref[2]
     dot = functools.partial(jnp.dot, preferred_element_type=f32)
     bias = b1_ref[...]
     bias2 = jnp.concatenate([bias, bias], axis=-1)
@@ -417,10 +427,12 @@
     def wide(ref, n):
         return ref[n].astype(f32)
 
-    second = jnp.where(north, wide(across_ref, 1), wide(down_ref, 0))
-    first = jnp.where(north, wide(across_ref, 0), wide(down_ref, 1))
+    above = [jnp.where(descends, wide(round_ref, n), wide(back_ref, n)) for n in range(2)]
+    beneath = [jnp.where(descends, wide(back_ref, n), wide(round_ref, n)) for n in range(2)]
+    second = jnp.where(north, above[1], above[0])
+    first = jnp.where(north, above[0], above[1])
     own = [wide(own_ref, n) for n in range(4)]
-    below = jnp.where(south, wide(across_ref, 3), wide(up_ref, 0))
+    below = jnp.where(south, beneath[1], beneath[0])
     top = (jnp.where(north, own[0], second), first, jnp.where(north, second, own[0]))
     for slab, row in ((0, second), (1, first), (130, below)):
         for m, at in enumerate((128, 129, 64, 0, 127, 63, 130)):
@@ -500,11 +512,11 @@
         lax.fori_loop(0, 4, finish, 0)
 
 
-def rim(band, blocks, *rest):
+def rim(place, blocks, *rest):
     return pl.pallas_call(
         rim_kernel,
         out_shape=[pltpu.VMEM(b.shape, b.dtype) for b in blocks] + [jax.ShapeDtypeStruct((64, 64, 128), jnp.bfloat16)],
-        in_specs=[SMEM] + [VMEM] * 20,
+        in_specs=[SMEM] + [VMEM] * 19,
         out_specs=[VMEM] * 5,
         scratch_shapes=[
             pltpu.VMEM((7, 144, 128), jnp.float32),
@@ -517,21 +529,24 @@
         input_output_aliases={1: 0, 2: 1, 3: 2, 4: 3},
         compiler_params=pltpu.CompilerParams(vmem_limit_bytes=20 << 20),
         name="rim",
-    )(band, *map(on_chip, blocks), *rest)[4]
+    )(place, *map(on_chip, blocks), *rest)[4]
 
 
 def shards(background, values, cells, counts, w1, b1, w2, b2):
     lat, lon = lax.axis_size("lat"), lax.axis_size("lon")
-    band = lax.axis_index("lat")[None]
+    half = lon // 2
+    place = jnp.stack([lax.axis_index("lat"), lax.axis_index("lon"), jnp.int32(half)])
     east_pairs = [(i, (i + 1) % lon) for i in range(lon)]
     west_pairs = [(j, i) for i, j in east_pairs]
-    down_pairs = [(i, i + 1) for i in range(lat - 1)]
-    up_pairs = [(j, i) for i, j in down_pairs]
-    pole_pairs = [(b * lon + i, b * lon + (i + lon // 2) % lon) for b in (0, lat - 1) for i in range(lon)]
+    round_pairs = []
+    for i in range(half):
+        circle = [b * lon + i for b in range(lat)] + [b * lon + i + half for b in reversed(range(lat))]
+        round_pairs += zip(circle, circle[1:] + circle[:1])
+    back_pairs = [(j, i) for i, j in round_pairs]
 
     sent = pack(values[0], cells[0].T, counts)
     got = lax.all_to_all(sent, ("lat", "lon"), split_axis=0, concat_axis=0, tiled=True)
-    field, right, left, near, rows = scatter(band, got, spread(background))
+    field, right, left, near, rows = scatter(place, got, spread(background))
 
     flat = w1.reshape(3, 384, 128)
     blank = jnp.zeros((3, 128, 128), jnp.bfloat16)
@@ -541,13 +556,12 @@
     west = lax.ppermute(right, "lon", east_pairs)
     east = lax.ppermute(left, "lon", west_pairs)
     *upper, upper_edge = inner(0, field, paired, b1[None])
-    lower_rows, upper_rows, own = frame(upper_edge, rows, west, east)
-    down = lax.ppermute(lower_rows, "lat", down_pairs)
-    up = lax.ppermute(upper_rows, "lat", up_pairs)
-    across = lax.ppermute(own, ("lat", "lon"), pole_pairs)
+    ahead, behind, own = frame(place, upper_edge, rows, west, east)
+    ahead = lax.ppermute(ahead, ("lat", "lon"), round_pairs)
+    behind = lax.ppermute(behind, ("lat", "lon"), back_pairs)
     *lower, lower_edge = inner(64, field, paired, b1[None])
     return rim(
-        band,
+        place,
         (*upper, *lower),
         upper_edge,
         lower_edge,
@@ -557,9 +571,8 @@
         west,
         east,
         own,
-        down,
-        up,
-        across,
+        ahead,
+        behind,
         paired,
         flat,
         b1[None],

time: 104 us -> 102 us (0.981)
  starting transfers between devices: 24.1 us -> 20.3 us
  Pallas kernels: 38.5 us -> 39.7 us
    ppermute x3 -> x2, starting transfers between devices: 6.88 us -> 3.07 us  [the longest x1 3.07 us: shards(): ahead = lax.ppermute(ahead, ('lat', 'lon'), round_pairs)]
  transfers between devices with their start and end apart: 6 -> 5, of which waited for: 1 -> 1; matrix products, arithmetic and copies ran while one was open for 0% -> 0% of each run, Pallas kernels for 14% -> 14%
where the time goes in v7:
time: 102 us; the launch traced here: 101 us
  Pallas kernels  39.7 us (39%)
  waiting for transfers between devices  38.7 us (38%)
  starting transfers between devices  20.3 us (20%)
  local copies, waits for them, and re-layouts  2.2 us (2%)
    all_to_all x1, waiting for transfers between devices, shards(): lax.all_to_all(sent, ('lat', 'lon'), split_axis=0, concat_axis=0, tiled=T...  38.6 us
    pallas_call x1, Pallas kernels, scatter(): pl.pallas_call(scatter_kernel, out_shape=[pltpu.VMEM((SLABS * PITCH, 128)...  15.4 us
    all_to_all x1, starting transfers between devices, shards(): lax.all_to_all(sent, ('lat', 'lon'), split_axis=0, concat_axis=0, tiled=T...  11.5 us
    pallas_call x2, Pallas kernels, inner(): pl.pallas_call(functools.partial(inner_kernel, low), out_shape=[pltpu.VME...  10.3 us
    pallas_call x1, Pallas kernels, rim(): pl.pallas_call(rim_kernel, out_shape=[pltpu.VMEM(b.shape, b.dtype) for b...  6.51 us
    ppermute x1, starting transfers between devices, shards(): east = lax.ppermute(left, 'lon', west_pairs)  5.67 us
    pallas_call x1, Pallas kernels, spread(): pl.pallas_call(spread_kernel, out_shape=pltpu.HBM(field.shape, field.dtyp...  3.77 us
    ppermute x1, starting transfers between devices, shards(): ahead = lax.ppermute(ahead, ('lat', 'lon'), round_pairs)  3.07 us
  transfers between devices with their start and end apart: 5, of which 1 were waited for; matrix products, arithmetic and copies ran while one was open for 0% of the time, Pallas kernels for 14%

profile of v7, /device:TPU:1, one launch (start us, length us, event | category | flops | bytes accessed | tf_op | source)
XLA Modules:
  0.0 101.1 jit_solution(15612666788628057018)
XLA Ops:
  0.0 3.0 %pack.1 = bf16[128,104,128]{2,1,0:T(8,128)(2,1)} custom-call(bf16[128,96,128]{2,1,0:T(8,128)(2,1)} %bitcast.17, s32[96,128]{1,0:T(8,128)} %bitcast.18, s32[1,128]{1,0:T(1,128)} %counts_ref.1), custom_call_target="tpu_custom_call" | custom-call | tf_op jit(solution)/shard_map/pack/pallas_call | solution.py:90
  3.0 11.5 %all-to-all-start = ((bf16[128,104,128]{2,1,0:T(8,128)(2,1)}), bf16[128,104,128]{2,1,0:T(8,128)(2,1)S(1)}, u32[]{:S(2)}, u32[]{:S(2)}) async-start(bf16[128,104,128]{2,1,0:T(8,128)(2,1)} %pack.1), calls=%async_computation | async-start | bytes 6815744 | tf_op jit(solution)/shard_map/all_to_all | solution.py:548
  14.5 0.0 copy-start
  14.6 2.2 %copy-done = bf16[128,128,128]{2,1,0:T(8,128)(2,1)S(1)} copy-done((bf16[128,128,128]{2,1,0:T(8,128)(2,1)S(1)}, bf16[128,128,128]{2,1,0:T(8,128)(2,1)}, u32[]{:S(2)}) %copy-start) | copy-done | bytes 4194328
  16.7 3.8 %spread.1.parted_ref = bf16[128,128,128]{2,1,0:T(8,128)(2,1)} custom-call(bf16[128,128,128]{2,1,0:T(8,128)(2,1)S(1)} %copy-done), custom_call_target="tpu_custom_call" | custom-call | tf_op jit(solution)/shard_map/spread/pallas_call | solution.py:119
  20.5 0.1 pad_add_fusion.place_ref
  20.6 38.6 %all-to-all-done.got_ref = bf16[128,104,128]{2,1,0:T(8,128)(2,1)S(1)} async-done(((bf16[128,104,128]{2,1,0:T(8,128)(2,1)}), bf16[128,104,128]{2,1,0:T(8,128)(2,1)S(1)}, u32[]{:S(2)}, u32[]{:S(2)}) %all-to-all-start) | async-done | bytes 3407904 | tf_op jit(solution)/shard_map/all_to_all | solution.py:548
  59.2 15.4 %scatter.1 = (f32[19912,128]{1,0:T(8,128)S(1)}, bf16[264,128]{1,0:T(8,128)(2,1)S(1)}, bf16[136,128]{1,0:T(8,128)(2,1)S(1)}, bf16[128,128]{1,0:T(8,128)(2,1)S(1)}, bf16[4,128,128]{2,1,0:T(8,128)(2,1)S(1)}) custom-call(s32[3]{0:T(128)S(1)} %pad_add_fusion.place_ref, bf16[128,104,128]{2,1,0:T(8,128)(2,1)S(1)} %all-to-all-done.got_ref, ...), custom_call_target="tpu_custom_call" | custom-call | tf_op jit(solution)/shard_map/scatter/pallas_call | solution.py:268
  74.6 0.1 collective-permute-start
  74.7 5.7 %collective-permute-start.1 = (bf16[136,128]{1,0:T(8,128)(2,1)S(1)}, bf16[136,128]{1,0:T(8,128)(2,1)S(1)}, u32[]{:S(2)}, u32[]{:S(2)}) collective-permute-start(bf16[136,128]{1,0:T(8,128)(2,1)S(1)} %get-tuple-element.28.left_ref), channel_id=1, source_target_pairs={{1,0},{2,1},{3,2},{4,3},{5,4},{6,5},{7,6},{8,7},{9,8},{10,9},{11,1... | collective-permute-start | bytes 104456 | tf_op jit(solution)/shard_map/ppermute | solution.py:557
  80.4 0.0 copy-done.1
  80.4 0.1 fusion.2.w1_ref
  80.5 0.0 copy-done.3
  80.5 5.2 %inner.2 = (bf16[32,64,384]{2,1,0:T(8,128)(2,1)S(1)}, bf16[33,64,384]{2,1,0:T(8,128)(2,1)S(1)}, f32[3,64,128]{2,1,0:T(8,128)S(1)}) custom-call(f32[19912,128]{1,0:T(8,128)S(1)} %get-tuple-element.20.field_ref, bf16[3,512,256]{2,1,0:T(8,128)(2,1)S(1)} %fusion.2.w1_ref, f32[1,128]{1,0:T(1,128)S(1)} %bitcast.13), custom_call_target="tpu_custom_call" | custom-call | tf_op jit(solution)/shard_map/inner/pallas_call | solution.py:356
  85.7 0.0 collective-permute-done.1.east_ref
  85.7 0.0 collective-permute-done.west_ref
  85.7 0.6 frame.1
  86.3 3.1 %collective-permute-start.2 = (bf16[2,136,128]{2,1,0:T(8,128)(2,1)S(1)}, bf16[2,136,128]{2,1,0:T(8,128)(2,1)S(1)}, u32[]{:S(2)}, u32[]{:S(2)}) collective-permute-start(bf16[2,136,128]{2,1,0:T(8,128)(2,1)S(1)} %get-tuple-element.32), channel_id=1, source_target_pairs={{0,32},{32,64},{64,96},{96,112},{112,80},{80,48},{48,16},{16,0},{1... | collective-permute-start | bytes 208904 | tf_op jit(solution)/shard_map/ppermute | solution.py:560
  89.3 0.0 collective-permute-start.3
  89.3 5.2 %inner.3 = (bf16[32,64,384]{2,1,0:T(8,128)(2,1)S(1)}, bf16[33,64,384]{2,1,0:T(8,128)(2,1)S(1)}, f32[3,64,128]{2,1,0:T(8,128)S(1)}) custom-call(f32[19912,128]{1,0:T(8,128)S(1)} %get-tuple-element.20.field_ref, bf16[3,512,256]{2,1,0:T(8,128)(2,1)S(1)} %fusion.2.w1_ref, f32[1,128]{1,0:T(1,128)S(1)} %bitcast.14), custom_call_target="tpu_custom_call" | custom-call | tf_op jit(solution)/shard_map/inner/pallas_call | solution.py:356
  94.5 0.0 collective-permute-done.2.round_ref
  94.5 0.0 collective-permute-done.3.back_ref
  94.6 0.0 copy-done.2
  94.6 6.5 %rim.1 = (bf16[32,64,384]{2,1,0:T(8,128)(2,1)S(1)}, bf16[33,64,384]{2,1,0:T(8,128)(2,1)S(1)}, bf16[32,64,384]{2,1,0:T(8,128)(2,1)S(1)}, bf16[33,64,384]{2,1,0:T(8,128)(2,1)S(1)}, bf16[64,64,128]{2,1,0:T(8,128)(2,1)}) custom-call(s32[3]{0:T(128)S(1)} %pad_add_fusion.place_ref, ...), custom_call_target="tpu_custom_call", output_to_operand_aliasing={{0}: (1, {}), {1}: (2, {}), {2}: (3, {}), {3}: (4, {})} | custom-call | tf_op jit(solution)/shard_map/rim/pallas_call | solution.py:516
  (5 shorter events, 0.0 us)
Async XLA Ops:
  3.0 56.2 %all-to-all-start = ((bf16[128,104,128]{2,1,0:T(8,128)(2,1)}), bf16[128,104,128]{2,1,0:T(8,128)(2,1)S(1)}, u32[]{:S(2)}, u32[]{:S(2)}) async-start(bf16[128,104,128]{2,1,0:T(8,128)(2,1)} %pack.1), calls=%async_computation | async-start | bytes 6815744 | tf_op jit(solution)/shard_map/all_to_all | solution.py:548
  14.5 2.2 %copy-start = (bf16[128,128,128]{2,1,0:T(8,128)(2,1)S(1)}, bf16[128,128,128]{2,1,0:T(8,128)(2,1)}, u32[]{:S(2)}) copy-start(bf16[128,128,128]{2,1,0:T(8,128)(2,1)} %field_ref.1) | copy-start | bytes 12582916
  20.6 59.9 %copy-start.3 = (f32[128]{0:T(128)S(1)}, f32[128]{0:T(128)}, u32[]{:S(2)}) copy-start(f32[128]{0:T(128)} %param.13) | copy-start | bytes 1540
  59.2 21.2 %copy-start.1 = (bf16[3,3,128,128]{3,2,1,0:T(8,128)(2,1)S(1)}, bf16[3,3,128,128]{3,2,1,0:T(8,128)(2,1)}, u32[]{:S(2)}) copy-start(bf16[3,3,128,128]{3,2,1,0:T(8,128)(2,1)} %param.12) | copy-start | bytes 884740
  74.6 11.0 %collective-permute-start = (bf16[264,128]{1,0:T(8,128)(2,1)S(1)}, bf16[264,128]{1,0:T(8,128)(2,1)S(1)}, u32[]{:S(2)}, u32[]{:S(2)}) collective-permute-start(bf16[264,128]{1,0:T(8,128)(2,1)S(1)} %get-tuple-element.27.right_ref), channel_id=1, source_target_pairs={{0,1},{1,2},{2,3},{3,4},{4,5},{5,6},{6,7},{7,8},{8,9},{9,10},{10,1... | collective-permute-start | bytes 202760 | tf_op jit(solution)/shard_map/ppermute | solution.py:556
  74.7 10.9 %collective-permute-start.1 = (bf16[136,128]{1,0:T(8,128)(2,1)S(1)}, bf16[136,128]{1,0:T(8,128)(2,1)S(1)}, u32[]{:S(2)}, u32[]{:S(2)}) collective-permute-start(bf16[136,128]{1,0:T(8,128)(2,1)S(1)} %get-tuple-element.28.left_ref), channel_id=1, source_target_pairs={{1,0},{2,1},{3,2},{4,3},{5,4},{6,5},{7,6},{8,7},{9,8},{10,9},{11,1... | collective-permute-start | bytes 104456 | tf_op jit(solution)/shard_map/ppermute | solution.py:557
  86.3 8.3 %collective-permute-start.2 = (bf16[2,136,128]{2,1,0:T(8,128)(2,1)S(1)}, bf16[2,136,128]{2,1,0:T(8,128)(2,1)S(1)}, u32[]{:S(2)}, u32[]{:S(2)}) collective-permute-start(bf16[2,136,128]{2,1,0:T(8,128)(2,1)S(1)} %get-tuple-element.32), channel_id=1, source_target_pairs={{0,32},{32,64},{64,96},{96,112},{112,80},{80,48},{48,16},{16,0},{1... | collective-permute-start | bytes 208904 | tf_op jit(solution)/shard_map/ppermute | solution.py:560
  89.3 5.2 %copy-start.2 = (bf16[3,3,128,128]{3,2,1,0:T(8,128)(2,1)S(1)}, bf16[3,3,128,128]{3,2,1,0:T(8,128)(2,1)}, u32[]{:S(2)}) copy-start(bf16[3,3,128,128]{3,2,1,0:T(8,128)(2,1)} %param.14) | copy-start | bytes 884740
  89.3 5.2 %copy-start.4 = (f32[128]{0:T(128)S(1)}, f32[128]{0:T(128)}, u32[]{:S(2)}) copy-start(f32[128]{0:T(128)} %param.15) | copy-start | bytes 1540
  89.3 5.2 %collective-permute-start.3 = (bf16[2,136,128]{2,1,0:T(8,128)(2,1)S(1)}, bf16[2,136,128]{2,1,0:T(8,128)(2,1)S(1)}, u32[]{:S(2)}, u32[]{:S(2)}) collective-permute-start(bf16[2,136,128]{2,1,0:T(8,128)(2,1)S(1)} %get-tuple-element.33), channel_id=1, source_target_pairs={{32,0},{64,32},{96,64},{112,96},{80,112},{48,80},{16,48},{0,16},{3... | collective-permute-start | bytes 208904 | tf_op jit(solution)/shard_map/ppermute | solution.py:561

commit v8 on v7

--- a/solution.py
+++ b/solution.py
@@ -68,14 +68,18 @@
     for back in range(1, BATCH):
         same = (pltpu.roll(marked, back, 0) == marked) & live & (place % BATCH >= back)
         again = jnp.where(same, 1, again)
+    again = again.astype(jnp.float32)
+    count = jnp.sum(again, axis=0, keepdims=True)
+    furthest = jnp.max(again * place.astype(jnp.float32), axis=0, keepdims=True)
     blank = jnp.zeros((128 - slots, owners), jnp.float32)
-
-    def turned(x):
-        return jnp.concatenate([x.astype(jnp.float32), blank], axis=0).T
-
-    meta_ref[pl.ds(0, owners, stride=META), :] = turned(high)
-    meta_ref[pl.ds(1, owners, stride=META), :] = turned(low)
-    meta_ref[pl.ds(2, owners, stride=META), :] = turned(again)
+    notes = jnp.concatenate([count, furthest, count, blank[3:]], axis=0)
+
+    def turned(x, spare):
+        return jnp.concatenate([x.astype(jnp.float32), spare], axis=0).T
+
+    meta_ref[pl.ds(0, owners, stride=META), :] = turned(high, blank)
+    meta_ref[pl.ds(1, owners, stride=META), :] = turned(low, blank)
+    meta_ref[pl.ds(2, owners, stride=META), :] = turned(again, notes)
     for m in range(3, META):
         meta_ref[pl.ds(m, owners, stride=META), :] = jnp.zeros((owners, 128), jnp.float32)
     tail_ref[...] = meta_ref[...].reshape(owners, META, 128).astype(jnp.bfloat16)
@@ -127,8 +131,8 @@
     )(field)
 
 
-def scatter_kernel(place_ref, got_ref, parted_ref, acc_ref, right_ref, left_ref, near_ref, rows_ref, *rest):
-    other_ref, start_ref, wide_ref, meta_ref, index_ref, late_ref, cells0_ref, cells1_ref, list_ref, sem = rest
+def scatter_kernel(place_ref, got_ref, parted_ref, acc_ref, other_ref, right_ref, left_ref, near_ref, rows_ref, *rest):
+    start_ref, wide_ref, meta_ref, index_ref, late_ref, cells0_ref, cells1_ref, list_ref, sem = rest
     del place_ref
     sources, slots = got_ref.shape[0], got_ref.shape[1] - META
     part = 128 // CHUNKS
@@ -149,13 +153,9 @@
     spot = high * PITCH + low
     index_ref[...] = jnp.where(again > 0, 0.0, spot).astype(jnp.int32)
     lane = lax.broadcasted_iota(jnp.int32, again.shape, 1)
-    inside = lane < slots
-    count = jnp.sum(jnp.where(inside, again, 0.0), axis=1, keepdims=True)
-    furthest = jnp.max(jnp.where(inside & (again > 0), lane, 0).astype(jnp.float32), axis=1, keepdims=True)
-    crowd = jnp.sum(count.reshape(sources // GROUP, GROUP, 1), axis=1, keepdims=True)
+    crowd = jnp.sum(again.reshape(sources // GROUP, GROUP, 128), axis=1, keepdims=True)
     crowd = jnp.broadcast_to(crowd, (sources // GROUP, GROUP, 128)).reshape(sources, 128)
-    notes = jnp.where(lane == slots, count, jnp.where(lane == slots + 1, furthest, crowd))
-    late = jnp.where(inside, again * spot, notes)
+    late = jnp.where(lane < slots, again * spot, jnp.where(lane == slots + 2, crowd, again))
     late_ref[...] = late.astype(jnp.int32)
 
     cells = (cells0_ref, cells1_ref)
@@ -170,8 +170,8 @@
 
     def clear(r, carry):
         base = pl.multiple_of((r + 2) * PITCH, 8)
-        for at in (ODD, EVEN):
-            other_ref[pl.ds(base + at, 64), :] = jnp.zeros((64, 128), jnp.float32)
+        for at, size in ((0, 72), (EVEN, 72)):
+            other_ref[pl.ds(base + at, size), :] = jnp.zeros((size, 128), jnp.float32)
         return carry
 
     lax.fori_loop(0, 128, clear, 0)
@@ -240,34 +240,31 @@
             lax.fori_loop(group * GROUP, (group + 1) * GROUP, rest_of, 0)
 
 
-    def merge(r, carry):
-        base = pl.multiple_of((r + 2) * PITCH, 8)
-        for at in (ODD, EVEN):
-            here = pl.ds(base + at, 64)
-            acc_ref[here, :] = acc_ref[here, :] + other_ref[here, :]
-        return carry
-
-    lax.fori_loop(0, 128, merge, 0)
+    def total(start, size, stride=1):
+        here = pl.ds(start, size) if stride == 1 else pl.ds(start, size, stride=stride)
+        return acc_ref[here, :] + other_ref[here, :]
+
     bf16 = jnp.bfloat16
     ends = (0, 1, 126, 127)
     for n, at in enumerate((EVEN + 63, ODD + 63)):
-        right_ref[pl.ds(n * 128, 128), :] = acc_ref[pl.ds(2 * PITCH + at, 128, stride=PITCH), :].astype(bf16)
-    left_ref[pl.ds(0, 128), :] = acc_ref[pl.ds(2 * PITCH + EVEN, 128, stride=PITCH), :].astype(bf16)
-    near_ref[...] = acc_ref[pl.ds(2 * PITCH + ODD, 128, stride=PITCH), :].astype(bf16)
-    east = [acc_ref[pl.ds((r + 2) * PITCH + at, 1), :] for r in ends for at in (EVEN + 63, ODD + 63)]
-    west = [acc_ref[pl.ds((r + 2) * PITCH + EVEN, 1), :] for r in ends]
+        right_ref[pl.ds(n * 128, 128), :] = total(2 * PITCH + at, 128, PITCH).astype(bf16)
+    left_ref[pl.ds(0, 128), :] = total(2 * PITCH + EVEN, 128, PITCH).astype(bf16)
+    near_ref[...] = total(2 * PITCH + ODD, 128, PITCH).astype(bf16)
+    east = [total((r + 2) * PITCH + at, 1) for r in ends for at in (EVEN + 63, ODD + 63)]
+    west = [total((r + 2) * PITCH + EVEN, 1) for r in ends]
     right_ref[pl.ds(256, 8), :] = jnp.concatenate(east, axis=0).astype(bf16)
     left_ref[pl.ds(128, 8), :] = jnp.concatenate(west + west, axis=0).astype(bf16)
     for n, r in enumerate(ends):
         base = (r + 2) * PITCH
-        rows_ref[n, pl.ds(0, 64), :] = acc_ref[pl.ds(base + ODD, 64), :].astype(bf16)
-        rows_ref[n, pl.ds(64, 64), :] = acc_ref[pl.ds(base + EVEN, 64), :].astype(bf16)
+        rows_ref[n, pl.ds(0, 64), :] = total(base + ODD, 64).astype(bf16)
+        rows_ref[n, pl.ds(64, 64), :] = total(base + EVEN, 64).astype(bf16)
 
 
 def scatter(place, got, start):
     return pl.pallas_call(
         scatter_kernel,
         out_shape=[
+            pltpu.VMEM((SLABS * PITCH, 128), jnp.float32),
             pltpu.VMEM((SLABS * PITCH, 128), jnp.float32),
             jax.ShapeDtypeStruct((264, 128), jnp.bfloat16),
             jax.ShapeDtypeStruct((136, 128), jnp.bfloat16),
@@ -275,9 +272,8 @@
             jax.ShapeDtypeStruct((4, 128, 128), jnp.bfloat16),
         ],
         in_specs=[SMEM, VMEM, ANY],
-        out_specs=[VMEM] * 5,
+        out_specs=[VMEM] * 6,
         scratch_shapes=[
-            pltpu.VMEM((130 * PITCH, 128), jnp.float32),
             pltpu.VMEM((128, 128, 128), jnp.bfloat16),
             pltpu.VMEM((2, 96, 128), jnp.float32),
             pltpu.VMEM((128 * META, 128), jnp.float32),
@@ -288,7 +284,7 @@
             pltpu.SMEM((128, 128), jnp.int32),
             pltpu.SemaphoreType.DMA((3 + CHUNKS,)),
         ],
-        compiler_params=pltpu.CompilerParams(vmem_limit_bytes=24 << 20),
+        compiler_params=pltpu.CompilerParams(vmem_limit_bytes=16 << 20),
         name="scatter",
     )(place, on_chip(got), off_chip(start))
 
@@ -324,7 +320,7 @@
     )(place, after, rows, west, east)
 
 
-def inner_kernel(low, field_ref, w1_ref, b1_ref, even_ref, odd_ref, edge_ref, lhs_ref, shift_ref, tail_ref):
+def inner_kernel(low, field_ref, other_ref, w1_ref, b1_ref, even_ref, odd_ref, edge_ref, lhs_ref, shift_ref, tail_ref):
     f32, bf16 = jnp.float32, jnp.bfloat16
     bias = jnp.concatenate([b1_ref[...], b1_ref[...]], axis=-1)
     weight = w1_ref[...].reshape(1536, 256)
@@ -332,7 +328,8 @@
     def step(b, carry):
         for n in range(ROWS + 2):
             base = pl.multiple_of((low + 1 + b * ROWS + n) * PITCH, 8)
-            parts = [field_ref[pl.ds(base + at, 64), :].astype(bf16) for at in (ODD - 1, EVEN, ODD, EVEN + 1)]
+            spans = [pl.ds(base + at, 64) for at in (ODD - 1, EVEN, ODD, EVEN + 1)]
+            parts = [(field_ref[span, :] + other_ref[span, :]).astype(bf16) for span in spans]
             lhs_ref[n] = jnp.concatenate(parts, axis=-1)
         window = jnp.concatenate([lhs_ref[pl.ds(di, ROWS)].reshape(ROWS * 64, 512) for di in range(3)], axis=-1)
         hid = gelu(jnp.dot(window, weight, preferred_element_type=f32) + bias).reshape(ROWS, 64, 256)
@@ -352,7 +349,7 @@
     lax.fori_loop(0, 64 // ROWS, step, 0)
 
 
-def inner(low, field, w1, b1):
+def inner(low, field, other, w1, b1):
     return pl.pallas_call(
         functools.partial(inner_kernel, low),
         out_shape=[
@@ -360,12 +357,12 @@
             pltpu.VMEM((33, 64, 384), jnp.bfloat16),
             jax.ShapeDtypeStruct((3, 64, 128), jnp.float32),
         ],
-        in_specs=[VMEM] * 3,
+        in_specs=[VMEM] * 4,
         out_specs=[VMEM] * 3,
         scratch_shapes=[pltpu.VMEM((ROWS + 2, 64, 512), jnp.bfloat16), pltpu.VMEM((ROWS, 72, 128), jnp.float32), pltpu.VMEM((ROWS, 8, 128), jnp.float32)],
         compiler_params=pltpu.CompilerParams(vmem_limit_bytes=24 << 20),
         name="inner",
-    )(on_chip(field), w1, b1)
+    )(on_chip(field), on_chip(other), w1, b1)
 
 
 def rim_kernel(
@@ -546,7 +543,7 @@
 
     sent = pack(values[0], cells[0].T, counts)
     got = lax.all_to_all(sent, ("lat", "lon"), split_axis=0, concat_axis=0, tiled=True)
-    field, right, left, near, rows = scatter(place, got, spread(background))
+    field, other, right, left, near, rows = scatter(place, got, spread(background))
 
     flat = w1.reshape(3, 384, 128)
     blank = jnp.zeros((3, 128, 128), jnp.bfloat16)
@@ -555,11 +552,11 @@
     )
     west = lax.ppermute(right, "lon", east_pairs)
     east = lax.ppermute(left, "lon", west_pairs)
-    *upper, upper_edge = inner(0, field, paired, b1[None])
+    *upper, upper_edge = inner(0, field, other, paired, b1[None])
     ahead, behind, own = frame(place, upper_edge, rows, west, east)
     ahead = lax.ppermute(ahead, ("lat", "lon"), round_pairs)
     behind = lax.ppermute(behind, ("lat", "lon"), back_pairs)
-    *lower, lower_edge = inner(64, field, paired, b1[None])
+    *lower, lower_edge = inner(64, field, other, paired, b1[None])
     return rim(
         place,
         (*upper, *lower),

time: 102 us -> 101 us (level)
    pallas_call x1, Pallas kernels: 15.4 us -> 14.2 us  [scatter(): pl.pallas_call(scatter_kernel, out_shape=[pltpu.VMEM((SLABS * PITCH, 128)...]
  transfers between devices with their start and end apart: 5 -> 5, of which waited for: 1 -> 1; matrix products, arithmetic and copies ran while one was open for 0% -> 0% of each run, Pallas kernels for 14% -> 15%
where the time goes in v8:
time: 101 us; the launch traced here: 99.6 us
  Pallas kernels  39.1 us (39%)
  waiting for transfers between devices  38.6 us (38%)
  starting transfers between devices  19.4 us (19%)
  local copies, waits for them, and re-layouts  2.2 us (2%)
    all_to_all x1, waiting for transfers between devices, shards(): lax.all_to_all(sent, ('lat', 'lon'), split_axis=0, concat_axis=0, tiled=T...  38.6 us
    pallas_call x1, Pallas kernels, scatter(): pl.pallas_call(scatter_kernel, out_shape=[pltpu.VMEM((SLABS * PITCH, 128)...  14.2 us
    all_to_all x1, starting transfers between devices, shards(): lax.all_to_all(sent, ('lat', 'lon'), split_axis=0, concat_axis=0, tiled=T...  11.5 us
    pallas_call x2, Pallas kernels, inner(): pl.pallas_call(functools.partial(inner_kernel, low), out_shape=[pltpu.VME...  11 us
    pallas_call x1, Pallas kernels, rim(): pl.pallas_call(rim_kernel, out_shape=[pltpu.VMEM(b.shape, b.dtype) for b...  6.52 us
    ppermute x1, starting transfers between devices, shards(): east = lax.ppermute(left, 'lon', west_pairs)  5.67 us
    pallas_call x1, Pallas kernels, spread(): pl.pallas_call(spread_kernel, out_shape=pltpu.HBM(field.shape, field.dtyp...  3.77 us
    pallas_call x1, Pallas kernels, pack(): pl.pallas_call(pack_kernel, out_shape=pltpu.HBM((owners, slots + META, ch...  3.03 us
  transfers between devices with their start and end apart: 5, of which 1 were waited for; matrix products, arithmetic and copies ran while one was open for 0% of the time, Pallas kernels for 15%

profile of v8, /device:TPU:1, one launch (start us, length us, event | category | flops | bytes accessed | tf_op | source)
XLA Modules:
  0.0 99.6 jit_solution(289563395992003994)
XLA Ops:
  0.0 3.0 %pack.1 = bf16[128,104,128]{2,1,0:T(8,128)(2,1)} custom-call(bf16[128,96,128]{2,1,0:T(8,128)(2,1)} %bitcast.17, s32[96,128]{1,0:T(8,128)} %bitcast.18, s32[1,128]{1,0:T(1,128)} %counts_ref.1), custom_call_target="tpu_custom_call" | custom-call | tf_op jit(solution)/shard_map/pack/pallas_call | solution.py:94
  3.0 11.5 %all-to-all-start = ((bf16[128,104,128]{2,1,0:T(8,128)(2,1)}), bf16[128,104,128]{2,1,0:T(8,128)(2,1)S(1)}, u32[]{:S(2)}, u32[]{:S(2)}) async-start(bf16[128,104,128]{2,1,0:T(8,128)(2,1)} %pack.1), calls=%async_computation | async-start | bytes 6815744 | tf_op jit(solution)/shard_map/all_to_all | solution.py:545
  14.5 0.0 copy-start
  14.6 2.2 %copy-done = bf16[128,128,128]{2,1,0:T(8,128)(2,1)S(1)} copy-done((bf16[128,128,128]{2,1,0:T(8,128)(2,1)S(1)}, bf16[128,128,128]{2,1,0:T(8,128)(2,1)}, u32[]{:S(2)}) %copy-start) | copy-done | bytes 4194328
  16.7 3.8 %spread.1.parted_ref = bf16[128,128,128]{2,1,0:T(8,128)(2,1)} custom-call(bf16[128,128,128]{2,1,0:T(8,128)(2,1)S(1)} %copy-done), custom_call_target="tpu_custom_call" | custom-call | tf_op jit(solution)/shard_map/spread/pallas_call | solution.py:123
  20.5 0.1 pad_add_fusion.place_ref
  20.6 38.6 %all-to-all-done.got_ref = bf16[128,104,128]{2,1,0:T(8,128)(2,1)S(1)} async-done(((bf16[128,104,128]{2,1,0:T(8,128)(2,1)}), bf16[128,104,128]{2,1,0:T(8,128)(2,1)S(1)}, u32[]{:S(2)}, u32[]{:S(2)}) %all-to-all-start) | async-done | bytes 3407904 | tf_op jit(solution)/shard_map/all_to_all | solution.py:545
  59.2 14.2 %scatter.1 = (f32[19912,128]{1,0:T(8,128)S(1)}, f32[19912,128]{1,0:T(8,128)S(1)}, bf16[264,128]{1,0:T(8,128)(2,1)S(1)}, bf16[136,128]{1,0:T(8,128)(2,1)S(1)}, bf...) custom-call(s32[3]{0:T(128)S(1)} %pad_add_fusion.place_ref, ...), custom_call_target="tpu_custom_call" | custom-call | tf_op jit(solution)/shard_map/scatter/pallas_call | solution.py:264
  73.4 0.1 collective-permute-start
  73.5 5.7 %collective-permute-start.1 = (bf16[136,128]{1,0:T(8,128)(2,1)S(1)}, bf16[136,128]{1,0:T(8,128)(2,1)S(1)}, u32[]{:S(2)}, u32[]{:S(2)}) collective-permute-start(bf16[136,128]{1,0:T(8,128)(2,1)S(1)} %get-tuple-element.30.left_ref), channel_id=1, source_target_pairs={{1,0},{2,1},{3,2},{4,3},{5,4},{6,5},{7,6},{8,7},{9,8},{10,9},{11,1... | collective-permute-start | bytes 104456 | tf_op jit(solution)/shard_map/ppermute | solution.py:554
  79.1 0.0 copy-done.1
  79.1 0.1 fusion.2.w1_ref
  79.2 0.0 copy-done.3
  79.2 5.5 %inner.2 = (bf16[32,64,384]{2,1,0:T(8,128)(2,1)S(1)}, bf16[33,64,384]{2,1,0:T(8,128)(2,1)S(1)}, f32[3,64,128]{2,1,0:T(8,128)S(1)}) custom-call(f32[19912,128]{1,0:T(8,128)S(1)} %get-tuple-element.21.field_ref, f32[19912,128]{1,0:T(8,128)S(1)} %get-tuple-element.22.other_ref, bf16[3,512,256]{2,1,0:T(8,128)(2,1)S(1)} %fusion.2.w1_ref, f32[1,128]{1,0:T(1,128)S(1)} %bitcast.13), custom_call_target="tpu_custom_call" | custom-call | tf_op jit(solution)/shard_map/inner/pallas_call | solution.py:353
  84.8 0.0 collective-permute-done.1.east_ref
  84.8 0.0 collective-permute-done.west_ref
  84.8 0.6 frame.1
  85.4 2.1 %collective-permute-start.2 = (bf16[2,136,128]{2,1,0:T(8,128)(2,1)S(1)}, bf16[2,136,128]{2,1,0:T(8,128)(2,1)S(1)}, u32[]{:S(2)}, u32[]{:S(2)}) collective-permute-start(bf16[2,136,128]{2,1,0:T(8,128)(2,1)S(1)} %get-tuple-element.34), channel_id=1, source_target_pairs={{0,32},{32,64},{64,96},{96,112},{112,80},{80,48},{48,16},{16,0},{1... | collective-permute-start | bytes 208904 | tf_op jit(solution)/shard_map/ppermute | solution.py:557
  87.5 0.0 collective-permute-start.3
  87.5 5.5 %inner.3 = (bf16[32,64,384]{2,1,0:T(8,128)(2,1)S(1)}, bf16[33,64,384]{2,1,0:T(8,128)(2,1)S(1)}, f32[3,64,128]{2,1,0:T(8,128)S(1)}) custom-call(f32[19912,128]{1,0:T(8,128)S(1)} %get-tuple-element.21.field_ref, f32[19912,128]{1,0:T(8,128)S(1)} %get-tuple-element.22.other_ref, bf16[3,512,256]{2,1,0:T(8,128)(2,1)S(1)} %fusion.2.w1_ref, f32[1,128]{1,0:T(1,128)S(1)} %bitcast.14), custom_call_target="tpu_custom_call" | custom-call | tf_op jit(solution)/shard_map/inner/pallas_call | solution.py:353
  93.0 0.0 collective-permute-done.2.round_ref
  93.0 0.0 collective-permute-done.3.back_ref
  93.0 0.0 copy-done.2
  93.0 6.5 %rim.1 = (bf16[32,64,384]{2,1,0:T(8,128)(2,1)S(1)}, bf16[33,64,384]{2,1,0:T(8,128)(2,1)S(1)}, bf16[32,64,384]{2,1,0:T(8,128)(2,1)S(1)}, bf16[33,64,384]{2,1,0:T(8,128)(2,1)S(1)}, bf16[64,64,128]{2,1,0:T(8,128)(2,1)}) custom-call(s32[3]{0:T(128)S(1)} %pad_add_fusion.place_ref, ...), custom_call_target="tpu_custom_call", output_to_operand_aliasing={{0}: (1, {}), {1}: (2, {}), {2}: (3, {}), {3}: (4, {})} | custom-call | tf_op jit(solution)/shard_map/rim/pallas_call | solution.py:513
  (5 shorter events, 0.0 us)
Async XLA Ops:
  3.0 56.2 %all-to-all-start = ((bf16[128,104,128]{2,1,0:T(8,128)(2,1)}), bf16[128,104,128]{2,1,0:T(8,128)(2,1)S(1)}, u32[]{:S(2)}, u32[]{:S(2)}) async-start(bf16[128,104,128]{2,1,0:T(8,128)(2,1)} %pack.1), calls=%async_computation | async-start | bytes 6815744 | tf_op jit(solution)/shard_map/all_to_all | solution.py:545
  14.5 2.2 %copy-start = (bf16[128,128,128]{2,1,0:T(8,128)(2,1)S(1)}, bf16[128,128,128]{2,1,0:T(8,128)(2,1)}, u32[]{:S(2)}) copy-start(bf16[128,128,128]{2,1,0:T(8,128)(2,1)} %field_ref.1) | copy-start | bytes 12582916
  20.6 58.6 %copy-start.3 = (f32[128]{0:T(128)S(1)}, f32[128]{0:T(128)}, u32[]{:S(2)}) copy-start(f32[128]{0:T(128)} %param.13) | copy-start | bytes 1540
  59.2 19.9 %copy-start.1 = (bf16[3,3,128,128]{3,2,1,0:T(8,128)(2,1)S(1)}, bf16[3,3,128,128]{3,2,1,0:T(8,128)(2,1)}, u32[]{:S(2)}) copy-start(bf16[3,3,128,128]{3,2,1,0:T(8,128)(2,1)} %param.12) | copy-start | bytes 884740
  73.4 11.4 %collective-permute-start = (bf16[264,128]{1,0:T(8,128)(2,1)S(1)}, bf16[264,128]{1,0:T(8,128)(2,1)S(1)}, u32[]{:S(2)}, u32[]{:S(2)}) collective-permute-start(bf16[264,128]{1,0:T(8,128)(2,1)S(1)} %get-tuple-element.29.right_ref), channel_id=1, source_target_pairs={{0,1},{1,2},{2,3},{3,4},{4,5},{5,6},{6,7},{7,8},{8,9},{9,10},{10,1... | collective-permute-start | bytes 202760 | tf_op jit(solution)/shard_map/ppermute | solution.py:553
  73.5 11.3 %collective-permute-start.1 = (bf16[136,128]{1,0:T(8,128)(2,1)S(1)}, bf16[136,128]{1,0:T(8,128)(2,1)S(1)}, u32[]{:S(2)}, u32[]{:S(2)}) collective-permute-start(bf16[136,128]{1,0:T(8,128)(2,1)S(1)} %get-tuple-element.30.left_ref), channel_id=1, source_target_pairs={{1,0},{2,1},{3,2},{4,3},{5,4},{6,5},{7,6},{8,7},{9,8},{10,9},{11,1... | collective-permute-start | bytes 104456 | tf_op jit(solution)/shard_map/ppermute | solution.py:554
  85.4 7.6 %collective-permute-start.2 = (bf16[2,136,128]{2,1,0:T(8,128)(2,1)S(1)}, bf16[2,136,128]{2,1,0:T(8,128)(2,1)S(1)}, u32[]{:S(2)}, u32[]{:S(2)}) collective-permute-start(bf16[2,136,128]{2,1,0:T(8,128)(2,1)S(1)} %get-tuple-element.34), channel_id=1, source_target_pairs={{0,32},{32,64},{64,96},{96,112},{112,80},{80,48},{48,16},{16,0},{1... | collective-permute-start | bytes 208904 | tf_op jit(solution)/shard_map/ppermute | solution.py:557
  87.5 5.5 %copy-start.2 = (bf16[3,3,128,128]{3,2,1,0:T(8,128)(2,1)S(1)}, bf16[3,3,128,128]{3,2,1,0:T(8,128)(2,1)}, u32[]{:S(2)}) copy-start(bf16[3,3,128,128]{3,2,1,0:T(8,128)(2,1)} %param.14) | copy-start | bytes 884740
  87.5 5.6 %copy-start.4 = (f32[128]{0:T(128)S(1)}, f32[128]{0:T(128)}, u32[]{:S(2)}) copy-start(f32[128]{0:T(128)} %param.15) | copy-start | bytes 1540
  87.5 5.5 %collective-permute-start.3 = (bf16[2,136,128]{2,1,0:T(8,128)(2,1)S(1)}, bf16[2,136,128]{2,1,0:T(8,128)(2,1)S(1)}, u32[]{:S(2)}, u32[]{:S(2)}) collective-permute-start(bf16[2,136,128]{2,1,0:T(8,128)(2,1)S(1)} %get-tuple-element.35), channel_id=1, source_target_pairs={{32,0},{64,32},{96,64},{112,96},{80,112},{48,80},{16,48},{0,16},{3... | collective-permute-start | bytes 208904 | tf_op jit(solution)/shard_map/ppermute | solution.py:558

commit v9 on v8

--- a/solution.py
+++ b/solution.py
@@ -409,6 +409,20 @@
     taps1 = w1s_ref[...].reshape(1152, 128)
     taps2 = w2_ref[...].reshape(1152, 128)
 
+    def second_layer(b):
+        even_ref, odd_ref = ((even0_ref, odd0_ref), (even1_ref, odd1_ref))[b // 4]
+        p = b % 4 * 8
+        window = [
+            odd_ref[pl.ds(p, 8)].reshape(512, 384),
+            even_ref[pl.ds(p, 8)].reshape(512, 384),
+            odd_ref[pl.ds(p + 1, 8)].reshape(512, 384),
+        ]
+        total = dot(jnp.concatenate(window, axis=-1), taps2) + b2_ref[...]
+        total_ref[pl.ds(b * 8, 8)] = total.reshape(8, 64, 128)
+
+    odd1_ref[0] = odd0_ref[32]
+    second_layer(1)
+
     body = (
         west_ref[pl.ds(0, 128), :],
         west_ref[pl.ds(128, 128), :],
@@ -450,6 +464,7 @@
         corner.extend(jnp.broadcast_to(row[at : at + 1], (8, 128)) for at in (128, 129, 64))
     corner = jnp.concatenate(corner, axis=-1).astype(bf16)
     stack = [jnp.concatenate([lhs[n] for n in picks], axis=-1) for picks in ((0, 1, 2), (1, 3, 4), (5, 6, 7))]
+    second_layer(2)
     hid = gelu(dot(jnp.concatenate([*stack, corner, corner], axis=0), pairs) + bias2)
 
     windows = []
@@ -457,6 +472,7 @@
         parts = [cols_ref[at + m, pl.ds(di, 136), :] for di in range(3) for m in range(3)]
         windows.append(jnp.concatenate(parts, axis=-1))
     cols = gelu(dot(jnp.concatenate(windows, axis=0).astype(bf16), taps1) + bias)
+    second_layer(3)
     for n, to in enumerate((0, 1, 5)):
         side_ref[to] = cols[n * 136 : (n + 1) * 136]
     for n in range(3):
@@ -479,7 +495,7 @@
         else:
             odd1_ref[32] = line
     side_ref[0, pl.ds(0, 1), :] = hid[192:193, 128:]
-    odd1_ref[0] = odd0_ref[32]
+    second_layer(4)
 
     windows = []
     for at in (0, 3):
@@ -487,26 +503,16 @@
         windows.append(jnp.concatenate(parts, axis=-1))
     ends_ref[...] = dot(jnp.concatenate(windows, axis=0).astype(bf16), taps2) + b2_ref[...]
 
-    for half, (even_ref, odd_ref) in enumerate(((even0_ref, odd0_ref), (even1_ref, odd1_ref))):
-
-        def finish(b, carry):
-            p = b * 8
-            window = jnp.concatenate(
-                [
-                    odd_ref[pl.ds(p, 8)].reshape(512, 384),
-                    even_ref[pl.ds(p, 8)].reshape(512, 384),
-                    odd_ref[pl.ds(p + 1, 8)].reshape(512, 384),
-                ],
-                axis=-1,
-            )
-            total_ref[...] = (dot(window, taps2) + b2_ref[...]).reshape(8, 64, 128)
-            for n in range(8):
-                total_ref[n, pl.ds(0, 1), :] = ends_ref[pl.ds(half * 32 + p + n, 1), :]
-                total_ref[n, pl.ds(63, 1), :] = ends_ref[pl.ds(64 + half * 32 + p + n, 1), :]
-            out_ref[pl.ds(half * 32 + p, 8)] = total_ref[...].astype(bf16)
-            return carry
-
-        lax.fori_loop(0, 4, finish, 0)
+    for b in (5, 6, 0, 7):
+        second_layer(b)
+
+    def finish(p, carry):
+        total_ref[p, pl.ds(0, 1), :] = ends_ref[pl.ds(p, 1), :]
+        total_ref[p, pl.ds(63, 1), :] = ends_ref[pl.ds(64 + p, 1), :]
+        out_ref[p] = total_ref[p].astype(bf16)
+        return carry
+
+    lax.fori_loop(0, 64, finish, 0, unroll=8)
 
 
 def rim(place, blocks, *rest):
@@ -521,7 +527,7 @@
             pltpu.VMEM((72, 128), jnp.float32),
             pltpu.VMEM((6, 136, 128), jnp.float32),
             pltpu.VMEM((128, 128), jnp.float32),
-            pltpu.VMEM((8, 64, 128), jnp.float32),
+            pltpu.VMEM((64, 64, 128), jnp.float32),
         ],
         input_output_aliases={1: 0, 2: 1, 3: 2, 4: 3},
         compiler_params=pltpu.CompilerParams(vmem_limit_bytes=20 << 20),

time: 101 us -> 99.7 us (0.987)
  Pallas kernels: 39.1 us -> 37.3 us
    pallas_call x1, Pallas kernels: 6.52 us -> 4.95 us  [rim(): pl.pallas_call(rim_kernel, out_shape=[pltpu.VMEM(b.shape, b.dtype) for b...]
where the time goes in v9:
time: 99.7 us; the launch traced here: 98.5 us
  waiting for transfers between devices  38.6 us (39%)
  Pallas kernels  37.3 us (37%)
  starting transfers between devices  20 us (20%)
  local copies, waits for them, and re-layouts  2.2 us (2%)
    all_to_all x1, waiting for transfers between devices, shards(): lax.all_to_all(sent, ('lat', 'lon'), split_axis=0, concat_axis=0, tiled=T...  38.6 us
    pallas_call x1, Pallas kernels, scatter(): pl.pallas_call(scatter_kernel, out_shape=[pltpu.VMEM((SLABS * PITCH, 128)...  14 us
    all_to_all x1, starting transfers between devices, shards(): lax.all_to_all(sent, ('lat', 'lon'), split_axis=0, concat_axis=0, tiled=T...  11.5 us
    pallas_call x2, Pallas kernels, inner(): pl.pallas_call(functools.partial(inner_kernel, low), out_shape=[pltpu.VME...  11 us
    ppermute x1, starting transfers between devices, shards(): east = lax.ppermute(left, 'lon', west_pairs)  5.4 us
    pallas_call x1, Pallas kernels, rim(): pl.pallas_call(rim_kernel, out_shape=[pltpu.VMEM(b.shape, b.dtype) for b...  4.95 us
    pallas_call x1, Pallas kernels, spread(): pl.pallas_call(spread_kernel, out_shape=pltpu.HBM(field.shape, field.dtyp...  3.77 us
    pallas_call x1, Pallas kernels, pack(): pl.pallas_call(pack_kernel, out_shape=pltpu.HBM((owners, slots + META, ch...  3.03 us
  transfers between devices with their start and end apart: 5, of which 1 were waited for; matrix products, arithmetic and copies ran while one was open for 0% of the time, Pallas kernels for 15%

profile of v9, /device:TPU:1, one launch (start us, length us, event | category | flops | bytes accessed | tf_op | source)
XLA Modules:
  0.0 98.5 jit_solution(1291164750954874522)
XLA Ops:
  0.0 3.0 %pack.1 = bf16[128,104,128]{2,1,0:T(8,128)(2,1)} custom-call(bf16[128,96,128]{2,1,0:T(8,128)(2,1)} %bitcast.17, s32[96,128]{1,0:T(8,128)} %bitcast.18, s32[1,128]{1,0:T(1,128)} %counts_ref.1), custom_call_target="tpu_custom_call" | custom-call | tf_op jit(solution)/shard_map/pack/pallas_call | solution.py:94
  3.0 11.5 %all-to-all-start = ((bf16[128,104,128]{2,1,0:T(8,128)(2,1)}), bf16[128,104,128]{2,1,0:T(8,128)(2,1)S(1)}, u32[]{:S(2)}, u32[]{:S(2)}) async-start(bf16[128,104,128]{2,1,0:T(8,128)(2,1)} %pack.1), calls=%async_computation | async-start | bytes 6815744 | tf_op jit(solution)/shard_map/all_to_all | solution.py:551
  14.5 0.0 copy-start
  14.6 2.2 %copy-done = bf16[128,128,128]{2,1,0:T(8,128)(2,1)S(1)} copy-done((bf16[128,128,128]{2,1,0:T(8,128)(2,1)S(1)}, bf16[128,128,128]{2,1,0:T(8,128)(2,1)}, u32[]{:S(2)}) %copy-start) | copy-done | bytes 4194328
  16.7 3.8 %spread.1.parted_ref = bf16[128,128,128]{2,1,0:T(8,128)(2,1)} custom-call(bf16[128,128,128]{2,1,0:T(8,128)(2,1)S(1)} %copy-done), custom_call_target="tpu_custom_call" | custom-call | tf_op jit(solution)/shard_map/spread/pallas_call | solution.py:123
  20.5 0.1 pad_add_fusion.place_ref
  20.6 38.6 %all-to-all-done.got_ref = bf16[128,104,128]{2,1,0:T(8,128)(2,1)S(1)} async-done(((bf16[128,104,128]{2,1,0:T(8,128)(2,1)}), bf16[128,104,128]{2,1,0:T(8,128)(2,1)S(1)}, u32[]{:S(2)}, u32[]{:S(2)}) %all-to-all-start) | async-done | bytes 3407904 | tf_op jit(solution)/shard_map/all_to_all | solution.py:551
  59.2 14.0 %scatter.1 = (f32[19912,128]{1,0:T(8,128)S(1)}, f32[19912,128]{1,0:T(8,128)S(1)}, bf16[264,128]{1,0:T(8,128)(2,1)S(1)}, bf16[136,128]{1,0:T(8,128)(2,1)S(1)}, bf...) custom-call(s32[3]{0:T(128)S(1)} %pad_add_fusion.place_ref, ...), custom_call_target="tpu_custom_call" | custom-call | tf_op jit(solution)/shard_map/scatter/pallas_call | solution.py:264
  73.2 0.4 collective-permute-start
  73.5 5.4 %collective-permute-start.1 = (bf16[136,128]{1,0:T(8,128)(2,1)S(1)}, bf16[136,128]{1,0:T(8,128)(2,1)S(1)}, u32[]{:S(2)}, u32[]{:S(2)}) collective-permute-start(bf16[136,128]{1,0:T(8,128)(2,1)S(1)} %get-tuple-element.30.left_ref), channel_id=1, source_target_pairs={{1,0},{2,1},{3,2},{4,3},{5,4},{6,5},{7,6},{8,7},{9,8},{10,9},{11,1... | collective-permute-start | bytes 104456 | tf_op jit(solution)/shard_map/ppermute | solution.py:560
  78.9 0.0 copy-done.1
  78.9 0.1 fusion.2.w1_ref
  79.0 5.5 %inner.2 = (bf16[32,64,384]{2,1,0:T(8,128)(2,1)S(1)}, bf16[33,64,384]{2,1,0:T(8,128)(2,1)S(1)}, f32[3,64,128]{2,1,0:T(8,128)S(1)}) custom-call(f32[19912,128]{1,0:T(8,128)S(1)} %get-tuple-element.21.field_ref, f32[19912,128]{1,0:T(8,128)S(1)} %get-tuple-element.22.other_ref, bf16[3,512,256]{2,1,0:T(8,128)(2,1)S(1)} %fusion.2.w1_ref, f32[1,128]{1,0:T(1,128)S(1)} %bitcast.13), custom_call_target="tpu_custom_call" | custom-call | tf_op jit(solution)/shard_map/inner/pallas_call | solution.py:353
  84.6 0.0 collective-permute-done.1.east_ref
  84.6 0.0 collective-permute-done.west_ref
  84.6 0.6 frame.1
  85.2 2.8 %collective-permute-start.2 = (bf16[2,136,128]{2,1,0:T(8,128)(2,1)S(1)}, bf16[2,136,128]{2,1,0:T(8,128)(2,1)S(1)}, u32[]{:S(2)}, u32[]{:S(2)}) collective-permute-start(bf16[2,136,128]{2,1,0:T(8,128)(2,1)S(1)} %get-tuple-element.34), channel_id=1, source_target_pairs={{0,32},{32,64},{64,96},{96,112},{112,80},{80,48},{48,16},{16,0},{1... | collective-permute-start | bytes 208904 | tf_op jit(solution)/shard_map/ppermute | solution.py:563
  87.9 0.0 collective-permute-start.3
  88.0 5.5 %inner.3 = (bf16[32,64,384]{2,1,0:T(8,128)(2,1)S(1)}, bf16[33,64,384]{2,1,0:T(8,128)(2,1)S(1)}, f32[3,64,128]{2,1,0:T(8,128)S(1)}) custom-call(f32[19912,128]{1,0:T(8,128)S(1)} %get-tuple-element.21.field_ref, f32[19912,128]{1,0:T(8,128)S(1)} %get-tuple-element.22.other_ref, bf16[3,512,256]{2,1,0:T(8,128)(2,1)S(1)} %fusion.2.w1_ref, f32[1,128]{1,0:T(1,128)S(1)} %bitcast.14), custom_call_target="tpu_custom_call" | custom-call | tf_op jit(solution)/shard_map/inner/pallas_call | solution.py:353
  93.5 0.0 collective-permute-done.2.round_ref
  93.5 0.0 collective-permute-done.3.back_ref
  93.5 0.0 copy-done.2
  93.5 0.0 copy-done.4
  93.5 4.9 %rim.1 = (bf16[32,64,384]{2,1,0:T(8,128)(2,1)S(1)}, bf16[33,64,384]{2,1,0:T(8,128)(2,1)S(1)}, bf16[32,64,384]{2,1,0:T(8,128)(2,1)S(1)}, bf16[33,64,384]{2,1,0:T(8,128)(2,1)S(1)}, bf16[64,64,128]{2,1,0:T(8,128)(2,1)}) custom-call(s32[3]{0:T(128)S(1)} %pad_add_fusion.place_ref, ...), custom_call_target="tpu_custom_call", output_to_operand_aliasing={{0}: (1, {}), {1}: (2, {}), {2}: (3, {}), {3}: (4, {})} | custom-call | tf_op jit(solution)/shard_map/rim/pallas_call | solution.py:519
  (5 shorter events, 0.0 us)
Async XLA Ops:
  3.0 56.2 %all-to-all-start = ((bf16[128,104,128]{2,1,0:T(8,128)(2,1)}), bf16[128,104,128]{2,1,0:T(8,128)(2,1)S(1)}, u32[]{:S(2)}, u32[]{:S(2)}) async-start(bf16[128,104,128]{2,1,0:T(8,128)(2,1)} %pack.1), calls=%async_computation | async-start | bytes 6815744 | tf_op jit(solution)/shard_map/all_to_all | solution.py:551
  14.5 2.2 %copy-start = (bf16[128,128,128]{2,1,0:T(8,128)(2,1)S(1)}, bf16[128,128,128]{2,1,0:T(8,128)(2,1)}, u32[]{:S(2)}) copy-start(bf16[128,128,128]{2,1,0:T(8,128)(2,1)} %field_ref.1) | copy-start | bytes 12582916
  20.6 58.4 %copy-start.3 = (f32[128]{0:T(128)S(1)}, f32[128]{0:T(128)}, u32[]{:S(2)}) copy-start(f32[128]{0:T(128)} %param.13) | copy-start | bytes 1540
  59.2 19.7 %copy-start.1 = (bf16[3,3,128,128]{3,2,1,0:T(8,128)(2,1)S(1)}, bf16[3,3,128,128]{3,2,1,0:T(8,128)(2,1)}, u32[]{:S(2)}) copy-start(bf16[3,3,128,128]{3,2,1,0:T(8,128)(2,1)} %param.12) | copy-start | bytes 884740
  73.2 11.4 %collective-permute-start = (bf16[264,128]{1,0:T(8,128)(2,1)S(1)}, bf16[264,128]{1,0:T(8,128)(2,1)S(1)}, u32[]{:S(2)}, u32[]{:S(2)}) collective-permute-start(bf16[264,128]{1,0:T(8,128)(2,1)S(1)} %get-tuple-element.29.right_ref), channel_id=1, source_target_pairs={{0,1},{1,2},{2,3},{3,4},{4,5},{5,6},{6,7},{7,8},{8,9},{9,10},{10,1... | collective-permute-start | bytes 202760 | tf_op jit(solution)/shard_map/ppermute | solution.py:559
  73.5 11.0 %collective-permute-start.1 = (bf16[136,128]{1,0:T(8,128)(2,1)S(1)}, bf16[136,128]{1,0:T(8,128)(2,1)S(1)}, u32[]{:S(2)}, u32[]{:S(2)}) collective-permute-start(bf16[136,128]{1,0:T(8,128)(2,1)S(1)} %get-tuple-element.30.left_ref), channel_id=1, source_target_pairs={{1,0},{2,1},{3,2},{4,3},{5,4},{6,5},{7,6},{8,7},{9,8},{10,9},{11,1... | collective-permute-start | bytes 104456 | tf_op jit(solution)/shard_map/ppermute | solution.py:560
  85.2 8.3 %collective-permute-start.2 = (bf16[2,136,128]{2,1,0:T(8,128)(2,1)S(1)}, bf16[2,136,128]{2,1,0:T(8,128)(2,1)S(1)}, u32[]{:S(2)}, u32[]{:S(2)}) collective-permute-start(bf16[2,136,128]{2,1,0:T(8,128)(2,1)S(1)} %get-tuple-element.34), channel_id=1, source_target_pairs={{0,32},{32,64},{64,96},{96,112},{112,80},{80,48},{48,16},{16,0},{1... | collective-permute-start | bytes 208904 | tf_op jit(solution)/shard_map/ppermute | solution.py:563
  87.9 5.5 %copy-start.2 = (bf16[3,3,128,128]{3,2,1,0:T(8,128)(2,1)S(1)}, bf16[3,3,128,128]{3,2,1,0:T(8,128)(2,1)}, u32[]{:S(2)}) copy-start(bf16[3,3,128,128]{3,2,1,0:T(8,128)(2,1)} %param.14) | copy-start | bytes 884740
  87.9 5.6 %copy-start.4 = (f32[128]{0:T(128)S(1)}, f32[128]{0:T(128)}, u32[]{:S(2)}) copy-start(f32[128]{0:T(128)} %param.15) | copy-start | bytes 1540
  87.9 5.5 %collective-permute-start.3 = (bf16[2,136,128]{2,1,0:T(8,128)(2,1)S(1)}, bf16[2,136,128]{2,1,0:T(8,128)(2,1)S(1)}, u32[]{:S(2)}, u32[]{:S(2)}) collective-permute-start(bf16[2,136,128]{2,1,0:T(8,128)(2,1)S(1)} %get-tuple-element.35), channel_id=1, source_target_pairs={{32,0},{64,32},{96,64},{112,96},{80,112},{48,80},{16,48},{0,16},{3... | collective-permute-start | bytes 208904 | tf_op jit(solution)/shard_map/ppermute | solution.py:564

commit v10 on v9

--- a/solution.py
+++ b/solution.py
@@ -325,14 +325,22 @@
     bias = jnp.concatenate([b1_ref[...], b1_ref[...]], axis=-1)
     weight = w1_ref[...].reshape(1536, 256)
 
-    def step(b, carry):
+    def fill(b):
         for n in range(ROWS + 2):
-            base = pl.multiple_of((low + 1 + b * ROWS + n) * PITCH, 8)
+            base = (low + 1 + b * ROWS + n) * PITCH
             spans = [pl.ds(base + at, 64) for at in (ODD - 1, EVEN, ODD, EVEN + 1)]
             parts = [(field_ref[span, :] + other_ref[span, :]).astype(bf16) for span in spans]
-            lhs_ref[n] = jnp.concatenate(parts, axis=-1)
-        window = jnp.concatenate([lhs_ref[pl.ds(di, ROWS)].reshape(ROWS * 64, 512) for di in range(3)], axis=-1)
-        hid = gelu(jnp.dot(window, weight, preferred_element_type=f32) + bias).reshape(ROWS, 64, 256)
+            lhs_ref[b % 2, n] = jnp.concatenate(parts, axis=-1)
+
+    steps = 64 // ROWS
+    fill(0)
+    for b in range(steps):
+        held = lhs_ref.at[b % 2]
+        window = jnp.concatenate([held[pl.ds(di, ROWS)].reshape(ROWS * 64, 512) for di in range(3)], axis=-1)
+        pre = jnp.dot(window, weight, preferred_element_type=f32)
+        if b + 1 < steps:
+            fill(b + 1)
+        hid = gelu(pre + bias).reshape(ROWS, 64, 256)
         shift_ref[:, pl.ds(8, 64), :] = hid[:, :, 128:]
         tail_ref[...] = hid[:, 56:, :128]
         for n in range(ROWS):
@@ -344,9 +352,6 @@
         wide = wide.astype(bf16).reshape(ROWS // 2, 2, 64, 384)
         even_ref[pl.ds(b * (ROWS // 2), ROWS // 2)] = wide[:, 0]
         odd_ref[pl.ds(b * (ROWS // 2) + 1, ROWS // 2)] = wide[:, 1]
-        return carry
-
-    lax.fori_loop(0, 64 // ROWS, step, 0)
 
 
 def inner(low, field, other, w1, b1):
@@ -359,7 +364,7 @@
         ],
         in_specs=[VMEM] * 4,
         out_specs=[VMEM] * 3,
-        scratch_shapes=[pltpu.VMEM((ROWS + 2, 64, 512), jnp.bfloat16), pltpu.VMEM((ROWS, 72, 128), jnp.float32), pltpu.VMEM((ROWS, 8, 128), jnp.float32)],
+        scratch_shapes=[pltpu.VMEM((2, ROWS + 2, 64, 512), jnp.bfloat16), pltpu.VMEM((ROWS, 72, 128), jnp.float32), pltpu.VMEM((ROWS, 8, 128), jnp.float32)],
         compiler_params=pltpu.CompilerParams(vmem_limit_bytes=24 << 20),
         name="inner",
     )(on_chip(field), on_chip(other), w1, b1)

time: 99.7 us -> 99 us (level)
  transfers between devices with their start and end apart: 5 -> 5, of which waited for: 1 -> 1; matrix products, arithmetic and copies ran while one was open for 0% -> 0% of each run, Pallas kernels for 15% -> 14%
where the time goes in v10:
time: 99 us; the launch traced here: 98 us
  waiting for transfers between devices  38.7 us (39%)
  Pallas kernels  36.8 us (37%)
  starting transfers between devices  20 us (20%)
  local copies, waits for them, and re-layouts  2.2 us (2%)
    all_to_all x1, waiting for transfers between devices, shards(): lax.all_to_all(sent, ('lat', 'lon'), split_axis=0, concat_axis=0, tiled=T...  38.6 us
    pallas_call x1, Pallas kernels, scatter(): pl.pallas_call(scatter_kernel, out_shape=[pltpu.VMEM((SLABS * PITCH, 128)...  14.2 us
    all_to_all x1, starting transfers between devices, shards(): lax.all_to_all(sent, ('lat', 'lon'), split_axis=0, concat_axis=0, tiled=T...  11.5 us
    pallas_call x2, Pallas kernels, inner(): pl.pallas_call(functools.partial(inner_kernel, low), out_shape=[pltpu.VME...  10.4 us
    ppermute x1, starting transfers between devices, shards(): east = lax.ppermute(left, 'lon', west_pairs)  5.42 us
    pallas_call x1, Pallas kernels, rim(): pl.pallas_call(rim_kernel, out_shape=[pltpu.VMEM(b.shape, b.dtype) for b...  4.93 us
    pallas_call x1, Pallas kernels, spread(): pl.pallas_call(spread_kernel, out_shape=pltpu.HBM(field.shape, field.dtyp...  3.77 us
    pallas_call x1, Pallas kernels, pack(): pl.pallas_call(pack_kernel, out_shape=pltpu.HBM((owners, slots + META, ch...  3.03 us
  transfers between devices with their start and end apart: 5, of which 1 were waited for; matrix products, arithmetic and copies ran while one was open for 0% of the time, Pallas kernels for 14%

profile of v10, /device:TPU:1, one launch (start us, length us, event | category | flops | bytes accessed | tf_op | source)
XLA Modules:
  0.0 98.0 jit_solution(18316333355421511343)
XLA Ops:
  0.0 3.0 %pack.1 = bf16[128,104,128]{2,1,0:T(8,128)(2,1)} custom-call(bf16[128,96,128]{2,1,0:T(8,128)(2,1)} %bitcast.17, s32[96,128]{1,0:T(8,128)} %bitcast.18, s32[1,128]{1,0:T(1,128)} %counts_ref.1), custom_call_target="tpu_custom_call" | custom-call | tf_op jit(solution)/shard_map/pack/pallas_call | solution.py:94
  3.0 11.5 %all-to-all-start = ((bf16[128,104,128]{2,1,0:T(8,128)(2,1)}), bf16[128,104,128]{2,1,0:T(8,128)(2,1)S(1)}, u32[]{:S(2)}, u32[]{:S(2)}) async-start(bf16[128,104,128]{2,1,0:T(8,128)(2,1)} %pack.1), calls=%async_computation | async-start | bytes 6815744 | tf_op jit(solution)/shard_map/all_to_all | solution.py:556
  14.5 0.0 copy-start
  14.6 2.2 %copy-done = bf16[128,128,128]{2,1,0:T(8,128)(2,1)S(1)} copy-done((bf16[128,128,128]{2,1,0:T(8,128)(2,1)S(1)}, bf16[128,128,128]{2,1,0:T(8,128)(2,1)}, u32[]{:S(2)}) %copy-start) | copy-done | bytes 4194328
  16.7 3.8 %spread.1.parted_ref = bf16[128,128,128]{2,1,0:T(8,128)(2,1)} custom-call(bf16[128,128,128]{2,1,0:T(8,128)(2,1)S(1)} %copy-done), custom_call_target="tpu_custom_call" | custom-call | tf_op jit(solution)/shard_map/spread/pallas_call | solution.py:123
  20.5 0.1 pad_add_fusion.place_ref
  20.6 38.6 %all-to-all-done.got_ref = bf16[128,104,128]{2,1,0:T(8,128)(2,1)S(1)} async-done(((bf16[128,104,128]{2,1,0:T(8,128)(2,1)}), bf16[128,104,128]{2,1,0:T(8,128)(2,1)S(1)}, u32[]{:S(2)}, u32[]{:S(2)}) %all-to-all-start) | async-done | bytes 3407904 | tf_op jit(solution)/shard_map/all_to_all | solution.py:556
  59.2 14.2 %scatter.1 = (f32[19912,128]{1,0:T(8,128)S(1)}, f32[19912,128]{1,0:T(8,128)S(1)}, bf16[264,128]{1,0:T(8,128)(2,1)S(1)}, bf16[136,128]{1,0:T(8,128)(2,1)S(1)}, bf...) custom-call(s32[3]{0:T(128)S(1)} %pad_add_fusion.place_ref, ...), custom_call_target="tpu_custom_call" | custom-call | tf_op jit(solution)/shard_map/scatter/pallas_call | solution.py:264
  73.4 0.3 collective-permute-start
  73.7 5.4 %collective-permute-start.1 = (bf16[136,128]{1,0:T(8,128)(2,1)S(1)}, bf16[136,128]{1,0:T(8,128)(2,1)S(1)}, u32[]{:S(2)}, u32[]{:S(2)}) collective-permute-start(bf16[136,128]{1,0:T(8,128)(2,1)S(1)} %get-tuple-element.30.left_ref), channel_id=1, source_target_pairs={{1,0},{2,1},{3,2},{4,3},{5,4},{6,5},{7,6},{8,7},{9,8},{10,9},{11,1... | collective-permute-start | bytes 104456 | tf_op jit(solution)/shard_map/ppermute | solution.py:565
  79.1 0.0 copy-done.1
  79.1 0.1 fusion.2.w1_ref
  79.2 0.0 copy-done.3
  79.2 5.2 %inner.2 = (bf16[32,64,384]{2,1,0:T(8,128)(2,1)S(1)}, bf16[33,64,384]{2,1,0:T(8,128)(2,1)S(1)}, f32[3,64,128]{2,1,0:T(8,128)S(1)}) custom-call(f32[19912,128]{1,0:T(8,128)S(1)} %get-tuple-element.21.field_ref, f32[19912,128]{1,0:T(8,128)S(1)} %get-tuple-element.22.other_ref, bf16[3,512,256]{2,1,0:T(8,128)(2,1)S(1)} %fusion.2.w1_ref, f32[1,128]{1,0:T(1,128)S(1)} %bitcast.13), custom_call_target="tpu_custom_call" | custom-call | tf_op jit(solution)/shard_map/inner/pallas_call | solution.py:358
  84.4 0.0 collective-permute-done.1.east_ref
  84.4 0.0 collective-permute-done.west_ref
  84.4 0.6 frame.1
  85.0 2.8 %collective-permute-start.2 = (bf16[2,136,128]{2,1,0:T(8,128)(2,1)S(1)}, bf16[2,136,128]{2,1,0:T(8,128)(2,1)S(1)}, u32[]{:S(2)}, u32[]{:S(2)}) collective-permute-start(bf16[2,136,128]{2,1,0:T(8,128)(2,1)S(1)} %get-tuple-element.34), channel_id=1, source_target_pairs={{0,32},{32,64},{64,96},{96,112},{112,80},{80,48},{48,16},{16,0},{1... | collective-permute-start | bytes 208904 | tf_op jit(solution)/shard_map/ppermute | solution.py:568
  87.8 0.0 collective-permute-start.3
  87.8 5.2 %inner.3 = (bf16[32,64,384]{2,1,0:T(8,128)(2,1)S(1)}, bf16[33,64,384]{2,1,0:T(8,128)(2,1)S(1)}, f32[3,64,128]{2,1,0:T(8,128)S(1)}) custom-call(f32[19912,128]{1,0:T(8,128)S(1)} %get-tuple-element.21.field_ref, f32[19912,128]{1,0:T(8,128)S(1)} %get-tuple-element.22.other_ref, bf16[3,512,256]{2,1,0:T(8,128)(2,1)S(1)} %fusion.2.w1_ref, f32[1,128]{1,0:T(1,128)S(1)} %bitcast.14), custom_call_target="tpu_custom_call" | custom-call | tf_op jit(solution)/shard_map/inner/pallas_call | solution.py:358
  93.0 0.0 collective-permute-done.2.round_ref
  93.0 0.0 collective-permute-done.3.back_ref
  93.0 0.0 copy-done.2
  93.0 4.9 %rim.1 = (bf16[32,64,384]{2,1,0:T(8,128)(2,1)S(1)}, bf16[33,64,384]{2,1,0:T(8,128)(2,1)S(1)}, bf16[32,64,384]{2,1,0:T(8,128)(2,1)S(1)}, bf16[33,64,384]{2,1,0:T(8,128)(2,1)S(1)}, bf16[64,64,128]{2,1,0:T(8,128)(2,1)}) custom-call(s32[3]{0:T(128)S(1)} %pad_add_fusion.place_ref, ...), custom_call_target="tpu_custom_call", output_to_operand_aliasing={{0}: (1, {}), {1}: (2, {}), {2}: (3, {}), {3}: (4, {})} | custom-call | tf_op jit(solution)/shard_map/rim/pallas_call | solution.py:524
  (5 shorter events, 0.0 us)
Async XLA Ops:
  3.0 56.2 %all-to-all-start = ((bf16[128,104,128]{2,1,0:T(8,128)(2,1)}), bf16[128,104,128]{2,1,0:T(8,128)(2,1)S(1)}, u32[]{:S(2)}, u32[]{:S(2)}) async-start(bf16[128,104,128]{2,1,0:T(8,128)(2,1)} %pack.1), calls=%async_computation | async-start | bytes 6815744 | tf_op jit(solution)/shard_map/all_to_all | solution.py:556
  14.5 2.2 %copy-start = (bf16[128,128,128]{2,1,0:T(8,128)(2,1)S(1)}, bf16[128,128,128]{2,1,0:T(8,128)(2,1)}, u32[]{:S(2)}) copy-start(bf16[128,128,128]{2,1,0:T(8,128)(2,1)} %field_ref.1) | copy-start | bytes 12582916
  20.6 58.6 %copy-start.3 = (f32[128]{0:T(128)S(1)}, f32[128]{0:T(128)}, u32[]{:S(2)}) copy-start(f32[128]{0:T(128)} %param.13) | copy-start | bytes 1540
  59.2 19.9 %copy-start.1 = (bf16[3,3,128,128]{3,2,1,0:T(8,128)(2,1)S(1)}, bf16[3,3,128,128]{3,2,1,0:T(8,128)(2,1)}, u32[]{:S(2)}) copy-start(bf16[3,3,128,128]{3,2,1,0:T(8,128)(2,1)} %param.12) | copy-start | bytes 884740
  73.4 11.0 %collective-permute-start = (bf16[264,128]{1,0:T(8,128)(2,1)S(1)}, bf16[264,128]{1,0:T(8,128)(2,1)S(1)}, u32[]{:S(2)}, u32[]{:S(2)}) collective-permute-start(bf16[264,128]{1,0:T(8,128)(2,1)S(1)} %get-tuple-element.29.right_ref), channel_id=1, source_target_pairs={{0,1},{1,2},{2,3},{3,4},{4,5},{5,6},{6,7},{7,8},{8,9},{9,10},{10,1... | collective-permute-start | bytes 202760 | tf_op jit(solution)/shard_map/ppermute | solution.py:564
  73.7 10.7 %collective-permute-start.1 = (bf16[136,128]{1,0:T(8,128)(2,1)S(1)}, bf16[136,128]{1,0:T(8,128)(2,1)S(1)}, u32[]{:S(2)}, u32[]{:S(2)}) collective-permute-start(bf16[136,128]{1,0:T(8,128)(2,1)S(1)} %get-tuple-element.30.left_ref), channel_id=1, source_target_pairs={{1,0},{2,1},{3,2},{4,3},{5,4},{6,5},{7,6},{8,7},{9,8},{10,9},{11,1... | collective-permute-start | bytes 104456 | tf_op jit(solution)/shard_map/ppermute | solution.py:565
  85.0 8.0 %collective-permute-start.2 = (bf16[2,136,128]{2,1,0:T(8,128)(2,1)S(1)}, bf16[2,136,128]{2,1,0:T(8,128)(2,1)S(1)}, u32[]{:S(2)}, u32[]{:S(2)}) collective-permute-start(bf16[2,136,128]{2,1,0:T(8,128)(2,1)S(1)} %get-tuple-element.34), channel_id=1, source_target_pairs={{0,32},{32,64},{64,96},{96,112},{112,80},{80,48},{48,16},{16,0},{1... | collective-permute-start | bytes 208904 | tf_op jit(solution)/shard_map/ppermute | solution.py:568
  87.8 5.2 %copy-start.2 = (bf16[3,3,128,128]{3,2,1,0:T(8,128)(2,1)S(1)}, bf16[3,3,128,128]{3,2,1,0:T(8,128)(2,1)}, u32[]{:S(2)}) copy-start(bf16[3,3,128,128]{3,2,1,0:T(8,128)(2,1)} %param.14) | copy-start | bytes 884740
  87.8 5.2 %copy-start.4 = (f32[128]{0:T(128)S(1)}, f32[128]{0:T(128)}, u32[]{:S(2)}) copy-start(f32[128]{0:T(128)} %param.15) | copy-start | bytes 1540
  87.8 5.2 %collective-permute-start.3 = (bf16[2,136,128]{2,1,0:T(8,128)(2,1)S(1)}, bf16[2,136,128]{2,1,0:T(8,128)(2,1)S(1)}, u32[]{:S(2)}, u32[]{:S(2)}) collective-permute-start(bf16[2,136,128]{2,1,0:T(8,128)(2,1)S(1)} %get-tuple-element.35), channel_id=1, source_target_pairs={{32,0},{64,32},{96,64},{112,96},{80,112},{48,80},{16,48},{0,16},{3... | collective-permute-start | bytes 208904 | tf_op jit(solution)/shard_map/ppermute | solution.py:569
